TPU v7x, 128 devices: a whole 4x4x4 slice. The times are simulated.
128 devices in a mesh: dp: 8 (over y, core), ctx: 16 (over z, x).
Axes of the slice: x: 4, y: 4, z: 4, core: 2. Of those that a mesh axis runs over, the one named last changes fastest.
Arguments:
- queries: bfloat16 [8, 4096, 256], P('dp', 'ctx'), may hold values from -6 to 6
- keys: bfloat16 [8, 4096, 256], P('dp', 'ctx'), may hold values from -6 to 6
- values: bfloat16 [8, 4096, 256], P('dp', 'ctx'), may hold values from -6 to 6
- grad_out: bfloat16 [8, 4096, 256], P('dp', 'ctx'), may hold values from -6 to 6
- log_norm: float32 [8, 2, 4096], P('dp', None, 'ctx'), may hold values from 5 to 7
- offsets: int32 [2, 5], replicated, may hold values from 0 to 15
- q_gain: float32 [256], replicated, may hold values from 0.5 to 2
Outputs:
- grad_queries: bfloat16 [8, 4096, 256], P('dp', 'ctx')
- grad_keys: bfloat16 [8, 4096, 256], P('dp', 'ctx')
- grad_values: bfloat16 [8, 4096, 256], P('dp', 'ctx')
- grad_gain: float32 [256], replicated
All inputs are finite; a program needn't handle non-finite values.
Results may differ from a plain program's by a relative error of at most 0.013.
The roundings to bfloat16 on the way count: a program that leaves them out, or rounds other values in their place, can miss the bound.
Values may be sent and summed in bfloat16 or wider, within the bound.
No kernel may reach another device: no remote copies, remote signals or barrier semaphores. Data moves between devices by JAX's collectives and lax.ppermute only.
A program may use at most 64 MiB of HBM per device.

v0:
```python
import math

import jax
import jax.numpy as jnp
from jax import lax
from jax.sharding import PartitionSpec as P

BLOCK = 128
LEVELS = 5


def swapped(block, axis, stride):
    count = lax.axis_size(axis)
    route = []
    for low in range(count):
        high = low | 1 << stride
        if high != low and high < count:
            route += [(low, high), (high, low)]
    return lax.ppermute(block, axis, route)


def slot_table(device_local, offset_vec, stride, block_count):
    slot_count = (block_count + stride - 1) // stride
    base_block = device_local * block_count + jnp.zeros_like(offset_vec)
    first_step = jnp.maximum((base_block - offset_vec + stride - 1) // stride, 0)
    step_index = first_step[..., None] + jnp.arange(slot_count, dtype=jnp.int32)
    global_block = offset_vec[..., None] + stride * step_index
    local_block = global_block - base_block[..., None]
    usable = (step_index < block_count) & (local_block >= 0) & (local_block < block_count)
    return (jnp.clip(local_block, 0, block_count - 1), usable.astype(jnp.float32))


def segment_slots(shift_vec, span_len, block_count):
    device_col = jnp.arange(span_len, dtype=jnp.int32)[:, None]
    seg_block, seg_usable = slot_table(device_col, shift_vec[None, :], span_len, block_count)
    return (seg_block.transpose(1, 0, 2), seg_usable.transpose(1, 0, 2))


def select_table(local_block, block_count):
    return (local_block[..., None] == jnp.arange(block_count, dtype=jnp.int32)).astype(jnp.float32)


def pick_blocks(data, table):
    head_count, block_count = (data.shape[0], data.shape[1])
    flat = data.reshape(head_count, block_count, -1).astype(jnp.float32)
    chosen = jnp.einsum(
        "hsb,hbx->hsx",
        table,
        flat,
        precision=lax.Precision.HIGHEST,
        preferred_element_type=jnp.float32,
    ).astype(data.dtype)
    return chosen.reshape((head_count, -1) + data.shape[3:])


def place_rows(accum, contrib, table, usable):
    head_count, block_count = (accum.shape[0], accum.shape[1])
    slot_count = table.shape[1]
    weights = table * usable[..., None]
    shaped = contrib.reshape(head_count, slot_count, -1)
    added = jnp.einsum(
        "hsb,hsx->hbx",
        weights,
        shaped,
        precision=lax.Precision.HIGHEST,
        preferred_element_type=jnp.float32,
    )
    return accum + added.reshape(accum.shape)


def attend(
    query_rows,
    dout_rows,
    norm_rows,
    query_mask,
    key_rows,
    value_rows,
    key_mask,
    score_scale,
    row_block,
):
    head_count, query_count, head_dim = query_rows.shape
    steps = query_count // row_block

    def split(array):
        return jnp.moveaxis(array.reshape((head_count, steps, row_block) + array.shape[2:]), 1, 0)

    def step_fn(carry, parts):
        query_blk, dout_blk, norm_blk, mask_blk = parts
        scores = (
            jnp.einsum("hqd,hkd->hqk", query_blk, key_rows, preferred_element_type=jnp.float32)
            * score_scale
        )
        probs = jnp.exp(scores - norm_blk[:, :, None]) * mask_blk[:, :, None] * key_mask[:, None, :]
        probs_low = probs.astype(jnp.bfloat16)
        prob_grad = jnp.einsum(
            "hqd,hkd->hqk", dout_blk, value_rows, preferred_element_type=jnp.float32
        )
        dscore = (probs * prob_grad).astype(jnp.bfloat16)
        query_grad = (
            jnp.einsum("hqk,hkd->hqd", dscore, key_rows, preferred_element_type=jnp.float32)
            * score_scale
        )
        key_part = (
            jnp.einsum("hqk,hqd->hkd", dscore, query_blk, preferred_element_type=jnp.float32)
            * score_scale
        )
        value_part = jnp.einsum(
            "hqk,hqd->hkd", probs_low, dout_blk, preferred_element_type=jnp.float32
        )
        return ((carry[0] + key_part, carry[1] + value_part), query_grad)

    start = jnp.zeros((head_count, key_rows.shape[1], head_dim), jnp.float32)
    totals, query_parts = lax.scan(
        step_fn,
        (start, start),
        (split(query_rows), split(dout_rows), split(norm_rows), split(query_mask)),
    )
    query_grad = jnp.moveaxis(query_parts, 0, 1).reshape(head_count, query_count, head_dim)
    return (query_grad, totals[0], totals[1])


def swap_up(payload, my_index, bit_total):
    for bit_idx in range(bit_total):
        partner = swapped(payload, "ctx", bit_idx)
        lower_half = my_index >> bit_idx & 1 == 0
        payload = jnp.where(
            lower_half,
            jnp.concatenate([payload, partner], axis=1),
            jnp.concatenate([partner, payload], axis=1),
        )
    return payload


def swap_down(sums_kv, my_index, bit_total):
    head_count = sums_kv.shape[0]
    for bit_idx in reversed(range(bit_total)):
        halves = sums_kv.reshape(head_count, 2, -1, sums_kv.shape[-1])
        lower_half = my_index >> bit_idx & 1 == 0
        kept_half = jnp.where(lower_half, halves[:, 0], halves[:, 1])
        sent_half = jnp.where(lower_half, halves[:, 1], halves[:, 0])
        sums_kv = kept_half + swapped(sent_half.astype(jnp.bfloat16), "ctx", bit_idx).astype(
            sent_half.dtype
        )
    return sums_kv


def body(queries, keys, values, grad_out, log_norm, offsets, q_gain):
    query_raw = queries[0]
    token_count, proj_width = query_raw.shape
    head_count = log_norm.shape[1]
    head_dim = proj_width // head_count
    block_count = token_count // BLOCK
    ctx_size = lax.axis_size("ctx")
    score_scale = head_dim ** (-0.5)
    scaled = (query_raw.astype(jnp.float32) * q_gain).astype(jnp.bfloat16)

    def heads(matrix):
        return (
            matrix.reshape(token_count, head_count, head_dim)
            .transpose(1, 0, 2)
            .reshape(head_count, block_count, BLOCK, head_dim)
        )

    query_all = heads(scaled)
    key_all = heads(keys[0])
    value_all = heads(values[0])
    dout_all = heads(grad_out[0])
    norm_all = log_norm[0].reshape(head_count, block_count, BLOCK)
    query_acc = jnp.zeros((head_count, block_count, BLOCK, head_dim), jnp.float32)
    kv_acc = jnp.zeros((head_count, block_count, BLOCK, 2 * head_dim), jnp.float32)
    my_index = lax.axis_index("ctx")
    for level_idx in range(LEVELS):
        span_len = min(2**level_idx, ctx_size)
        shift_vec = offsets[:, level_idx] % span_len
        local_block, usable = slot_table(my_index % span_len, shift_vec, span_len, block_count)
        table = select_table(local_block, block_count)
        slot_count = local_block.shape[1]
        row_block = BLOCK * math.gcd(slot_count, max(1, 512 // BLOCK))
        query_own = pick_blocks(query_all, table)
        dout_own = pick_blocks(dout_all, table)
        norm_own = pick_blocks(norm_all, table)
        mask_own = jnp.repeat(usable, BLOCK, axis=1)
        payload = jnp.concatenate(
            [pick_blocks(key_all, table), pick_blocks(value_all, table)], axis=2
        )
        bit_total = span_len.bit_length() - 1
        payload = swap_up(payload, my_index, bit_total)
        seg_block, seg_usable = segment_slots(shift_vec, span_len, block_count)
        seg_mask = jnp.repeat(seg_usable.reshape(head_count, -1), BLOCK, axis=1)
        level_query, level_key, level_value = attend(
            query_own,
            dout_own,
            norm_own,
            mask_own,
            payload[..., :head_dim],
            payload[..., head_dim:],
            seg_mask,
            score_scale,
            row_block,
        )
        sums_kv = jnp.concatenate([level_key, level_value], axis=2)
        sums_kv = swap_down(sums_kv, my_index, bit_total)
        query_acc = place_rows(query_acc, level_query, table, usable)
        kv_acc = place_rows(kv_acc, sums_kv, table, usable)

    def to_rows(field_acc):
        return (
            field_acc.reshape(head_count, token_count, -1)
            .transpose(1, 0, 2)
            .reshape(token_count, -1)
        )

    dq_rows = to_rows(query_acc)
    grad_queries = (dq_rows * q_gain).astype(jnp.bfloat16)
    grad_keys = to_rows(kv_acc[..., :head_dim]).astype(jnp.bfloat16)
    grad_values = to_rows(kv_acc[..., head_dim:]).astype(jnp.bfloat16)
    gain_total = lax.psum(jnp.sum(query_raw.astype(jnp.float32) * dq_rows, axis=0), ("dp", "ctx"))
    return (grad_queries[None], grad_keys[None], grad_values[None], gain_total)


def solution(mesh):
    in_specs = (
        P("dp", "ctx", None),
        P("dp", "ctx", None),
        P("dp", "ctx", None),
        P("dp", "ctx", None),
        P("dp", None, "ctx"),
        P(),
        P(),
    )
    out_specs = (P("dp", "ctx", None), P("dp", "ctx", None), P("dp", "ctx", None), P())
    return jax.shard_map(body, mesh=mesh, in_specs=in_specs, out_specs=out_specs, check_vma=False)
```

profile of v0, /device:TPU:1, one launch (start us, length us, event | category | flops | bytes accessed | tf_op | source)
XLA Modules:
  0.0 272.1 jit_solution(3529592541120777040)
XLA Ops:
  33.7 3.0 %collective-permute-start.2 = (bf16[2,256,256]{2,1,0:T(8,128)(2,1)S(1)}, bf16[2,256,256]{2,1,0:T(8,128)(2,1)S(1)}, u32[]{:S(2)}, u32[]{:S(2)}) collective-permute-start(bf16[2,256,256]{2,1,0:T(8,128)(2,1)S(1)} %maximum_select_fusion.7), channel_id=1, source_target_pairs={{0,2},{2,0},{1,3},{3,1},{4,6},{6,4},{5,7},{7,5},{8,10},{10,8},{9,1... | collective-permute-start | bytes 786440 | tf_op jit(solution)/shard_map/ppermute | solution.py:19
  45.1 10.2 %collective-permute-done.4 = bf16[2,256,256]{2,1,0:T(8,128)(2,1)} collective-permute-done((bf16[2,256,256]{2,1,0:T(8,128)(2,1)}, bf16[2,256,256]{2,1,0:T(8,128)(2,1)}, u32[]{:S(2)}, u32[]{:S(2)}) %collective-permute-start.4) | collective-permute-done | bytes 262176 | tf_op jit(solution)/shard_map/ppermute | solution.py:19
  56.6 2.3 collective-permute-start.5
  61.2 2.7 %collective-permute-start.11 = (bf16[2,256,256]{2,1,0:T(8,128)(2,1)}, bf16[2,256,256]{2,1,0:T(8,128)(2,1)}, u32[]{:S(2)}, u32[]{:S(2)}) collective-permute-start(bf16[2,256,256]{2,1,0:T(8,128)(2,1)} %fusion.49), channel_id=1, source_target_pairs={{0,2},{2,0},{1,3},{3,1},{4,6},{6,4},{5,7},{7,5},{8,10},{10,8},{9,1... | collective-permute-start | bytes 786440 | tf_op jit(solution)/shard_map/ppermute | solution.py:19
  64.0 2.2 maximum_select_fusion.5
  66.1 2.4 collective-permute-done.5
  73.9 3.0 %reshape.1673 = f32[2,2,512,256]{2,1,3,0:T(2,128)S(1)} reshape(f32[2,1024,256]{1,2,0:T(8,128)} %pad_maximum_fusion.1) | data formatting | bytes 4194304 | tf_op jit(solution)/shard_map/reshape | solution.py:138
  76.9 2.9 %fusion.212 = (f32[2,1,512,256]{2,1,3,0:T(1,128)}, f32[2,1,512,256]{2,1,3,0:T(1,128)}) fusion(f32[2,2,512,256]{2,1,3,0:T(2,128)S(1)} %reshape.1673), kind=kLoop, calls=%fused_computation.413 | loop fusion | bytes 4194304 | tf_op jit(solution)/shard_map/slice | solution.py:140
  79.9 2.3 copy.151
  82.2 2.4 copy.152
  87.8 3.4 %collective-permute-start.9 = (bf16[2,1024,256]{2,1,0:T(8,128)(2,1)S(1)}, bf16[2,1024,256]{2,1,0:T(8,128)(2,1)S(1)}, u32[]{:S(2)}, u32[]{:S(2)}) collective-permute-start(bf16[2,1024,256]{2,1,0:T(8,128)(2,1)S(1)} %maximum_select_fusion.2), channel_id=1, source_target_pairs={{0,8},{8,0},{1,9},{9,1},{2,10},{10,2},{3,11},{11,3},{4,12},{12,4},... | collective-permute-start | bytes 3145736 | tf_op jit(solution)/shard_map/ppermute | solution.py:19
  96.6 20.2 %collective-permute-done.9 = bf16[2,1024,256]{2,1,0:T(8,128)(2,1)S(1)} collective-permute-done((bf16[2,1024,256]{2,1,0:T(8,128)(2,1)S(1)}, bf16[2,1024,256]{2,1,0:T(8,128)(2,1)S(1)}, u32[]{:S(2)}, u32[]{:S(2)}) %collective-permute-start.9) | collective-permute-done | bytes 1048608 | tf_op jit(solution)/shard_map/ppermute | solution.py:19
  120.7 2.5 pad_maximum_fusion
  123.2 6.6 %reshape.1677 = f32[2,2,1024,256]{2,1,3,0:T(2,128)} reshape(f32[2,2048,256]{1,2,0:T(8,128)} %pad_maximum_fusion) | data formatting | bytes 8388608 | tf_op jit(solution)/shard_map/reshape | solution.py:138
  129.8 9.1 %fusion.211 = (f32[2,1,1024,256]{2,1,3,0:T(1,128)}, f32[2,1,1024,256]{2,1,3,0:T(1,128)}) fusion(f32[2,2,1024,256]{2,1,3,0:T(2,128)} %reshape.1677), kind=kLoop, calls=%fused_computation.412 | loop fusion | bytes 8388608 | tf_op jit(solution)/shard_map/slice | solution.py:140
  138.9 4.6 %copy.157 = f32[2,1,1024,256]{3,2,0,1:T(8,128)S(1)} copy(f32[2,1,1024,256]{2,1,3,0:T(1,128)} %get-tuple-element.141) | data formatting | bytes 4194304
  143.5 6.0 %copy.158 = f32[2,1,1024,256]{3,2,0,1:T(8,128)} copy(f32[2,1,1024,256]{2,1,3,0:T(1,128)} %get-tuple-element.142) | data formatting | bytes 4194304
  151.6 2.8 %collective-permute-start.14 = (bf16[2,256,256]{2,1,0:T(8,128)(2,1)S(1)}, bf16[2,256,256]{2,1,0:T(8,128)(2,1)S(1)}, u32[]{:S(2)}, u32[]{:S(2)}) collective-permute-start(bf16[2,256,256]{2,1,0:T(8,128)(2,1)S(1)} %fusion.50), channel_id=1, source_target_pairs={{0,2},{2,0},{1,3},{3,1},{4,6},{6,4},{5,7},{7,5},{8,10},{10,8},{9,1... | collective-permute-start | bytes 786440 | tf_op jit(solution)/shard_map/ppermute | solution.py:19
  159.8 10.1 %collective-permute-done.16 = bf16[2,1024,256]{2,1,0:T(8,128)(2,1)S(1)} collective-permute-done((bf16[2,1024,256]{2,1,0:T(8,128)(2,1)S(1)}, bf16[2,1024,256]{2,1,0:T(8,128)(2,1)S(1)}, u32[]{:S(2)}, u32[]{:S(2)}) %collective-permute-start.16) | collective-permute-done | bytes 1048608 | tf_op jit(solution)/shard_map/ppermute | solution.py:19
  172.7 8.0 %collective-permute-done.17 = bf16[2,512,256]{2,1,0:T(8,128)(2,1)S(1)} collective-permute-done((bf16[2,512,256]{2,1,0:T(8,128)(2,1)S(1)}, bf16[2,512,256]{2,1,0:T(8,128)(2,1)S(1)}, u32[]{:S(2)}, u32[]{:S(2)}) %collective-permute-start.17) | collective-permute-done | bytes 524320 | tf_op jit(solution)/shard_map/ppermute | solution.py:19
  181.7 2.5 collective-permute-start.18
  186.3 76.2 %psum.7 = f32[256]{0:T(256)} all-reduce(f32[256]{0:T(256)S(1)} %bitcast.569), channel_id=1, replica_groups=mesh['dp'=8,'ctx'=16] {'dp','ctx'}, use_global_device_ids=true, to_apply=%region_1.2 | all-reduce | flops 256 | bytes 2048 | tf_op jit(solution)/shard_map/psum | solution.py:218
  264.3 2.9 %collective-permute-done.19 = bf16[2,128,256]{2,1,0:T(8,128)(2,1)S(1)} collective-permute-done((bf16[2,128,256]{2,1,0:T(8,128)(2,1)S(1)}, bf16[2,128,256]{2,1,0:T(8,128)(2,1)S(1)}, u32[]{:S(2)}, u32[]{:S(2)}) %collective-permute-start.19) | collective-permute-done | bytes 131104 | tf_op jit(solution)/shard_map/ppermute | solution.py:19
  267.5 2.4 fusion.3
  (336 shorter events, 78.7 us)
Async XLA Ops:
  5.4 25.6 %collective-permute-start = (bf16[2,128,256]{2,1,0:T(8,128)(2,1)S(1)}, bf16[2,128,256]{2,1,0:T(8,128)(2,1)S(1)}, u32[]{:S(2)}, u32[]{:S(2)}) collective-permute-start(bf16[2,128,256]{2,1,0:T(8,128)(2,1)S(1)} %bitcast_dynamic-update-slice_fusion.6), channel_id=1, source_target_pairs={{0,1},{1,0},{2,3},{3,2},{4,5},{5,4},{6,7},{7,6},{8,9},{9,8},{10,11... | collective-permute-start | bytes 393224 | tf_op jit(solution)/shard_map/ppermute | solution.py:19
  8.4 25.2 %collective-permute-start.1 = (bf16[2,128,256]{2,1,0:T(8,128)(2,1)S(1)}, bf16[2,128,256]{2,1,0:T(8,128)(2,1)S(1)}, u32[]{:S(2)}, u32[]{:S(2)}) collective-permute-start(bf16[2,128,256]{2,1,0:T(8,128)(2,1)S(1)} %bitcast_dynamic-update-slice_fusion.4), channel_id=1, source_target_pairs={{0,1},{1,0},{2,3},{3,2},{4,5},{5,4},{6,7},{7,6},{8,9},{9,8},{10,11... | collective-permute-start | bytes 393224 | tf_op jit(solution)/shard_map/ppermute | solution.py:19
  9.4 31.1 %collective-permute-start.3 = (bf16[2,128,256]{2,1,0:T(8,128)(2,1)S(1)}, bf16[2,128,256]{2,1,0:T(8,128)(2,1)S(1)}, u32[]{:S(2)}, u32[]{:S(2)}) collective-permute-start(bf16[2,128,256]{2,1,0:T(8,128)(2,1)S(1)} %bitcast_dynamic-update-slice_fusion.2), channel_id=1, source_target_pairs={{0,1},{1,0},{2,3},{3,2},{4,5},{5,4},{6,7},{7,6},{8,9},{9,8},{10,11... | collective-permute-start | bytes 393224 | tf_op jit(solution)/shard_map/ppermute | solution.py:19
  11.8 26.2 %collective-permute-start.6 = (bf16[2,128,256]{2,1,0:T(8,128)(2,1)S(1)}, bf16[2,128,256]{2,1,0:T(8,128)(2,1)S(1)}, u32[]{:S(2)}, u32[]{:S(2)}) collective-permute-start(bf16[2,128,256]{2,1,0:T(8,128)(2,1)S(1)} %bitcast_dynamic-update-slice_fusion), channel_id=1, source_target_pairs={{0,1},{1,0},{2,3},{3,2},{4,5},{5,4},{6,7},{7,6},{8,9},{9,8},{10,11... | collective-permute-start | bytes 393224 | tf_op jit(solution)/shard_map/ppermute | solution.py:19
  33.7 8.9 %collective-permute-start.2 = (bf16[2,256,256]{2,1,0:T(8,128)(2,1)S(1)}, bf16[2,256,256]{2,1,0:T(8,128)(2,1)S(1)}, u32[]{:S(2)}, u32[]{:S(2)}) collective-permute-start(bf16[2,256,256]{2,1,0:T(8,128)(2,1)S(1)} %maximum_select_fusion.7), channel_id=1, source_target_pairs={{0,2},{2,0},{1,3},{3,1},{4,6},{6,4},{5,7},{7,5},{8,10},{10,8},{9,1... | collective-permute-start | bytes 786440 | tf_op jit(solution)/shard_map/ppermute | solution.py:19
  37.7 53.5 %collective-permute-start.10 = (bf16[2,128,256]{2,1,0:T(8,128)(2,1)}, bf16[2,128,256]{2,1,0:T(8,128)(2,1)}, u32[]{:S(2)}, u32[]{:S(2)}) collective-permute-start(bf16[2,128,256]{2,1,0:T(8,128)(2,1)} %fusion.67), channel_id=1, source_target_pairs={{0,1},{1,0},{2,3},{3,2},{4,5},{5,4},{6,7},{7,6},{8,9},{9,8},{10,11... | collective-permute-start | bytes 393224 | tf_op jit(solution)/shard_map/ppermute | solution.py:19
  38.8 25.2 %collective-permute-start.7 = (bf16[2,256,256]{2,1,0:T(8,128)(2,1)}, bf16[2,256,256]{2,1,0:T(8,128)(2,1)}, u32[]{:S(2)}, u32[]{:S(2)}) collective-permute-start(bf16[2,256,256]{2,1,0:T(8,128)(2,1)} %maximum_select_fusion.9), channel_id=1, source_target_pairs={{0,2},{2,0},{1,3},{3,1},{4,6},{6,4},{5,7},{7,5},{8,10},{10,8},{9,1... | collective-permute-start | bytes 786440 | tf_op jit(solution)/shard_map/ppermute | solution.py:19
  41.4 13.9 %collective-permute-start.4 = (bf16[2,256,256]{2,1,0:T(8,128)(2,1)}, bf16[2,256,256]{2,1,0:T(8,128)(2,1)}, u32[]{:S(2)}, u32[]{:S(2)}) collective-permute-start(bf16[2,256,256]{2,1,0:T(8,128)(2,1)} %maximum_select_fusion.8), channel_id=1, source_target_pairs={{0,2},{2,0},{1,3},{3,1},{4,6},{6,4},{5,7},{7,5},{8,10},{10,8},{9,1... | collective-permute-start | bytes 786440 | tf_op jit(solution)/shard_map/ppermute | solution.py:19
  56.6 11.9 %collective-permute-start.5 = (bf16[2,512,256]{2,1,0:T(8,128)(2,1)S(1)}, bf16[2,512,256]{2,1,0:T(8,128)(2,1)}, u32[]{:S(2)}, u32[]{:S(2)}) collective-permute-start(bf16[2,512,256]{2,1,0:T(8,128)(2,1)S(1)} %maximum_select_fusion.4), channel_id=1, source_target_pairs={{0,4},{4,0},{1,5},{5,1},{2,6},{6,2},{3,7},{7,3},{8,12},{12,8},{9,1... | collective-permute-start | bytes 1572872 | tf_op jit(solution)/shard_map/ppermute | solution.py:19
  61.2 31.8 %collective-permute-start.11 = (bf16[2,256,256]{2,1,0:T(8,128)(2,1)}, bf16[2,256,256]{2,1,0:T(8,128)(2,1)}, u32[]{:S(2)}, u32[]{:S(2)}) collective-permute-start(bf16[2,256,256]{2,1,0:T(8,128)(2,1)} %fusion.49), channel_id=1, source_target_pairs={{0,2},{2,0},{1,3},{3,1},{4,6},{6,4},{5,7},{7,5},{8,10},{10,8},{9,1... | collective-permute-start | bytes 786440 | tf_op jit(solution)/shard_map/ppermute | solution.py:19
  66.1 19.9 %collective-permute-start.8 = (bf16[2,512,256]{2,1,0:T(8,128)(2,1)}, bf16[2,512,256]{2,1,0:T(8,128)(2,1)}, u32[]{:S(2)}, u32[]{:S(2)}) collective-permute-start(bf16[2,512,256]{2,1,0:T(8,128)(2,1)} %maximum_select_fusion.5), channel_id=1, source_target_pairs={{0,4},{4,0},{1,5},{5,1},{2,6},{6,2},{3,7},{7,3},{8,12},{12,8},{9,1... | collective-permute-start | bytes 1572872 | tf_op jit(solution)/shard_map/ppermute | solution.py:19
  84.8 11.6 %collective-permute-start.13 = (bf16[2,512,256]{2,1,0:T(8,128)(2,1)S(1)}, bf16[2,512,256]{2,1,0:T(8,128)(2,1)S(1)}, u32[]{:S(2)}, u32[]{:S(2)}) collective-permute-start(bf16[2,512,256]{2,1,0:T(8,128)(2,1)S(1)} %fusion.42), channel_id=1, source_target_pairs={{0,4},{4,0},{1,5},{5,1},{2,6},{6,2},{3,7},{7,3},{8,12},{12,8},{9,1... | collective-permute-start | bytes 1572872 | tf_op jit(solution)/shard_map/ppermute | solution.py:19
  87.8 29.1 %collective-permute-start.9 = (bf16[2,1024,256]{2,1,0:T(8,128)(2,1)S(1)}, bf16[2,1024,256]{2,1,0:T(8,128)(2,1)S(1)}, u32[]{:S(2)}, u32[]{:S(2)}) collective-permute-start(bf16[2,1024,256]{2,1,0:T(8,128)(2,1)S(1)} %maximum_select_fusion.2), channel_id=1, source_target_pairs={{0,8},{8,0},{1,9},{9,1},{2,10},{10,2},{3,11},{11,3},{4,12},{12,4},... | collective-permute-start | bytes 3145736 | tf_op jit(solution)/shard_map/ppermute | solution.py:19
  94.8 59.9 %collective-permute-start.12 = (bf16[2,128,256]{2,1,0:T(8,128)(2,1)}, bf16[2,128,256]{2,1,0:T(8,128)(2,1)}, u32[]{:S(2)}, u32[]{:S(2)}) collective-permute-start(bf16[2,128,256]{2,1,0:T(8,128)(2,1)} %fusion.68), channel_id=1, source_target_pairs={{0,1},{1,0},{2,3},{3,2},{4,5},{5,4},{6,7},{7,6},{8,9},{9,8},{10,11... | collective-permute-start | bytes 393224 | tf_op jit(solution)/shard_map/ppermute | solution.py:19
  151.5 18.4 %collective-permute-start.16 = (bf16[2,1024,256]{2,1,0:T(8,128)(2,1)S(1)}, bf16[2,1024,256]{2,1,0:T(8,128)(2,1)S(1)}, u32[]{:S(2)}, u32[]{:S(2)}) collective-permute-start(bf16[2,1024,256]{2,1,0:T(8,128)(2,1)S(1)} %fusion.36), channel_id=1, source_target_pairs={{0,8},{8,0},{1,9},{9,1},{2,10},{10,2},{3,11},{11,3},{4,12},{12,4},... | collective-permute-start | bytes 3145736 | tf_op jit(solution)/shard_map/ppermute | solution.py:19
  151.6 6.8 %collective-permute-start.14 = (bf16[2,256,256]{2,1,0:T(8,128)(2,1)S(1)}, bf16[2,256,256]{2,1,0:T(8,128)(2,1)S(1)}, u32[]{:S(2)}, u32[]{:S(2)}) collective-permute-start(bf16[2,256,256]{2,1,0:T(8,128)(2,1)S(1)} %fusion.50), channel_id=1, source_target_pairs={{0,2},{2,0},{1,3},{3,1},{4,6},{6,4},{5,7},{7,5},{8,10},{10,8},{9,1... | collective-permute-start | bytes 786440 | tf_op jit(solution)/shard_map/ppermute | solution.py:19
  158.6 12.6 %collective-permute-start.15 = (bf16[2,128,256]{2,1,0:T(8,128)(2,1)S(1)}, bf16[2,128,256]{2,1,0:T(8,128)(2,1)S(1)}, u32[]{:S(2)}, u32[]{:S(2)}) collective-permute-start(bf16[2,128,256]{2,1,0:T(8,128)(2,1)S(1)} %fusion.69), channel_id=1, source_target_pairs={{0,1},{1,0},{2,3},{3,2},{4,5},{5,4},{6,7},{7,6},{8,9},{9,8},{10,11... | collective-permute-start | bytes 393224 | tf_op jit(solution)/shard_map/ppermute | solution.py:19
  170.4 10.4 %collective-permute-start.17 = (bf16[2,512,256]{2,1,0:T(8,128)(2,1)S(1)}, bf16[2,512,256]{2,1,0:T(8,128)(2,1)S(1)}, u32[]{:S(2)}, u32[]{:S(2)}) collective-permute-start(bf16[2,512,256]{2,1,0:T(8,128)(2,1)S(1)} %fusion.43), channel_id=1, source_target_pairs={{0,4},{4,0},{1,5},{5,1},{2,6},{6,2},{3,7},{7,3},{8,12},{12,8},{9,1... | collective-permute-start | bytes 1572872 | tf_op jit(solution)/shard_map/ppermute | solution.py:19
  181.7 80.8 %collective-permute-start.18 = (bf16[2,256,256]{2,1,0:T(8,128)(2,1)}, bf16[2,256,256]{2,1,0:T(8,128)(2,1)S(1)}, u32[]{:S(2)}, u32[]{:S(2)}) collective-permute-start(bf16[2,256,256]{2,1,0:T(8,128)(2,1)} %fusion.51), channel_id=1, source_target_pairs={{0,2},{2,0},{1,3},{3,1},{4,6},{6,4},{5,7},{7,5},{8,10},{10,8},{9,1... | collective-permute-start | bytes 786440 | tf_op jit(solution)/shard_map/ppermute | solution.py:19
  185.5 78.1 %copy-start.37 = (f32[256]{0:T(256)S(1)}, f32[256]{0:T(256)}, u32[]{:S(2)}) copy-start(f32[256]{0:T(256)} %param.13) | copy-start | bytes 3076
  186.3 81.2 %copy-start.17 = (f32[2,2,32768]{2,1,0:T(2,128)S(1)}, f32[2,2,32768]{2,1,0:T(2,128)}, u32[]{:S(2)}) copy-start(f32[2,2,32768]{2,1,0:T(2,128)} %reshape.1667) | copy-start | bytes 1572868
  186.3 81.2 %copy-start.21 = (f32[1,2,128,256]{3,1,2,0:T(2,128)S(1)}, f32[1,2,128,256]{3,1,2,0:T(2,128)}, u32[]{:S(2)}) copy-start(f32[1,2,128,256]{3,1,2,0:T(2,128)} %copy.191) | copy-start | bytes 786436
  186.3 81.2 %copy-start.22 = (f32[1,2,128,256]{3,1,2,0:T(2,128)S(1)}, f32[1,2,128,256]{3,1,2,0:T(2,128)}, u32[]{:S(2)}) copy-start(f32[1,2,128,256]{3,1,2,0:T(2,128)} %copy.192) | copy-start | bytes 786436
  262.7 4.6 %collective-permute-start.19 = (bf16[2,128,256]{2,1,0:T(8,128)(2,1)S(1)}, bf16[2,128,256]{2,1,0:T(8,128)(2,1)S(1)}, u32[]{:S(2)}, u32[]{:S(2)}) collective-permute-start(bf16[2,128,256]{2,1,0:T(8,128)(2,1)S(1)} %fusion.70), channel_id=1, source_target_pairs={{0,1},{1,0},{2,3},{3,2},{4,5},{5,4},{6,7},{7,6},{8,9},{9,8},{10,11... | collective-permute-start | bytes 393224 | tf_op jit(solution)/shard_map/ppermute | solution.py:19
  (59 other events, 420.1 us)
where the time goes:
time: 277 us; the launch traced here: 272 us
  blocking collectives  76.2 us (28%)
  local copies, waits for them, and re-layouts  59.1 us (21%)
  waiting for transfers between devices  55.6 us (20%)
  starting transfers between devices  29.6 us (11%)
  other arithmetic  27.5 us (10%)
  matrix products  21.6 us (8%)
    psum x1, blocking collectives, body(): lax.psum(jnp.sum(query_raw.astype(jnp.float32) * dq_rows, axis=0), ('dp',...  76.2 us
    ppermute x20, waiting for transfers between devices, swapped(): return lax.ppermute(block, axis, route)  55.6 us
    ppermute x20, starting transfers between devices, swapped(): return lax.ppermute(block, axis, route)  29.6 us
    unnamed x153, local copies, waits for them, and re-layouts  24.6 us
    slice x3, local copies, waits for them, and re-layouts, swap_down(): kept_half = jnp.where(lower_half, halves[:, 0], halves[:, 1])  12.9 us
    reshape x3, local copies, waits for them, and re-layouts, swap_down(): halves = sums_kv.reshape(head_count, 2, -1, sums_kv.shape[-1])  10.3 us
    dot_general x25, matrix products, pick_blocks(): jnp.einsum('hsb,hbx->hsx', table, flat, precision=lax.Precision.HIGHEST,...  10.3 us
    select_n x10, other arithmetic, swap_up(): jnp.where(lower_half, jnp.concatenate([payload, partner], axis=1), jnp.co...  9.28 us
  transfers between devices with their start and end apart: 20, of which 7 were waited for; matrix products, arithmetic and copies ran while one was open for 34% of the time, Pallas kernels for 0%

commit v1 on v0

v1 whole, which is shorter than its diff:
```python
import functools

import jax
import jax.numpy as jnp
from jax import lax
from jax.experimental import pallas as pl
from jax.experimental.pallas import tpu as pltpu
from jax.sharding import PartitionSpec as P

BLOCK = 128
LEVELS = 5
HEADS = 2
HD = 128
SCALE = HD**-0.5
ROW_Q, ROW_K, ROW_V, ROW_D, ROW_N, ROWS = 0, 128, 256, 384, 512, 528

VMEM = pl.BlockSpec(memory_space=pltpu.VMEM)
SMEM = pl.BlockSpec(memory_space=pltpu.SMEM)
NT = (((1,), (1,)), ((), ()))
TN = (((0,), (0,)), ((), ()))
NN = (((1,), (0,)), ((), ()))


def dot(left, right, dims):
    return lax.dot_general(left, right, dims, preferred_element_type=jnp.float32)


def cols(head):
    return slice(head * HD, (head + 1) * HD)


def place(offsets, me, head, level):
    half = 1 << (level - 1)
    shift = offsets[head, level] & (2 * half - 1)
    return (me & (half - 1)) == (shift >> 1), shift & 1


def block_rows(block):
    return pl.ds(pl.multiple_of(block * BLOCK, BLOCK), BLOCK)


def scale_rows(rows, gain):
    return (rows.astype(jnp.float32) * gain).astype(jnp.bfloat16)


def pack_kernel(offsets, gain, q, k, v, d, norm, *outs):
    row = lax.broadcasted_iota(jnp.int32, (16, BLOCK), 0)
    for head in range(HEADS):
        for level in range(1, LEVELS):
            out = outs[level - 1]
            block = offsets[head, level] & 1
            at = block_rows(block)
            out[head, ROW_Q : ROW_Q + BLOCK] = scale_rows(q[at, cols(head)], gain[:, cols(head)])
            out[head, ROW_K : ROW_K + BLOCK] = k[at, cols(head)]
            out[head, ROW_V : ROW_V + BLOCK] = v[at, cols(head)]
            out[head, ROW_D : ROW_D + BLOCK] = d[at, cols(head)]
            whole = jnp.where(block == 0, norm[head : head + 1, :BLOCK], norm[head : head + 1, BLOCK:])
            high = whole.astype(jnp.bfloat16).astype(jnp.float32)
            rest = whole - high
            mid = rest.astype(jnp.bfloat16).astype(jnp.float32)
            low = rest - mid
            parts = jnp.where(row == 0, high, jnp.where(row == 1, mid, jnp.where(row == 2, low, 0.0)))
            out[head, ROW_N:ROWS] = parts.astype(jnp.bfloat16)


def local_kernel(offsets, gain, q, k, v, d, norm, dq, dk, dv, norm_cols):
    me = lax.axis_index("ctx")
    for head in range(HEADS):
        c = cols(head)
        count = [jnp.float32(1.0), jnp.float32(1.0)]
        for level in range(1, LEVELS):
            active, block = place(offsets, me, head, level)
            for b in range(2):
                count[b] = count[b] + jnp.where(active & (block == b), 1.0, 0.0)
        query, key, value, dout = scale_rows(q[:, c], gain[:, c]), k[:, c], v[:, c], d[:, c]
        probs = jnp.exp(dot(key, query, NT) * SCALE - norm[head : head + 1, :])
        grads = (probs * dot(value, dout, NT)).astype(jnp.bfloat16)
        probs = probs.astype(jnp.bfloat16)
        for b in range(2):
            own, other = slice(b * BLOCK, (b + 1) * BLOCK), slice((1 - b) * BLOCK, (2 - b) * BLOCK)
            dq[own, c] = count[b] * dot(grads[own, own], key[own], TN) + dot(grads[other, own], key[other], TN)
            dk[own, c] = count[b] * dot(grads[own, own], query[own], NN) + dot(grads[own, other], query[other], NN)
            dv[own, c] = count[b] * dot(probs[own, own], dout[own], NN) + dot(probs[own, other], dout[other], NN)
        norm_cols[head] = jnp.transpose(jnp.broadcast_to(norm[head : head + 1, :], (BLOCK, 2 * BLOCK)))


def for_each_level(offsets, fn):
    me = lax.axis_index("ctx")
    for level in range(1, LEVELS):
        spots = [place(offsets, me, head, level) for head in range(HEADS)]

        def both(level=level, spots=spots):
            fn(level, spots)

        if level == 1:
            both()
        else:
            pl.when(spots[0][0] | spots[1][0])(both)


def query_kernel(offsets, gain, q, d, norm_cols, dq_in, r1, r2, r3, r4, grad_q, partial, acc):
    received = (r1, r2, r3, r4)
    acc[...] = dq_in[...]

    def one(level, spots):
        got = received[level - 1]
        for head in range(HEADS):
            active, block = spots[head]
            c, at = cols(head), block_rows(block)
            query = scale_rows(q[at, c], gain[:, c])
            key, value = got[head, ROW_K : ROW_K + BLOCK], got[head, ROW_V : ROW_V + BLOCK]
            probs = jnp.exp(dot(query, key, NT) * SCALE - norm_cols[head, at, :])
            grads = (probs * dot(d[at, c], value, NT)).astype(jnp.bfloat16)
            acc[at, c] += jnp.where(active, dot(grads, key, NN), 0.0)

    for_each_level(offsets, one)
    total = acc[...] * SCALE
    grad_q[...] = (total * gain[...]).astype(jnp.bfloat16)
    partial[...] = jnp.sum(q[...].astype(jnp.float32) * total, axis=0, keepdims=True)


def key_kernel(offsets, k, v, dk_in, dv_in, r1, r2, r3, r4, grad_k, grad_v, dk, dv):
    received = (r1, r2, r3, r4)
    dk[...] = dk_in[...]
    dv[...] = dv_in[...]

    def one(level, spots):
        got = received[level - 1]
        for head in range(HEADS):
            active, block = spots[head]
            c, at = cols(head), block_rows(block)
            query, dout = got[head, ROW_Q : ROW_Q + BLOCK], got[head, ROW_D : ROW_D + BLOCK]
            parts = got[head, ROW_N:ROWS].astype(jnp.float32)
            norm = parts[0:1] + parts[1:2] + parts[2:3]
            probs = jnp.exp(dot(k[at, c], query, NT) * SCALE - norm)
            grads = (probs * dot(v[at, c], dout, NT)).astype(jnp.bfloat16)
            dk[at, c] += jnp.where(active, dot(grads, query, NN), 0.0)
            dv[at, c] += jnp.where(active, dot(probs.astype(jnp.bfloat16), dout, NN), 0.0)

    for_each_level(offsets, one)
    grad_k[...] = (dk[...] * SCALE).astype(jnp.bfloat16)
    grad_v[...] = dv[...].astype(jnp.bfloat16)


def call(kernel, name, outs, in_specs, scratch=()):
    return pl.pallas_call(
        kernel,
        name=name,
        out_shape=outs,
        in_specs=in_specs,
        out_specs=[VMEM] * len(outs),
        scratch_shapes=list(scratch),
        compiler_params=pltpu.CompilerParams(vmem_limit_bytes=32 * 1024 * 1024),
    )


def body(queries, keys, values, grad_out, log_norm, offsets, q_gain):
    q, k, v, d = queries[0], keys[0], values[0], grad_out[0]
    norm = log_norm[0]
    tokens, width = q.shape
    gain = q_gain.reshape(1, width)
    f32 = functools.partial(jax.ShapeDtypeStruct, dtype=jnp.float32)
    bf16 = functools.partial(jax.ShapeDtypeStruct, dtype=jnp.bfloat16)
    sent = call(pack_kernel, "pack", [bf16((HEADS, ROWS, HD))] * (LEVELS - 1), [SMEM] + [VMEM] * 6)(
        offsets, gain, q, k, v, d, norm
    )
    got = []
    for level in range(1, LEVELS):
        half = 1 << (level - 1)
        route = [(i, i ^ half) for i in range(lax.axis_size("ctx"))]
        got.append(lax.ppermute(sent[level - 1], "ctx", route))
    dq, dk, dv, norm_cols = call(
        local_kernel, "local", [f32((tokens, width))] * 3 + [f32((HEADS, tokens, HD))], [SMEM] + [VMEM] * 6
    )(offsets, gain, q, k, v, d, norm)
    acc = pltpu.VMEM((tokens, width), jnp.float32)
    grad_q, partial = call(
        query_kernel, "remote_q", [bf16((tokens, width)), f32((1, width))], [SMEM] + [VMEM] * 9, [acc]
    )(offsets, gain, q, d, norm_cols, dq, *got)
    axes = ("dp", "ctx")
    everyone = lax.axis_size(axes)
    parts = lax.all_to_all(jnp.broadcast_to(partial, (everyone, width)), axes, 0, 0, tiled=True)
    grad_k, grad_v = call(
        key_kernel, "remote_kv", [bf16((tokens, width))] * 2, [SMEM] + [VMEM] * 8, [acc, acc]
    )(offsets, k, v, dk, dv, *got)
    return (grad_q[None], grad_k[None], grad_v[None], jnp.sum(parts, axis=0))


def solution(mesh):
    rows = P("dp", "ctx", None)
    in_specs = (rows, rows, rows, rows, P("dp", None, "ctx"), P(), P())
    out_specs = (rows, rows, rows, P())
    return jax.shard_map(body, mesh=mesh, in_specs=in_specs, out_specs=out_specs, check_vma=False)
```

time: 277 us -> 47.3 us (0.17); the launches traced: 272 us -> 47.1 us
  blocking collectives: 76.2 us -> 0 us
  local copies, waits for them, and re-layouts: 59.1 us -> 5.03 us
  waiting for transfers between devices: 55.6 us -> 17.5 us
  other arithmetic: 27.5 us -> 0.71 us
  matrix products: 21.6 us -> 0 us
  starting transfers between devices: 29.6 us -> 16.5 us
  Pallas kernels: 0 us -> 6.59 us
    psum x1 -> x0, blocking collectives: 76.2 us -> none  [body(): lax.psum(jnp.sum(query_raw.astype(jnp.float32) * dq_rows, axis=0), ('dp',...]
    ppermute x20 -> x4, waiting for transfers between devices: 55.6 us -> 9.61 us  [body(): got.append(lax.ppermute(sent[level - 1], 'ctx', route))]
    dot_general x52 -> x0, matrix products: 21.6 us -> none  [the longest x25 10.3 us: pick_blocks(): jnp.einsum('hsb,hbx->hsx', table, flat, precision=lax.Precision.HIGHEST,...]
    unnamed x153 -> x20, local copies, waits for them, and re-layouts: 24.6 us -> 4.31 us
    ppermute x20 -> x4, starting transfers between devices: 29.6 us -> 9.51 us  [body(): got.append(lax.ppermute(sent[level - 1], 'ctx', route))]
    slice x4 -> x0, local copies, waits for them, and re-layouts: 12.9 us -> none  [the longest x3 12.9 us: swap_down(): kept_half = jnp.where(lower_half, halves[:, 0], halves[:, 1])]
    reshape x7 -> x0, local copies, waits for them, and re-layouts: 11.9 us -> none  [the longest x3 10.3 us: swap_down(): halves = sums_kv.reshape(head_count, 2, -1, sums_kv.shape[-1])]
    select_n x12 -> x0, other arithmetic: 9.29 us -> none  [the longest x10 9.28 us: swap_up(): jnp.where(lower_half, jnp.concatenate([payload, partner], axis=1), jnp.co...]
  transfers between devices with their start and end apart: 20 -> 5, of which waited for: 7 -> 3; matrix products, arithmetic and copies ran while one was open for 34% -> 0% of each run, Pallas kernels for 0% -> 8%
where the time goes in v1:
time: 47.3 us; the launch traced here: 47.1 us
  waiting for transfers between devices  17.5 us (37%)
  starting transfers between devices  16.5 us (35%)
  Pallas kernels  6.59 us (14%)
  local copies, waits for them, and re-layouts  5.03 us (11%)
  other arithmetic  0.71 us (2%)
  between operations  0.71 us (2%)
    ppermute x4, waiting for transfers between devices, body(): got.append(lax.ppermute(sent[level - 1], 'ctx', route))  9.61 us
    ppermute x4, starting transfers between devices, body(): got.append(lax.ppermute(sent[level - 1], 'ctx', route))  9.51 us
    all_to_all x1, waiting for transfers between devices, body(): lax.all_to_all(jnp.broadcast_to(partial, (everyone, width)), axes, 0, 0,...  7.94 us
    all_to_all x1, starting transfers between devices, body(): lax.all_to_all(jnp.broadcast_to(partial, (everyone, width)), axes, 0, 0,...  7.02 us
    unnamed x20, local copies, waits for them, and re-layouts  4.31 us
    pallas_call x1, Pallas kernels, body(): call(key_kernel, 'remote_kv', [bf16((tokens, width))] * 2, [SMEM] + [VMEM...  2.25 us
    pallas_call x1, Pallas kernels, body(): call(query_kernel, 'remote_q', [bf16((tokens, width)), f32((1, width))],...  2.18 us
    pallas_call x1, Pallas kernels, body(): call(local_kernel, 'local', [f32((tokens, width))] * 3 + [f32((HEADS, tok...  1.43 us
  transfers between devices with their start and end apart: 5, of which 3 were waited for; matrix products, arithmetic and copies ran while one was open for 0% of the time, Pallas kernels for 8%

profile of v1, /device:TPU:1, one launch (start us, length us, event | category | flops | bytes accessed | tf_op | source)
XLA Modules:
  0.0 47.1 jit_solution(5679755167392804785)
XLA Ops:
  0.6 0.0 copy-start.9
  0.7 0.7 %copy-done.9 = f32[1,2,256]{2,1,0:T(2,128)S(1)} copy-done((f32[1,2,256]{2,1,0:T(2,128)S(1)}, f32[1,2,256]{2,1,0:T(2,128)}, u32[]{:S(2)}) %copy-start.9) | copy-done | bytes 2072
  1.3 0.0 copy-done.8
  1.3 0.0 copy-done.7
  1.3 0.9 %copy-done = bf16[1,256,256]{2,1,0:T(8,128)(2,1)S(1)} copy-done((bf16[1,256,256]{2,1,0:T(8,128)(2,1)S(1)}, bf16[1,256,256]{2,1,0:T(8,128)(2,1)}, u32[]{:S(2)}) %copy-start) | copy-done | bytes 131096
  2.2 0.9 %copy-done.1 = bf16[1,256,256]{2,1,0:T(8,128)(2,1)S(1)} copy-done((bf16[1,256,256]{2,1,0:T(8,128)(2,1)S(1)}, bf16[1,256,256]{2,1,0:T(8,128)(2,1)}, u32[]{:S(2)}) %copy-start.1) | copy-done | bytes 131096
  3.2 0.9 %copy-done.3 = bf16[1,256,256]{2,1,0:T(8,128)(2,1)S(1)} copy-done((bf16[1,256,256]{2,1,0:T(8,128)(2,1)S(1)}, bf16[1,256,256]{2,1,0:T(8,128)(2,1)}, u32[]{:S(2)}) %copy-start.3) | copy-done | bytes 131096
  4.1 0.9 %copy-done.5 = bf16[1,256,256]{2,1,0:T(8,128)(2,1)S(1)} copy-done((bf16[1,256,256]{2,1,0:T(8,128)(2,1)S(1)}, bf16[1,256,256]{2,1,0:T(8,128)(2,1)}, u32[]{:S(2)}) %copy-start.5) | copy-done | bytes 131096
  5.0 0.7 %pack.1 = (bf16[2,528,128]{2,1,0:T(8,128)(2,1)S(1)}, bf16[2,528,128]{2,1,0:T(8,128)(2,1)S(1)}, bf16[2,528,128]{2,1,0:T(8,128)(2,1)S(1)}, bf16[2,528,128]{2,1,0:T(8,128)(2,1)S(1)}) custom-call(s32[2,5]{1,0:T(2,128)S(1)} %copy-done.7, f32[1,256]{1,0:T(1,128)S(1)} %bitcast.22, bf16[256,256]{1,0:T(8,128)(2,1)S(1)} %bitcast.10, bf16[256,256]{1,0:T(8,128)(2,1)S(1)} %bitcast.16, ...), custom_call_target="tpu_custom_call" | custom-call | tf_op jit(solution)/shard_map/pack/pallas_call | solution.py:164
  5.7 2.1 %collective-permute-start = (bf16[2,528,128]{2,1,0:T(8,128)(2,1)S(1)}, bf16[2,528,128]{2,1,0:T(8,128)(2,1)S(1)}, u32[]{:S(2)}, u32[]{:S(2)}) collective-permute-start(bf16[2,528,128]{2,1,0:T(8,128)(2,1)S(1)} %get-tuple-element.18), channel_id=1, source_target_pairs={{0,1},{1,0},{2,3},{3,2},{4,5},{5,4},{6,7},{7,6},{8,9},{9,8},{10,11... | collective-permute-start | bytes 811016 | tf_op jit(solution)/shard_map/ppermute | solution.py:171
  7.8 2.5 %collective-permute-start.1 = (bf16[2,528,128]{2,1,0:T(8,128)(2,1)S(1)}, bf16[2,528,128]{2,1,0:T(8,128)(2,1)S(1)}, u32[]{:S(2)}, u32[]{:S(2)}) collective-permute-start(bf16[2,528,128]{2,1,0:T(8,128)(2,1)S(1)} %get-tuple-element.19), channel_id=1, source_target_pairs={{0,2},{1,3},{2,0},{3,1},{4,6},{5,7},{6,4},{7,5},{8,10},{9,11},{10,... | collective-permute-start | bytes 811016 | tf_op jit(solution)/shard_map/ppermute | solution.py:171
  10.3 1.6 %collective-permute-start.2 = (bf16[2,528,128]{2,1,0:T(8,128)(2,1)S(1)}, bf16[2,528,128]{2,1,0:T(8,128)(2,1)S(1)}, u32[]{:S(2)}, u32[]{:S(2)}) collective-permute-start(bf16[2,528,128]{2,1,0:T(8,128)(2,1)S(1)} %get-tuple-element.20), channel_id=1, source_target_pairs={{0,4},{1,5},{2,6},{3,7},{4,0},{5,1},{6,2},{7,3},{8,12},{9,13},{10,... | collective-permute-start | bytes 811016 | tf_op jit(solution)/shard_map/ppermute | solution.py:171
  11.9 3.3 %collective-permute-start.3 = (bf16[2,528,128]{2,1,0:T(8,128)(2,1)S(1)}, bf16[2,528,128]{2,1,0:T(8,128)(2,1)S(1)}, u32[]{:S(2)}, u32[]{:S(2)}) collective-permute-start(bf16[2,528,128]{2,1,0:T(8,128)(2,1)S(1)} %get-tuple-element.21), channel_id=1, source_target_pairs={{0,8},{1,9},{2,10},{3,11},{4,12},{5,13},{6,14},{7,15},{8,0},{9,1},... | collective-permute-start | bytes 811016 | tf_op jit(solution)/shard_map/ppermute | solution.py:171
  15.2 1.4 %local.1 = (f32[256,256]{1,0:T(8,128)S(1)}, f32[256,256]{1,0:T(8,128)S(1)}, f32[256,256]{1,0:T(8,128)S(1)}, f32[2,256,128]{2,1,0:T(8,128)S(1)}) custom-call(s32[2,5]{1,0:T(2,128)S(1)} %copy-done.7, f32[1,256]{1,0:T(1,128)S(1)} %bitcast.23, bf16[256,256]{1,0:T(8,128)(2,1)S(1)} %bitcast.11, bf16[256,256]{1,0:T(8,128)(2,1)S(1)} %bitcast.17, ...), custom_call_target="tpu_custom_call" | custom-call | tf_op jit(solution)/shard_map/local/pallas_call | solution.py:172
  16.7 0.0 collective-permute-done.r1
  16.7 5.3 %collective-permute-done.1.r2 = bf16[2,528,128]{2,1,0:T(8,128)(2,1)S(1)} collective-permute-done((bf16[2,528,128]{2,1,0:T(8,128)(2,1)S(1)}, bf16[2,528,128]{2,1,0:T(8,128)(2,1)S(1)}, u32[]{:S(2)}, u32[]{:S(2)}) %collective-permute-start.1) | collective-permute-done | bytes 270368 | tf_op jit(solution)/shard_map/ppermute | solution.py:171
  21.9 0.0 collective-permute-done.2.r3
  21.9 4.3 %collective-permute-done.3.r4 = bf16[2,528,128]{2,1,0:T(8,128)(2,1)S(1)} collective-permute-done((bf16[2,528,128]{2,1,0:T(8,128)(2,1)S(1)}, bf16[2,528,128]{2,1,0:T(8,128)(2,1)S(1)}, u32[]{:S(2)}, u32[]{:S(2)}) %collective-permute-start.3) | collective-permute-done | bytes 270368 | tf_op jit(solution)/shard_map/ppermute | solution.py:171
  26.3 2.2 %remote_q.1 = (bf16[256,256]{1,0:T(8,128)(2,1)}, f32[1,256]{1,0:T(1,128)S(1)}) custom-call(s32[2,5]{1,0:T(2,128)S(1)} %copy-done.7, f32[1,256]{1,0:T(1,128)S(1)} %bitcast.24, bf16[256,256]{1,0:T(8,128)(2,1)S(1)} %bitcast.12, bf16[256,256]{1,0:T(8,128)(2,1)S(1)} %bitcast.15, f32[2,256,128]{2,1,0:T(8,128)S(1)} %get-tuple-element.16.norm_cols, ...), custom_call_target="tpu_custom_call" | custom-call | tf_op jit(solution)/shard_map/remote_q/pallas_call | solution.py:176
  28.5 0.7 %broadcast_in_dim.17 = f32[128,1,256]{2,1,0:T(1,128)} broadcast(f32[256]{0:T(256)S(1)} %bitcast.27), dimensions={2} | broadcast | bytes 132096 | tf_op jit(solution)/shard_map/broadcast_in_dim | solution.py:181
  29.2 7.0 %all-to-all-start = ((f32[128,1,256]{2,1,0:T(1,128)}), f32[128,1,256]{2,1,0:T(1,128)S(1)}, u32[]{:S(2)}, u32[]{:S(2)}) async-start(f32[128,1,256]{2,1,0:T(1,128)} %broadcast_in_dim.17), calls=%async_computation | async-start | bytes 262144 | tf_op jit(solution)/shard_map/all_to_all | solution.py:181
  36.2 2.2 %remote_kv.1 = (bf16[256,256]{1,0:T(8,128)(2,1)}, bf16[256,256]{1,0:T(8,128)(2,1)}) custom-call(s32[2,5]{1,0:T(2,128)S(1)} %copy-done.7, bf16[256,256]{1,0:T(8,128)(2,1)S(1)} %bitcast.18, bf16[256,256]{1,0:T(8,128)(2,1)S(1)} %bitcast.21, f32[256,256]{1,0:T(8,128)S(1)} %get-tuple-element.23.dk_in, f32[256,256]{1,0:T(8,128)S(1)} %get-tuple-element.24.dv_in, ...), custom_call_target="tpu_custom_call" | custom-call | tf_op jit(solution)/shard_map/remote_kv/pallas_call | solution.py:182
  38.5 7.9 %all-to-all-done = f32[128,1,256]{2,1,0:T(1,128)S(1)} async-done(((f32[128,1,256]{2,1,0:T(1,128)}), f32[128,1,256]{2,1,0:T(1,128)S(1)}, u32[]{:S(2)}, u32[]{:S(2)}) %all-to-all-start) | async-done | bytes 131104 | tf_op jit(solution)/shard_map/all_to_all | solution.py:181
  46.4 0.7 %reduce_sum.9 = f32[256]{0:T(256)} reduce(f32[128,1,256]{2,1,0:T(1,128)S(1)} %all-to-all-done, f32[]{:T(128)} %constant.0.clone.1), dimensions={0,1}, to_apply=%region_0.0 | reduce | flops 32512 | bytes 132100 | tf_op jit(solution)/shard_map/reduce_sum | solution.py:185
  (12 shorter events, 0.0 us)
Async XLA Ops:
  0.6 0.7 %copy-start.9 = (f32[1,2,256]{2,1,0:T(2,128)S(1)}, f32[1,2,256]{2,1,0:T(2,128)}, u32[]{:S(2)}) copy-start(f32[1,2,256]{2,1,0:T(2,128)} %param.11) | copy-start | bytes 6148
  0.6 0.7 %copy-start.8 = (f32[256]{0:T(256)S(1)}, f32[256]{0:T(256)}, u32[]{:S(2)}) copy-start(f32[256]{0:T(256)} %param.13) | copy-start | bytes 3076
  0.7 0.7 %copy-start.7 = (s32[2,5]{1,0:T(2,128)S(1)}, s32[2,5]{1,0:T(2,128)}, u32[]{:S(2)}) copy-start(s32[2,5]{1,0:T(2,128)} %offsets.7) | copy-start | bytes 124
  1.3 0.9 %copy-start = (bf16[1,256,256]{2,1,0:T(8,128)(2,1)S(1)}, bf16[1,256,256]{2,1,0:T(8,128)(2,1)}, u32[]{:S(2)}) copy-start(bf16[1,256,256]{2,1,0:T(8,128)(2,1)} %param.7) | copy-start | bytes 393220
  2.2 0.9 %copy-start.1 = (bf16[1,256,256]{2,1,0:T(8,128)(2,1)S(1)}, bf16[1,256,256]{2,1,0:T(8,128)(2,1)}, u32[]{:S(2)}) copy-start(bf16[1,256,256]{2,1,0:T(8,128)(2,1)} %param.10) | copy-start | bytes 393220
  3.2 0.9 %copy-start.3 = (bf16[1,256,256]{2,1,0:T(8,128)(2,1)S(1)}, bf16[1,256,256]{2,1,0:T(8,128)(2,1)}, u32[]{:S(2)}) copy-start(bf16[1,256,256]{2,1,0:T(8,128)(2,1)} %param.8) | copy-start | bytes 393220
  4.1 0.9 %copy-start.5 = (bf16[1,256,256]{2,1,0:T(8,128)(2,1)S(1)}, bf16[1,256,256]{2,1,0:T(8,128)(2,1)}, u32[]{:S(2)}) copy-start(bf16[1,256,256]{2,1,0:T(8,128)(2,1)} %param.9) | copy-start | bytes 393220
  5.7 11.0 %collective-permute-start = (bf16[2,528,128]{2,1,0:T(8,128)(2,1)S(1)}, bf16[2,528,128]{2,1,0:T(8,128)(2,1)S(1)}, u32[]{:S(2)}, u32[]{:S(2)}) collective-permute-start(bf16[2,528,128]{2,1,0:T(8,128)(2,1)S(1)} %get-tuple-element.18), channel_id=1, source_target_pairs={{0,1},{1,0},{2,3},{3,2},{4,5},{5,4},{6,7},{7,6},{8,9},{9,8},{10,11... | collective-permute-start | bytes 811016 | tf_op jit(solution)/shard_map/ppermute | solution.py:171
  7.8 14.1 %collective-permute-start.1 = (bf16[2,528,128]{2,1,0:T(8,128)(2,1)S(1)}, bf16[2,528,128]{2,1,0:T(8,128)(2,1)S(1)}, u32[]{:S(2)}, u32[]{:S(2)}) collective-permute-start(bf16[2,528,128]{2,1,0:T(8,128)(2,1)S(1)} %get-tuple-element.19), channel_id=1, source_target_pairs={{0,2},{1,3},{2,0},{3,1},{4,6},{5,7},{6,4},{7,5},{8,10},{9,11},{10,... | collective-permute-start | bytes 811016 | tf_op jit(solution)/shard_map/ppermute | solution.py:171
  10.3 11.7 %collective-permute-start.2 = (bf16[2,528,128]{2,1,0:T(8,128)(2,1)S(1)}, bf16[2,528,128]{2,1,0:T(8,128)(2,1)S(1)}, u32[]{:S(2)}, u32[]{:S(2)}) collective-permute-start(bf16[2,528,128]{2,1,0:T(8,128)(2,1)S(1)} %get-tuple-element.20), channel_id=1, source_target_pairs={{0,4},{1,5},{2,6},{3,7},{4,0},{5,1},{6,2},{7,3},{8,12},{9,13},{10,... | collective-permute-start | bytes 811016 | tf_op jit(solution)/shard_map/ppermute | solution.py:171
  11.9 14.4 %copy-start.2 = (bf16[1,256,256]{2,1,0:T(8,128)(2,1)S(1)}, bf16[1,256,256]{2,1,0:T(8,128)(2,1)}, u32[]{:S(2)}) copy-start(bf16[1,256,256]{2,1,0:T(8,128)(2,1)} %param.10) | copy-start | bytes 393220
  11.9 14.4 %collective-permute-start.3 = (bf16[2,528,128]{2,1,0:T(8,128)(2,1)S(1)}, bf16[2,528,128]{2,1,0:T(8,128)(2,1)S(1)}, u32[]{:S(2)}, u32[]{:S(2)}) collective-permute-start(bf16[2,528,128]{2,1,0:T(8,128)(2,1)S(1)} %get-tuple-element.21), channel_id=1, source_target_pairs={{0,8},{1,9},{2,10},{3,11},{4,12},{5,13},{6,14},{7,15},{8,0},{9,1},... | collective-permute-start | bytes 811016 | tf_op jit(solution)/shard_map/ppermute | solution.py:171
  29.2 7.0 %copy-start.4 = (bf16[1,256,256]{2,1,0:T(8,128)(2,1)S(1)}, bf16[1,256,256]{2,1,0:T(8,128)(2,1)}, u32[]{:S(2)}) copy-start(bf16[1,256,256]{2,1,0:T(8,128)(2,1)} %param.8) | copy-start | bytes 393220
  29.2 7.0 %copy-start.6 = (bf16[1,256,256]{2,1,0:T(8,128)(2,1)S(1)}, bf16[1,256,256]{2,1,0:T(8,128)(2,1)}, u32[]{:S(2)}) copy-start(bf16[1,256,256]{2,1,0:T(8,128)(2,1)} %param.9) | copy-start | bytes 393220
  29.2 17.2 %all-to-all-start = ((f32[128,1,256]{2,1,0:T(1,128)}), f32[128,1,256]{2,1,0:T(1,128)S(1)}, u32[]{:S(2)}, u32[]{:S(2)}) async-start(f32[128,1,256]{2,1,0:T(1,128)} %broadcast_in_dim.17), calls=%async_computation | async-start | bytes 262144 | tf_op jit(solution)/shard_map/all_to_all | solution.py:181

commit v2 on v1

v2 whole, which is shorter than its diff:
```python
import functools

import jax
import jax.numpy as jnp
from jax import lax
from jax.experimental import pallas as pl
from jax.experimental.pallas import tpu as pltpu
from jax.sharding import PartitionSpec as P

BLOCK = 128
LEVELS = 5
HEADS = 2
HD = 128
SCALE = HD**-0.5
ROW_Q, ROW_D, ROW_N, ROWS = 0, 128, 256, 272

HBM = pl.BlockSpec(memory_space=pltpu.HBM)
VMEM = pl.BlockSpec(memory_space=pltpu.VMEM)
SMEM = pl.BlockSpec(memory_space=pltpu.SMEM)
NT = (((1,), (1,)), ((), ()))
TN = (((0,), (0,)), ((), ()))
NN = (((1,), (0,)), ((), ()))


def dot(left, right, dims):
    return lax.dot_general(left, right, dims, preferred_element_type=jnp.float32)


def cols(head):
    return slice(head * HD, (head + 1) * HD)


def place(offsets, me, head, level):
    half = 1 << (level - 1)
    shift = offsets[head, level] & (2 * half - 1)
    return (me & (half - 1)) == (shift >> 1), shift & 1


def block_rows(block):
    return pl.ds(pl.multiple_of(block * BLOCK, BLOCK), BLOCK)


def scale_rows(rows, gain):
    return (rows.astype(jnp.float32) * gain).astype(jnp.bfloat16)


def copy_blocks(offsets, sources, outs, sems):
    copies = []
    for level in range(1, LEVELS):
        for head in range(HEADS):
            at = block_rows(offsets[head, level] & 1)
            for i, source in enumerate(sources):
                copies.append(
                    pltpu.make_async_copy(
                        source.at[at, cols(head)],
                        outs[level - 1].at[head, i * BLOCK : (i + 1) * BLOCK],
                        sems.at[level - 1, head, i],
                    )
                )
    for copy in copies:
        copy.start()
    return copies


def pack_kv_kernel(offsets, k, v, *refs):
    for copy in copy_blocks(offsets, (k, v), refs[:-1], refs[-1]):
        copy.wait()


def pack_qd_kernel(offsets, q, d, norm, *refs):
    outs, sems = refs[:-1], refs[-1]
    copies = copy_blocks(offsets, (q, d), outs, sems)
    row = lax.broadcasted_iota(jnp.int32, (16, BLOCK), 0)
    for head in range(HEADS):
        for level in range(1, LEVELS):
            block = offsets[head, level] & 1
            whole = jnp.where(block == 0, norm[head : head + 1, :BLOCK], norm[head : head + 1, BLOCK:])
            high = whole.astype(jnp.bfloat16).astype(jnp.float32)
            rest = whole - high
            mid = rest.astype(jnp.bfloat16).astype(jnp.float32)
            low = rest - mid
            parts = jnp.where(row == 0, high, jnp.where(row == 1, mid, jnp.where(row == 2, low, 0.0)))
            outs[level - 1][head, ROW_N:ROWS] = parts.astype(jnp.bfloat16)
    for copy in copies:
        copy.wait()


def local_kernel(offsets, gain, q, k, v, d, norm, dq, dk, dv, norm_cols, scaled):
    me = lax.axis_index("ctx")
    for head in range(HEADS):
        c = cols(head)
        count = [jnp.float32(1.0), jnp.float32(1.0)]
        for level in range(1, LEVELS):
            active, block = place(offsets, me, head, level)
            for b in range(2):
                count[b] = count[b] + jnp.where(active & (block == b), 1.0, 0.0)
        query, key, value, dout = scale_rows(q[:, c], gain[:, c]), k[:, c], v[:, c], d[:, c]
        scaled[:, c] = query
        probs = jnp.exp(dot(key, query, NT) * SCALE - norm[head : head + 1, :])
        grads = (probs * dot(value, dout, NT)).astype(jnp.bfloat16)
        probs = probs.astype(jnp.bfloat16)
        for b in range(2):
            own, other = slice(b * BLOCK, (b + 1) * BLOCK), slice((1 - b) * BLOCK, (2 - b) * BLOCK)
            dq[own, c] = count[b] * dot(grads[own, own], key[own], TN) + dot(grads[other, own], key[other], TN)
            dk[own, c] = count[b] * dot(grads[own, own], query[own], NN) + dot(grads[own, other], query[other], NN)
            dv[own, c] = count[b] * dot(probs[own, own], dout[own], NN) + dot(probs[own, other], dout[other], NN)
        norm_cols[head] = jnp.transpose(jnp.broadcast_to(norm[head : head + 1, :], (BLOCK, 2 * BLOCK)))


def for_each_level(offsets, fn):
    me = lax.axis_index("ctx")
    for level in range(1, LEVELS):
        spots = [place(offsets, me, head, level) for head in range(HEADS)]

        def both(level=level, spots=spots):
            fn(level, spots)

        if level == 1:
            both()
        else:
            pl.when(spots[0][0] | spots[1][0])(both)


def query_kernel(offsets, scaled, q, d, norm_cols, dq_in, r1, r2, r3, r4, dq, partial):
    received = (r1, r2, r3, r4)
    dq[...] = dq_in[...]

    def one(level, spots):
        got = received[level - 1]
        for head in range(HEADS):
            active, block = spots[head]
            c, at = cols(head), block_rows(block)
            key, value = got[head, :BLOCK], got[head, BLOCK:]
            probs = jnp.exp(dot(scaled[at, c], key, NT) * SCALE - norm_cols[head, at, :])
            grads = (probs * dot(d[at, c], value, NT)).astype(jnp.bfloat16)
            dq[at, c] += jnp.where(active, dot(grads, key, NN), 0.0)

    for_each_level(offsets, one)
    total = jnp.sum(q[...].astype(jnp.float32) * (dq[...] * SCALE), axis=0, keepdims=True)
    partial[...] = jnp.broadcast_to(total[None], partial.shape)


def key_kernel(offsets, gain, k, v, dq, dk_in, dv_in, r1, r2, r3, r4, grad_q, grad_k, grad_v, dk, dv):
    received = (r1, r2, r3, r4)
    dk[...] = dk_in[...]
    dv[...] = dv_in[...]
    grad_q[...] = (dq[...] * SCALE * gain[...]).astype(jnp.bfloat16)

    def one(level, spots):
        got = received[level - 1]
        for head in range(HEADS):
            active, block = spots[head]
            c, at = cols(head), block_rows(block)
            query = scale_rows(got[head, ROW_Q : ROW_Q + BLOCK], gain[:, c])
            dout = got[head, ROW_D : ROW_D + BLOCK]
            parts = got[head, ROW_N:ROWS].astype(jnp.float32)
            norm = parts[0:1] + parts[1:2] + parts[2:3]
            probs = jnp.exp(dot(k[at, c], query, NT) * SCALE - norm)
            grads = (probs * dot(v[at, c], dout, NT)).astype(jnp.bfloat16)
            dk[at, c] += jnp.where(active, dot(grads, query, NN), 0.0)
            dv[at, c] += jnp.where(active, dot(probs.astype(jnp.bfloat16), dout, NN), 0.0)

    for_each_level(offsets, one)
    grad_k[...] = (dk[...] * SCALE).astype(jnp.bfloat16)
    grad_v[...] = dv[...].astype(jnp.bfloat16)


def call(kernel, name, outs, in_specs, scratch=()):
    return pl.pallas_call(
        kernel,
        name=name,
        out_shape=outs,
        in_specs=in_specs,
        out_specs=[VMEM] * len(outs),
        scratch_shapes=list(scratch),
        compiler_params=pltpu.CompilerParams(vmem_limit_bytes=32 * 1024 * 1024),
    )


def swap(payloads):
    count = lax.axis_size("ctx")
    return [lax.ppermute(p, "ctx", [(i, i ^ (1 << n)) for i in range(count)]) for n, p in enumerate(payloads)]


def body(queries, keys, values, grad_out, log_norm, offsets, q_gain):
    q, k, v, d = queries[0], keys[0], values[0], grad_out[0]
    norm = log_norm[0]
    tokens, width = q.shape
    gain = q_gain.reshape(1, width)
    f32 = functools.partial(jax.ShapeDtypeStruct, dtype=jnp.float32)
    bf16 = functools.partial(jax.ShapeDtypeStruct, dtype=jnp.bfloat16)
    sems = pltpu.SemaphoreType.DMA((LEVELS - 1, HEADS, 2))
    sent = call(pack_kv_kernel, "pack_kv", [bf16((HEADS, 2 * BLOCK, HD))] * (LEVELS - 1), [SMEM, HBM, HBM], [sems])(
        offsets, k, v
    )
    got_kv = swap(sent)
    sent = call(pack_qd_kernel, "pack_qd", [bf16((HEADS, ROWS, HD))] * (LEVELS - 1), [SMEM, HBM, HBM, VMEM], [sems])(
        offsets, q, d, norm
    )
    got_qd = swap(sent)
    dq, dk, dv, norm_cols, scaled = call(
        local_kernel,
        "local",
        [f32((tokens, width))] * 3 + [f32((HEADS, tokens, HD)), bf16((tokens, width))],
        [SMEM] + [VMEM] * 6,
    )(offsets, gain, q, k, v, d, norm)
    axes = ("dp", "ctx")
    everyone = lax.axis_size(axes)
    dq, partial = call(
        query_kernel, "remote_q", [f32((tokens, width)), f32((everyone, 1, width))], [SMEM] + [VMEM] * 9
    )(offsets, scaled, q, d, norm_cols, dq, *got_kv)
    parts = lax.all_to_all(partial, axes, 0, 0, tiled=True)
    acc = pltpu.VMEM((tokens, width), jnp.float32)
    grad_q, grad_k, grad_v = call(
        key_kernel, "remote_kv", [bf16((tokens, width))] * 3, [SMEM] + [VMEM] * 10, [acc, acc]
    )(offsets, gain, k, v, dq, dk, dv, *got_qd)
    return (grad_q[None], grad_k[None], grad_v[None], jnp.sum(parts, axis=(0, 1)))


def solution(mesh):
    rows = P("dp", "ctx", None)
    in_specs = (rows, rows, rows, rows, P("dp", None, "ctx"), P(), P())
    out_specs = (rows, rows, rows, P())
    return jax.shard_map(body, mesh=mesh, in_specs=in_specs, out_specs=out_specs, check_vma=False)
```

time: 47.3 us -> 44.5 us (0.941)
  waiting for transfers between devices: 17.5 us -> 7.39 us
  starting transfers between devices: 16.5 us -> 23.7 us
  Pallas kernels: 6.59 us -> 8.53 us
  local copies, waits for them, and re-layouts: 5.03 us -> 3.18 us
    ppermute x4 -> x8, waiting for transfers between devices: 9.61 us -> 0.02 us  [swap(): lax.ppermute(p, 'ctx', [(i, i ^ 1 << n) for i in range(count)])]
    ppermute x4 -> x8, starting transfers between devices: 9.51 us -> 13.6 us  [swap(): lax.ppermute(p, 'ctx', [(i, i ^ 1 << n) for i in range(count)])]
    all_to_all x1, starting transfers between devices: 7.02 us -> 10.1 us  [body(): parts = lax.all_to_all(partial, axes, 0, 0, tiled=True)]
    pallas_call x3 -> x4, Pallas kernels: 5.16 us -> 7.1 us  [the longest x1 2.78 us: body(): call(key_kernel, 'remote_kv', [bf16((tokens, width))] * 3, [SMEM] + [VMEM...]
    unnamed x20 -> x18, local copies, waits for them, and re-layouts: 4.31 us -> 3.18 us
    broadcast_in_dim x1 -> x0, local copies, waits for them, and re-layouts: 0.72 us -> none  [body(): jnp.broadcast_to(partial, (everyone, width))]
    all_to_all x1, waiting for transfers between devices: 7.94 us -> 7.37 us  [body(): parts = lax.all_to_all(partial, axes, 0, 0, tiled=True)]
  transfers between devices with their start and end apart: 5 -> 9, of which waited for: 3 -> 1; matrix products, arithmetic and copies ran while one was open for 0% -> 0% of each run, Pallas kernels for 8% -> 17%
where the time goes in v2:
time: 44.5 us; the launch traced here: 44.3 us
  starting transfers between devices  23.7 us (53%)
  Pallas kernels  8.53 us (19%)
  waiting for transfers between devices  7.39 us (17%)
  local copies, waits for them, and re-layouts  3.18 us (7%)
  between operations  0.76 us (2%)
  other arithmetic  0.71 us (2%)
    ppermute x8, starting transfers between devices, swap(): lax.ppermute(p, 'ctx', [(i, i ^ 1 << n) for i in range(count)])  13.6 us
    all_to_all x1, starting transfers between devices, body(): parts = lax.all_to_all(partial, axes, 0, 0, tiled=True)  10.1 us
    all_to_all x1, waiting for transfers between devices, body(): parts = lax.all_to_all(partial, axes, 0, 0, tiled=True)  7.37 us
    unnamed x18, local copies, waits for them, and re-layouts  3.18 us
    pallas_call x1, Pallas kernels, body(): call(key_kernel, 'remote_kv', [bf16((tokens, width))] * 3, [SMEM] + [VMEM...  2.78 us
    pallas_call x1, Pallas kernels, body(): call(query_kernel, 'remote_q', [f32((tokens, width)), f32((everyone, 1, w...  2.64 us
    pallas_call x1, Pallas kernels, body(): call(local_kernel, 'local', [f32((tokens, width))] * 3 + [f32((HEADS, tok...  1.43 us
  transfers between devices with their start and end apart: 9, of which 1 were waited for; matrix products, arithmetic and copies ran while one was open for 0% of the time, Pallas kernels for 17%

profile of v2, /device:TPU:1, one launch (start us, length us, event | category | flops | bytes accessed | tf_op | source)
XLA Modules:
  0.0 44.3 jit_solution(11611315387496866557)
XLA Ops:
  0.6 0.7 %copy-done.6 = s32[2,5]{1,0:T(2,128)S(1)} copy-done((s32[2,5]{1,0:T(2,128)S(1)}, s32[2,5]{1,0:T(2,128)}, u32[]{:S(2)}) %copy-start.6) | copy-done | bytes 64
  1.3 0.9 %copy-done.2 = bf16[1,256,256]{2,1,0:T(8,128)(2,1)S(1)} copy-done((bf16[1,256,256]{2,1,0:T(8,128)(2,1)S(1)}, bf16[1,256,256]{2,1,0:T(8,128)(2,1)}, u32[]{:S(2)}) %copy-start.2) | copy-done | bytes 131096
  2.2 0.9 %copy-done.4 = bf16[1,256,256]{2,1,0:T(8,128)(2,1)S(1)} copy-done((bf16[1,256,256]{2,1,0:T(8,128)(2,1)S(1)}, bf16[1,256,256]{2,1,0:T(8,128)(2,1)}, u32[]{:S(2)}) %copy-start.4) | copy-done | bytes 131096
  3.1 0.8 %pack_kv.1 = (bf16[2,256,128]{2,1,0:T(8,128)(2,1)S(1)}, bf16[2,256,128]{2,1,0:T(8,128)(2,1)S(1)}, bf16[2,256,128]{2,1,0:T(8,128)(2,1)S(1)}, bf16[2,256,128]{2,1,0:T(8,128)(2,1)S(1)}) custom-call(s32[2,5]{1,0:T(2,128)S(1)} %copy-done.6, bf16[256,256]{1,0:T(8,128)(2,1)S(1)} %bitcast.15, bf16[256,256]{1,0:T(8,128)(2,1)S(1)} %bitcast.18), custom_call_target="tpu_custom_call" | custom-call | tf_op jit(solution)/shard_map/pack_kv/pallas_call | solution.py:193
  4.0 2.1 %collective-permute-start = (bf16[2,256,128]{2,1,0:T(8,128)(2,1)S(1)}, bf16[2,256,128]{2,1,0:T(8,128)(2,1)S(1)}, u32[]{:S(2)}, u32[]{:S(2)}) collective-permute-start(bf16[2,256,128]{2,1,0:T(8,128)(2,1)S(1)} %get-tuple-element.25), channel_id=1, source_target_pairs={{0,1},{1,0},{2,3},{3,2},{4,5},{5,4},{6,7},{7,6},{8,9},{9,8},{10,11... | collective-permute-start | bytes 393224 | tf_op jit(solution)/shard_map/ppermute | solution.py:182
  6.1 2.5 %collective-permute-start.1 = (bf16[2,256,128]{2,1,0:T(8,128)(2,1)S(1)}, bf16[2,256,128]{2,1,0:T(8,128)(2,1)S(1)}, u32[]{:S(2)}, u32[]{:S(2)}) collective-permute-start(bf16[2,256,128]{2,1,0:T(8,128)(2,1)S(1)} %get-tuple-element.26), channel_id=1, source_target_pairs={{0,2},{1,3},{2,0},{3,1},{4,6},{5,7},{6,4},{7,5},{8,10},{9,11},{10,... | collective-permute-start | bytes 393224 | tf_op jit(solution)/shard_map/ppermute | solution.py:182
  8.5 1.6 %collective-permute-start.2 = (bf16[2,256,128]{2,1,0:T(8,128)(2,1)S(1)}, bf16[2,256,128]{2,1,0:T(8,128)(2,1)S(1)}, u32[]{:S(2)}, u32[]{:S(2)}) collective-permute-start(bf16[2,256,128]{2,1,0:T(8,128)(2,1)S(1)} %get-tuple-element.27), channel_id=1, source_target_pairs={{0,4},{1,5},{2,6},{3,7},{4,0},{5,1},{6,2},{7,3},{8,12},{9,13},{10,... | collective-permute-start | bytes 393224 | tf_op jit(solution)/shard_map/ppermute | solution.py:182
  10.2 3.3 %collective-permute-start.3 = (bf16[2,256,128]{2,1,0:T(8,128)(2,1)S(1)}, bf16[2,256,128]{2,1,0:T(8,128)(2,1)S(1)}, u32[]{:S(2)}, u32[]{:S(2)}) collective-permute-start(bf16[2,256,128]{2,1,0:T(8,128)(2,1)S(1)} %get-tuple-element.28), channel_id=1, source_target_pairs={{0,8},{1,9},{2,10},{3,11},{4,12},{5,13},{6,14},{7,15},{8,0},{9,1},... | collective-permute-start | bytes 393224 | tf_op jit(solution)/shard_map/ppermute | solution.py:182
  13.5 0.7 %copy-done.7 = f32[1,2,256]{2,1,0:T(2,128)S(1)} copy-done((f32[1,2,256]{2,1,0:T(2,128)S(1)}, f32[1,2,256]{2,1,0:T(2,128)}, u32[]{:S(2)}) %copy-start.7) | copy-done | bytes 2072
  14.2 0.9 %pack_qd.1 = (bf16[2,272,128]{2,1,0:T(8,128)(2,1)S(1)}, bf16[2,272,128]{2,1,0:T(8,128)(2,1)S(1)}, bf16[2,272,128]{2,1,0:T(8,128)(2,1)S(1)}, bf16[2,272,128]{2,1,0:T(8,128)(2,1)S(1)}) custom-call(s32[2,5]{1,0:T(2,128)S(1)} %copy-done.6, bf16[256,256]{1,0:T(8,128)(2,1)S(1)} %bitcast.9, bf16[256,256]{1,0:T(8,128)(2,1)S(1)} %bitcast.12, f32[2,256]{1,0:T(2,128)S(1)} %bitcast.21), custom_call_target="tpu_custom_call" | custom-call | tf_op jit(solution)/shard_map/pack_qd/pallas_call | solution.py:197
  15.0 0.1 collective-permute-start.4
  15.1 1.4 %collective-permute-start.5 = (bf16[2,272,128]{2,1,0:T(8,128)(2,1)S(1)}, bf16[2,272,128]{2,1,0:T(8,128)(2,1)S(1)}, u32[]{:S(2)}, u32[]{:S(2)}) collective-permute-start(bf16[2,272,128]{2,1,0:T(8,128)(2,1)S(1)} %get-tuple-element.33), channel_id=1, source_target_pairs={{0,2},{1,3},{2,0},{3,1},{4,6},{5,7},{6,4},{7,5},{8,10},{9,11},{10,... | collective-permute-start | bytes 417800 | tf_op jit(solution)/shard_map/ppermute | solution.py:182
  16.5 0.0 collective-permute-done.1.r2
  16.5 0.0 collective-permute-start.6
  16.5 0.0 collective-permute-done.2.r3
  16.5 0.0 copy-start.8
  16.5 2.7 %collective-permute-start.7 = (bf16[2,272,128]{2,1,0:T(8,128)(2,1)S(1)}, bf16[2,272,128]{2,1,0:T(8,128)(2,1)S(1)}, u32[]{:S(2)}, u32[]{:S(2)}) collective-permute-start(bf16[2,272,128]{2,1,0:T(8,128)(2,1)S(1)} %get-tuple-element.35), channel_id=1, source_target_pairs={{0,8},{1,9},{2,10},{3,11},{4,12},{5,13},{6,14},{7,15},{8,0},{9,1},... | collective-permute-start | bytes 417800 | tf_op jit(solution)/shard_map/ppermute | solution.py:182
  19.2 1.4 %local.1 = (f32[256,256]{1,0:T(8,128)S(1)}, f32[256,256]{1,0:T(8,128)S(1)}, f32[256,256]{1,0:T(8,128)S(1)}, f32[2,256,128]{2,1,0:T(8,128)S(1)}, bf16[256,256]{1,0:T(8,128)(2,1)S(1)}) custom-call(s32[2,5]{1,0:T(2,128)S(1)} %copy-done.6, f32[1,256]{1,0:T(1,128)S(1)} %bitcast.23, bf16[256,256]{1,0:T(8,128)(2,1)S(1)} %bitcast.10, bf16[256,256]{1,0:T(8,128)(2,1)S(1)} %bitcast.16, ...), custom_call_target="tpu_custom_call" | custom-call | tf_op jit(solution)/shard_map/local/pallas_call | solution.py:201
  20.6 2.6 %remote_q.1 = (f32[256,256]{1,0:T(8,128)S(1)}, f32[128,1,256]{2,1,0:T(1,128)}) custom-call(s32[2,5]{1,0:T(2,128)S(1)} %copy-done.6, bf16[256,256]{1,0:T(8,128)(2,1)S(1)} %get-tuple-element.22.scaled, bf16[256,256]{1,0:T(8,128)(2,1)S(1)} %bitcast.11, bf16[256,256]{1,0:T(8,128)(2,1)S(1)} %bitcast.14, f32[2,256,128]{2,1,0:T(8,128)S(1)} %get-tuple-element.23.norm_cols, ...), custom_call_target="tpu_custom_call" | custom-call | tf_op jit(solution)/shard_map/remote_q/pallas_call | solution.py:209
  23.3 10.1 %all-to-all-start = ((f32[128,1,256]{2,1,0:T(1,128)}), f32[128,1,256]{2,1,0:T(1,128)S(1)}, u32[]{:S(2)}, u32[]{:S(2)}) async-start(f32[128,1,256]{2,1,0:T(1,128)} %get-tuple-element.39), calls=%async_computation | async-start | bytes 262144 | tf_op jit(solution)/shard_map/all_to_all | solution.py:212
  33.3 0.0 collective-permute-done.4.r1
  33.4 2.8 %remote_kv.1 = (bf16[256,256]{1,0:T(8,128)(2,1)}, bf16[256,256]{1,0:T(8,128)(2,1)}, bf16[256,256]{1,0:T(8,128)(2,1)}) custom-call(s32[2,5]{1,0:T(2,128)S(1)} %copy-done.6, f32[1,256]{1,0:T(1,128)S(1)} %bitcast.24, bf16[256,256]{1,0:T(8,128)(2,1)S(1)} %bitcast.17, bf16[256,256]{1,0:T(8,128)(2,1)S(1)} %bitcast.20, f32[256,256]{1,0:T(8,128)S(1)} %get-tuple-element.29.dq, ...), custom_call_target="tpu_custom_call" | custom-call | tf_op jit(solution)/shard_map/remote_kv/pallas_call | solution.py:214
  36.2 7.4 %all-to-all-done = f32[128,1,256]{2,1,0:T(1,128)S(1)} async-done(((f32[128,1,256]{2,1,0:T(1,128)}), f32[128,1,256]{2,1,0:T(1,128)S(1)}, u32[]{:S(2)}, u32[]{:S(2)}) %all-to-all-start) | async-done | bytes 131104 | tf_op jit(solution)/shard_map/all_to_all | solution.py:212
  43.5 0.7 %reduce_sum.9 = f32[256]{0:T(256)} reduce(f32[128,1,256]{2,1,0:T(1,128)S(1)} %all-to-all-done, f32[]{:T(128)} %constant.0.clone.1), dimensions={0,1}, to_apply=%region_0.0 | reduce | flops 32512 | bytes 132100 | tf_op jit(solution)/shard_map/reduce_sum | solution.py:217
  (18 shorter events, 0.0 us)
Async XLA Ops:
  0.6 0.7 %copy-start.6 = (s32[2,5]{1,0:T(2,128)S(1)}, s32[2,5]{1,0:T(2,128)}, u32[]{:S(2)}) copy-start(s32[2,5]{1,0:T(2,128)} %offsets.9) | copy-start | bytes 124
  1.3 0.9 %copy-start.2 = (bf16[1,256,256]{2,1,0:T(8,128)(2,1)S(1)}, bf16[1,256,256]{2,1,0:T(8,128)(2,1)}, u32[]{:S(2)}) copy-start(bf16[1,256,256]{2,1,0:T(8,128)(2,1)} %param.8) | copy-start | bytes 393220
  2.2 0.9 %copy-start.4 = (bf16[1,256,256]{2,1,0:T(8,128)(2,1)S(1)}, bf16[1,256,256]{2,1,0:T(8,128)(2,1)}, u32[]{:S(2)}) copy-start(bf16[1,256,256]{2,1,0:T(8,128)(2,1)} %param.9) | copy-start | bytes 393220
  3.1 10.4 %copy-start = (bf16[1,256,256]{2,1,0:T(8,128)(2,1)S(1)}, bf16[1,256,256]{2,1,0:T(8,128)(2,1)}, u32[]{:S(2)}) copy-start(bf16[1,256,256]{2,1,0:T(8,128)(2,1)} %param.7) | copy-start | bytes 393220
  3.1 10.4 %copy-start.1 = (bf16[1,256,256]{2,1,0:T(8,128)(2,1)S(1)}, bf16[1,256,256]{2,1,0:T(8,128)(2,1)}, u32[]{:S(2)}) copy-start(bf16[1,256,256]{2,1,0:T(8,128)(2,1)} %param.10) | copy-start | bytes 393220
  4.0 11.2 %collective-permute-start = (bf16[2,256,128]{2,1,0:T(8,128)(2,1)S(1)}, bf16[2,256,128]{2,1,0:T(8,128)(2,1)S(1)}, u32[]{:S(2)}, u32[]{:S(2)}) collective-permute-start(bf16[2,256,128]{2,1,0:T(8,128)(2,1)S(1)} %get-tuple-element.25), channel_id=1, source_target_pairs={{0,1},{1,0},{2,3},{3,2},{4,5},{5,4},{6,7},{7,6},{8,9},{9,8},{10,11... | collective-permute-start | bytes 393224 | tf_op jit(solution)/shard_map/ppermute | solution.py:182
  6.1 10.4 %collective-permute-start.1 = (bf16[2,256,128]{2,1,0:T(8,128)(2,1)S(1)}, bf16[2,256,128]{2,1,0:T(8,128)(2,1)S(1)}, u32[]{:S(2)}, u32[]{:S(2)}) collective-permute-start(bf16[2,256,128]{2,1,0:T(8,128)(2,1)S(1)} %get-tuple-element.26), channel_id=1, source_target_pairs={{0,2},{1,3},{2,0},{3,1},{4,6},{5,7},{6,4},{7,5},{8,10},{9,11},{10,... | collective-permute-start | bytes 393224 | tf_op jit(solution)/shard_map/ppermute | solution.py:182
  8.5 8.0 %collective-permute-start.2 = (bf16[2,256,128]{2,1,0:T(8,128)(2,1)S(1)}, bf16[2,256,128]{2,1,0:T(8,128)(2,1)S(1)}, u32[]{:S(2)}, u32[]{:S(2)}) collective-permute-start(bf16[2,256,128]{2,1,0:T(8,128)(2,1)S(1)} %get-tuple-element.27), channel_id=1, source_target_pairs={{0,4},{1,5},{2,6},{3,7},{4,0},{5,1},{6,2},{7,3},{8,12},{9,13},{10,... | collective-permute-start | bytes 393224 | tf_op jit(solution)/shard_map/ppermute | solution.py:182
  10.2 10.5 %collective-permute-start.3 = (bf16[2,256,128]{2,1,0:T(8,128)(2,1)S(1)}, bf16[2,256,128]{2,1,0:T(8,128)(2,1)S(1)}, u32[]{:S(2)}, u32[]{:S(2)}) collective-permute-start(bf16[2,256,128]{2,1,0:T(8,128)(2,1)S(1)} %get-tuple-element.28), channel_id=1, source_target_pairs={{0,8},{1,9},{2,10},{3,11},{4,12},{5,13},{6,14},{7,15},{8,0},{9,1},... | collective-permute-start | bytes 393224 | tf_op jit(solution)/shard_map/ppermute | solution.py:182
  13.5 0.7 %copy-start.7 = (f32[1,2,256]{2,1,0:T(2,128)S(1)}, f32[1,2,256]{2,1,0:T(2,128)}, u32[]{:S(2)}) copy-start(f32[1,2,256]{2,1,0:T(2,128)} %param.11) | copy-start | bytes 6148
  14.2 5.0 %copy-start.3 = (bf16[1,256,256]{2,1,0:T(8,128)(2,1)S(1)}, bf16[1,256,256]{2,1,0:T(8,128)(2,1)}, u32[]{:S(2)}) copy-start(bf16[1,256,256]{2,1,0:T(8,128)(2,1)} %param.8) | copy-start | bytes 393220
  15.0 18.3 %collective-permute-start.4 = (bf16[2,272,128]{2,1,0:T(8,128)(2,1)S(1)}, bf16[2,272,128]{2,1,0:T(8,128)(2,1)S(1)}, u32[]{:S(2)}, u32[]{:S(2)}) collective-permute-start(bf16[2,272,128]{2,1,0:T(8,128)(2,1)S(1)} %get-tuple-element.32), channel_id=1, source_target_pairs={{0,1},{1,0},{2,3},{3,2},{4,5},{5,4},{6,7},{7,6},{8,9},{9,8},{10,11... | collective-permute-start | bytes 417800 | tf_op jit(solution)/shard_map/ppermute | solution.py:182
  15.1 18.2 %collective-permute-start.5 = (bf16[2,272,128]{2,1,0:T(8,128)(2,1)S(1)}, bf16[2,272,128]{2,1,0:T(8,128)(2,1)S(1)}, u32[]{:S(2)}, u32[]{:S(2)}) collective-permute-start(bf16[2,272,128]{2,1,0:T(8,128)(2,1)S(1)} %get-tuple-element.33), channel_id=1, source_target_pairs={{0,2},{1,3},{2,0},{3,1},{4,6},{5,7},{6,4},{7,5},{8,10},{9,11},{10,... | collective-permute-start | bytes 417800 | tf_op jit(solution)/shard_map/ppermute | solution.py:182
  16.5 16.9 %collective-permute-start.6 = (bf16[2,272,128]{2,1,0:T(8,128)(2,1)S(1)}, bf16[2,272,128]{2,1,0:T(8,128)(2,1)S(1)}, u32[]{:S(2)}, u32[]{:S(2)}) collective-permute-start(bf16[2,272,128]{2,1,0:T(8,128)(2,1)S(1)} %get-tuple-element.34), channel_id=1, source_target_pairs={{0,4},{1,5},{2,6},{3,7},{4,0},{5,1},{6,2},{7,3},{8,12},{9,13},{10,... | collective-permute-start | bytes 417800 | tf_op jit(solution)/shard_map/ppermute | solution.py:182
  16.5 2.7 %copy-start.8 = (f32[256]{0:T(256)S(1)}, f32[256]{0:T(256)}, u32[]{:S(2)}) copy-start(f32[256]{0:T(256)} %param.13) | copy-start | bytes 3076
  16.5 16.9 %collective-permute-start.7 = (bf16[2,272,128]{2,1,0:T(8,128)(2,1)S(1)}, bf16[2,272,128]{2,1,0:T(8,128)(2,1)S(1)}, u32[]{:S(2)}, u32[]{:S(2)}) collective-permute-start(bf16[2,272,128]{2,1,0:T(8,128)(2,1)S(1)} %get-tuple-element.35), channel_id=1, source_target_pairs={{0,8},{1,9},{2,10},{3,11},{4,12},{5,13},{6,14},{7,15},{8,0},{9,1},... | collective-permute-start | bytes 417800 | tf_op jit(solution)/shard_map/ppermute | solution.py:182
  23.3 10.1 %copy-start.5 = (bf16[1,256,256]{2,1,0:T(8,128)(2,1)S(1)}, bf16[1,256,256]{2,1,0:T(8,128)(2,1)}, u32[]{:S(2)}) copy-start(bf16[1,256,256]{2,1,0:T(8,128)(2,1)} %param.9) | copy-start | bytes 393220
  23.3 20.3 %all-to-all-start = ((f32[128,1,256]{2,1,0:T(1,128)}), f32[128,1,256]{2,1,0:T(1,128)S(1)}, u32[]{:S(2)}, u32[]{:S(2)}) async-start(f32[128,1,256]{2,1,0:T(1,128)} %get-tuple-element.39), calls=%async_computation | async-start | bytes 262144 | tf_op jit(solution)/shard_map/all_to_all | solution.py:212

commit v3 on v2

--- a/solution.py
+++ b/solution.py
@@ -177,6 +177,10 @@
     )
 
 
+def in_hbm(array):
+    return pltpu.with_memory_space_constraint(array, pltpu.HBM)
+
+
 def swap(payloads):
     count = lax.axis_size("ctx")
     return [lax.ppermute(p, "ctx", [(i, i ^ (1 << n)) for i in range(count)]) for n, p in enumerate(payloads)]
@@ -191,11 +195,11 @@
     bf16 = functools.partial(jax.ShapeDtypeStruct, dtype=jnp.bfloat16)
     sems = pltpu.SemaphoreType.DMA((LEVELS - 1, HEADS, 2))
     sent = call(pack_kv_kernel, "pack_kv", [bf16((HEADS, 2 * BLOCK, HD))] * (LEVELS - 1), [SMEM, HBM, HBM], [sems])(
-        offsets, k, v
+        offsets, in_hbm(k), in_hbm(v)
     )
     got_kv = swap(sent)
     sent = call(pack_qd_kernel, "pack_qd", [bf16((HEADS, ROWS, HD))] * (LEVELS - 1), [SMEM, HBM, HBM, VMEM], [sems])(
-        offsets, q, d, norm
+        offsets, in_hbm(q), in_hbm(d), norm
     )
     got_qd = swap(sent)
     dq, dk, dv, norm_cols, scaled = call(

time: 44.5 us -> 44.5 us (level)
  local copies, waits for them, and re-layouts: 3.18 us -> 1.37 us
  Pallas kernels: 8.53 us -> 10.2 us
    unnamed x18 -> x14, local copies, waits for them, and re-layouts: 3.18 us -> 1.37 us
    pallas_call x1, Pallas kernels: 0.83 us -> 1.69 us  [body(): call(pack_kv_kernel, 'pack_kv', [bf16((HEADS, 2 * BLOCK, HD))] * (LEVELS...]
    all_to_all x1, starting transfers between devices: 10.1 us -> 10.9 us  [body(): parts = lax.all_to_all(partial, axes, 0, 0, tiled=True)]
    ppermute x8, starting transfers between devices: 13.6 us -> 12.8 us  [swap(): lax.ppermute(p, 'ctx', [(i, i ^ 1 << n) for i in range(count)])]
    pallas_call x1, Pallas kernels: 0.86 us -> 1.69 us  [body(): call(pack_qd_kernel, 'pack_qd', [bf16((HEADS, ROWS, HD))] * (LEVELS - 1),...]
  transfers between devices with their start and end apart: 9 -> 9, of which waited for: 1 -> 1; matrix products, arithmetic and copies ran while one was open for 0% -> 0% of each run, Pallas kernels for 17% -> 19%
where the time goes in v3:
time: 44.5 us; the launch traced here: 44.2 us
  starting transfers between devices  23.7 us (53%)
  Pallas kernels  10.2 us (23%)
  waiting for transfers between devices  7.4 us (17%)
  local copies, waits for them, and re-layouts  1.37 us (3%)
  between operations  0.76 us (2%)
  other arithmetic  0.71 us (2%)
    ppermute x8, starting transfers between devices, swap(): lax.ppermute(p, 'ctx', [(i, i ^ 1 << n) for i in range(count)])  12.8 us
    all_to_all x1, starting transfers between devices, body(): parts = lax.all_to_all(partial, axes, 0, 0, tiled=True)  10.9 us
    all_to_all x1, waiting for transfers between devices, body(): parts = lax.all_to_all(partial, axes, 0, 0, tiled=True)  7.38 us
    pallas_call x1, Pallas kernels, body(): call(key_kernel, 'remote_kv', [bf16((tokens, width))] * 3, [SMEM] + [VMEM...  2.79 us
    pallas_call x1, Pallas kernels, body(): call(query_kernel, 'remote_q', [f32((tokens, width)), f32((everyone, 1, w...  2.65 us
    pallas_call x1, Pallas kernels, body(): call(pack_qd_kernel, 'pack_qd', [bf16((HEADS, ROWS, HD))] * (LEVELS - 1),...  1.69 us
    pallas_call x1, Pallas kernels, body(): call(pack_kv_kernel, 'pack_kv', [bf16((HEADS, 2 * BLOCK, HD))] * (LEVELS...  1.69 us
    pallas_call x1, Pallas kernels, body(): call(local_kernel, 'local', [f32((tokens, width))] * 3 + [f32((HEADS, tok...  1.43 us
  transfers between devices with their start and end apart: 9, of which 1 were waited for; matrix products, arithmetic and copies ran while one was open for 0% of the time, Pallas kernels for 19%

profile of v3, /device:TPU:1, one launch (start us, length us, event | category | flops | bytes accessed | tf_op | source)
XLA Modules:
  0.0 44.2 jit_solution(978890364910762774)
XLA Ops:
  0.6 0.7 %copy-done.4 = s32[2,5]{1,0:T(2,128)S(1)} copy-done((s32[2,5]{1,0:T(2,128)S(1)}, s32[2,5]{1,0:T(2,128)}, u32[]{:S(2)}) %copy-start.4) | copy-done | bytes 64
  1.3 1.7 %pack_kv.1 = (bf16[2,256,128]{2,1,0:T(8,128)(2,1)S(1)}, bf16[2,256,128]{2,1,0:T(8,128)(2,1)S(1)}, bf16[2,256,128]{2,1,0:T(8,128)(2,1)S(1)}, bf16[2,256,128]{2,1,0:T(8,128)(2,1)S(1)}) custom-call(s32[2,5]{1,0:T(2,128)S(1)} %copy-done.4, bf16[256,256]{1,0:T(8,128)(2,1)} %bitcast.15, bf16[256,256]{1,0:T(8,128)(2,1)} %bitcast.18), custom_call_target="tpu_custom_call" | custom-call | tf_op jit(solution)/shard_map/pack_kv/pallas_call | solution.py:197
  3.0 2.1 %collective-permute-start = (bf16[2,256,128]{2,1,0:T(8,128)(2,1)S(1)}, bf16[2,256,128]{2,1,0:T(8,128)(2,1)S(1)}, u32[]{:S(2)}, u32[]{:S(2)}) collective-permute-start(bf16[2,256,128]{2,1,0:T(8,128)(2,1)S(1)} %get-tuple-element.25), channel_id=1, source_target_pairs={{0,1},{1,0},{2,3},{3,2},{4,5},{5,4},{6,7},{7,6},{8,9},{9,8},{10,11... | collective-permute-start | bytes 393224 | tf_op jit(solution)/shard_map/ppermute | solution.py:186
  5.1 2.5 %collective-permute-start.1 = (bf16[2,256,128]{2,1,0:T(8,128)(2,1)S(1)}, bf16[2,256,128]{2,1,0:T(8,128)(2,1)S(1)}, u32[]{:S(2)}, u32[]{:S(2)}) collective-permute-start(bf16[2,256,128]{2,1,0:T(8,128)(2,1)S(1)} %get-tuple-element.26), channel_id=1, source_target_pairs={{0,2},{1,3},{2,0},{3,1},{4,6},{5,7},{6,4},{7,5},{8,10},{9,11},{10,... | collective-permute-start | bytes 393224 | tf_op jit(solution)/shard_map/ppermute | solution.py:186
  7.6 1.6 %collective-permute-start.2 = (bf16[2,256,128]{2,1,0:T(8,128)(2,1)S(1)}, bf16[2,256,128]{2,1,0:T(8,128)(2,1)S(1)}, u32[]{:S(2)}, u32[]{:S(2)}) collective-permute-start(bf16[2,256,128]{2,1,0:T(8,128)(2,1)S(1)} %get-tuple-element.27), channel_id=1, source_target_pairs={{0,4},{1,5},{2,6},{3,7},{4,0},{5,1},{6,2},{7,3},{8,12},{9,13},{10,... | collective-permute-start | bytes 393224 | tf_op jit(solution)/shard_map/ppermute | solution.py:186
  9.2 3.3 %collective-permute-start.3 = (bf16[2,256,128]{2,1,0:T(8,128)(2,1)S(1)}, bf16[2,256,128]{2,1,0:T(8,128)(2,1)S(1)}, u32[]{:S(2)}, u32[]{:S(2)}) collective-permute-start(bf16[2,256,128]{2,1,0:T(8,128)(2,1)S(1)} %get-tuple-element.28), channel_id=1, source_target_pairs={{0,8},{1,9},{2,10},{3,11},{4,12},{5,13},{6,14},{7,15},{8,0},{9,1},... | collective-permute-start | bytes 393224 | tf_op jit(solution)/shard_map/ppermute | solution.py:186
  12.5 0.7 %copy-done.5 = f32[1,2,256]{2,1,0:T(2,128)S(1)} copy-done((f32[1,2,256]{2,1,0:T(2,128)S(1)}, f32[1,2,256]{2,1,0:T(2,128)}, u32[]{:S(2)}) %copy-start.5) | copy-done | bytes 2072
  13.2 1.7 %pack_qd.1 = (bf16[2,272,128]{2,1,0:T(8,128)(2,1)S(1)}, bf16[2,272,128]{2,1,0:T(8,128)(2,1)S(1)}, bf16[2,272,128]{2,1,0:T(8,128)(2,1)S(1)}, bf16[2,272,128]{2,1,0:T(8,128)(2,1)S(1)}) custom-call(s32[2,5]{1,0:T(2,128)S(1)} %copy-done.4, bf16[256,256]{1,0:T(8,128)(2,1)} %bitcast.9, bf16[256,256]{1,0:T(8,128)(2,1)} %bitcast.12, f32[2,256]{1,0:T(2,128)S(1)} %bitcast.21), custom_call_target="tpu_custom_call" | custom-call | tf_op jit(solution)/shard_map/pack_qd/pallas_call | solution.py:201
  14.9 0.1 collective-permute-start.4
  15.0 0.0 collective-permute-done.r1
  15.0 1.4 %collective-permute-start.5 = (bf16[2,272,128]{2,1,0:T(8,128)(2,1)S(1)}, bf16[2,272,128]{2,1,0:T(8,128)(2,1)S(1)}, u32[]{:S(2)}, u32[]{:S(2)}) collective-permute-start(bf16[2,272,128]{2,1,0:T(8,128)(2,1)S(1)} %get-tuple-element.33), channel_id=1, source_target_pairs={{0,2},{1,3},{2,0},{3,1},{4,6},{5,7},{6,4},{7,5},{8,10},{9,11},{10,... | collective-permute-start | bytes 417800 | tf_op jit(solution)/shard_map/ppermute | solution.py:186
  16.4 0.0 collective-permute-done.1.r2
  16.4 0.0 collective-permute-start.6
  16.4 0.0 collective-permute-done.2.r3
  16.4 0.0 copy-start.6
  16.4 1.8 %collective-permute-start.7 = (bf16[2,272,128]{2,1,0:T(8,128)(2,1)S(1)}, bf16[2,272,128]{2,1,0:T(8,128)(2,1)S(1)}, u32[]{:S(2)}, u32[]{:S(2)}) collective-permute-start(bf16[2,272,128]{2,1,0:T(8,128)(2,1)S(1)} %get-tuple-element.35), channel_id=1, source_target_pairs={{0,8},{1,9},{2,10},{3,11},{4,12},{5,13},{6,14},{7,15},{8,0},{9,1},... | collective-permute-start | bytes 417800 | tf_op jit(solution)/shard_map/ppermute | solution.py:186
  18.3 1.4 %local.1 = (f32[256,256]{1,0:T(8,128)S(1)}, f32[256,256]{1,0:T(8,128)S(1)}, f32[256,256]{1,0:T(8,128)S(1)}, f32[2,256,128]{2,1,0:T(8,128)S(1)}, bf16[256,256]{1,0:T(8,128)(2,1)S(1)}) custom-call(s32[2,5]{1,0:T(2,128)S(1)} %copy-done.4, f32[1,256]{1,0:T(1,128)S(1)} %bitcast.23, bf16[256,256]{1,0:T(8,128)(2,1)S(1)} %bitcast.10, bf16[256,256]{1,0:T(8,128)(2,1)S(1)} %bitcast.16, ...), custom_call_target="tpu_custom_call" | custom-call | tf_op jit(solution)/shard_map/local/pallas_call | solution.py:205
  19.7 2.6 %remote_q.1 = (f32[256,256]{1,0:T(8,128)S(1)}, f32[128,1,256]{2,1,0:T(1,128)}) custom-call(s32[2,5]{1,0:T(2,128)S(1)} %copy-done.4, bf16[256,256]{1,0:T(8,128)(2,1)S(1)} %get-tuple-element.22.scaled, bf16[256,256]{1,0:T(8,128)(2,1)S(1)} %bitcast.11, bf16[256,256]{1,0:T(8,128)(2,1)S(1)} %bitcast.14, f32[2,256,128]{2,1,0:T(8,128)S(1)} %get-tuple-element.23.norm_cols, ...), custom_call_target="tpu_custom_call" | custom-call | tf_op jit(solution)/shard_map/remote_q/pallas_call | solution.py:213
  22.4 10.9 %all-to-all-start = ((f32[128,1,256]{2,1,0:T(1,128)}), f32[128,1,256]{2,1,0:T(1,128)S(1)}, u32[]{:S(2)}, u32[]{:S(2)}) async-start(f32[128,1,256]{2,1,0:T(1,128)} %get-tuple-element.39), calls=%async_computation | async-start | bytes 262144 | tf_op jit(solution)/shard_map/all_to_all | solution.py:216
  33.3 0.0 collective-permute-done.4.r1
  33.3 0.0 collective-permute-done.5.r2
  33.3 2.8 %remote_kv.1 = (bf16[256,256]{1,0:T(8,128)(2,1)}, bf16[256,256]{1,0:T(8,128)(2,1)}, bf16[256,256]{1,0:T(8,128)(2,1)}) custom-call(s32[2,5]{1,0:T(2,128)S(1)} %copy-done.4, f32[1,256]{1,0:T(1,128)S(1)} %bitcast.24, bf16[256,256]{1,0:T(8,128)(2,1)S(1)} %bitcast.17, bf16[256,256]{1,0:T(8,128)(2,1)S(1)} %bitcast.20, f32[256,256]{1,0:T(8,128)S(1)} %get-tuple-element.29.dq, ...), custom_call_target="tpu_custom_call" | custom-call | tf_op jit(solution)/shard_map/remote_kv/pallas_call | solution.py:218
  36.1 7.4 %all-to-all-done = f32[128,1,256]{2,1,0:T(1,128)S(1)} async-done(((f32[128,1,256]{2,1,0:T(1,128)}), f32[128,1,256]{2,1,0:T(1,128)S(1)}, u32[]{:S(2)}, u32[]{:S(2)}) %all-to-all-start) | async-done | bytes 131104 | tf_op jit(solution)/shard_map/all_to_all | solution.py:216
  43.5 0.7 %reduce_sum.9 = f32[256]{0:T(256)} reduce(f32[128,1,256]{2,1,0:T(1,128)S(1)} %all-to-all-done, f32[]{:T(128)} %constant.0.clone.1), dimensions={0,1}, to_apply=%region_0.0 | reduce | flops 32512 | bytes 132100 | tf_op jit(solution)/shard_map/reduce_sum | solution.py:221
  (14 shorter events, 0.0 us)
Async XLA Ops:
  0.6 0.7 %copy-start.4 = (s32[2,5]{1,0:T(2,128)S(1)}, s32[2,5]{1,0:T(2,128)}, u32[]{:S(2)}) copy-start(s32[2,5]{1,0:T(2,128)} %offsets.9) | copy-start | bytes 124
  1.3 16.9 %copy-start.2 = (bf16[1,256,256]{2,1,0:T(8,128)(2,1)S(1)}, bf16[1,256,256]{2,1,0:T(8,128)(2,1)}, u32[]{:S(2)}) copy-start(bf16[1,256,256]{2,1,0:T(8,128)(2,1)} %param.8) | copy-start | bytes 393220
  1.3 16.9 %copy-start.3 = (bf16[1,256,256]{2,1,0:T(8,128)(2,1)S(1)}, bf16[1,256,256]{2,1,0:T(8,128)(2,1)}, u32[]{:S(2)}) copy-start(bf16[1,256,256]{2,1,0:T(8,128)(2,1)} %param.9) | copy-start | bytes 393220
  3.0 12.0 %collective-permute-start = (bf16[2,256,128]{2,1,0:T(8,128)(2,1)S(1)}, bf16[2,256,128]{2,1,0:T(8,128)(2,1)S(1)}, u32[]{:S(2)}, u32[]{:S(2)}) collective-permute-start(bf16[2,256,128]{2,1,0:T(8,128)(2,1)S(1)} %get-tuple-element.25), channel_id=1, source_target_pairs={{0,1},{1,0},{2,3},{3,2},{4,5},{5,4},{6,7},{7,6},{8,9},{9,8},{10,11... | collective-permute-start | bytes 393224 | tf_op jit(solution)/shard_map/ppermute | solution.py:186
  5.1 11.2 %collective-permute-start.1 = (bf16[2,256,128]{2,1,0:T(8,128)(2,1)S(1)}, bf16[2,256,128]{2,1,0:T(8,128)(2,1)S(1)}, u32[]{:S(2)}, u32[]{:S(2)}) collective-permute-start(bf16[2,256,128]{2,1,0:T(8,128)(2,1)S(1)} %get-tuple-element.26), channel_id=1, source_target_pairs={{0,2},{1,3},{2,0},{3,1},{4,6},{5,7},{6,4},{7,5},{8,10},{9,11},{10,... | collective-permute-start | bytes 393224 | tf_op jit(solution)/shard_map/ppermute | solution.py:186
  7.6 8.8 %collective-permute-start.2 = (bf16[2,256,128]{2,1,0:T(8,128)(2,1)S(1)}, bf16[2,256,128]{2,1,0:T(8,128)(2,1)S(1)}, u32[]{:S(2)}, u32[]{:S(2)}) collective-permute-start(bf16[2,256,128]{2,1,0:T(8,128)(2,1)S(1)} %get-tuple-element.27), channel_id=1, source_target_pairs={{0,4},{1,5},{2,6},{3,7},{4,0},{5,1},{6,2},{7,3},{8,12},{9,13},{10,... | collective-permute-start | bytes 393224 | tf_op jit(solution)/shard_map/ppermute | solution.py:186
  9.2 10.5 %collective-permute-start.3 = (bf16[2,256,128]{2,1,0:T(8,128)(2,1)S(1)}, bf16[2,256,128]{2,1,0:T(8,128)(2,1)S(1)}, u32[]{:S(2)}, u32[]{:S(2)}) collective-permute-start(bf16[2,256,128]{2,1,0:T(8,128)(2,1)S(1)} %get-tuple-element.28), channel_id=1, source_target_pairs={{0,8},{1,9},{2,10},{3,11},{4,12},{5,13},{6,14},{7,15},{8,0},{9,1},... | collective-permute-start | bytes 393224 | tf_op jit(solution)/shard_map/ppermute | solution.py:186
  12.5 0.7 %copy-start.5 = (f32[1,2,256]{2,1,0:T(2,128)S(1)}, f32[1,2,256]{2,1,0:T(2,128)}, u32[]{:S(2)}) copy-start(f32[1,2,256]{2,1,0:T(2,128)} %param.11) | copy-start | bytes 6148
  13.2 5.0 %copy-start = (bf16[1,256,256]{2,1,0:T(8,128)(2,1)S(1)}, bf16[1,256,256]{2,1,0:T(8,128)(2,1)}, u32[]{:S(2)}) copy-start(bf16[1,256,256]{2,1,0:T(8,128)(2,1)} %param.7) | copy-start | bytes 393220
  13.2 5.0 %copy-start.1 = (bf16[1,256,256]{2,1,0:T(8,128)(2,1)S(1)}, bf16[1,256,256]{2,1,0:T(8,128)(2,1)}, u32[]{:S(2)}) copy-start(bf16[1,256,256]{2,1,0:T(8,128)(2,1)} %param.10) | copy-start | bytes 393220
  14.9 18.3 %collective-permute-start.4 = (bf16[2,272,128]{2,1,0:T(8,128)(2,1)S(1)}, bf16[2,272,128]{2,1,0:T(8,128)(2,1)S(1)}, u32[]{:S(2)}, u32[]{:S(2)}) collective-permute-start(bf16[2,272,128]{2,1,0:T(8,128)(2,1)S(1)} %get-tuple-element.32), channel_id=1, source_target_pairs={{0,1},{1,0},{2,3},{3,2},{4,5},{5,4},{6,7},{7,6},{8,9},{9,8},{10,11... | collective-permute-start | bytes 417800 | tf_op jit(solution)/shard_map/ppermute | solution.py:186
  15.0 18.2 %collective-permute-start.5 = (bf16[2,272,128]{2,1,0:T(8,128)(2,1)S(1)}, bf16[2,272,128]{2,1,0:T(8,128)(2,1)S(1)}, u32[]{:S(2)}, u32[]{:S(2)}) collective-permute-start(bf16[2,272,128]{2,1,0:T(8,128)(2,1)S(1)} %get-tuple-element.33), channel_id=1, source_target_pairs={{0,2},{1,3},{2,0},{3,1},{4,6},{5,7},{6,4},{7,5},{8,10},{9,11},{10,... | collective-permute-start | bytes 417800 | tf_op jit(solution)/shard_map/ppermute | solution.py:186
  16.4 16.9 %collective-permute-start.6 = (bf16[2,272,128]{2,1,0:T(8,128)(2,1)S(1)}, bf16[2,272,128]{2,1,0:T(8,128)(2,1)S(1)}, u32[]{:S(2)}, u32[]{:S(2)}) collective-permute-start(bf16[2,272,128]{2,1,0:T(8,128)(2,1)S(1)} %get-tuple-element.34), channel_id=1, source_target_pairs={{0,4},{1,5},{2,6},{3,7},{4,0},{5,1},{6,2},{7,3},{8,12},{9,13},{10,... | collective-permute-start | bytes 417800 | tf_op jit(solution)/shard_map/ppermute | solution.py:186
  16.4 1.9 %copy-start.6 = (f32[256]{0:T(256)S(1)}, f32[256]{0:T(256)}, u32[]{:S(2)}) copy-start(f32[256]{0:T(256)} %param.13) | copy-start | bytes 3076
  16.4 16.9 %collective-permute-start.7 = (bf16[2,272,128]{2,1,0:T(8,128)(2,1)S(1)}, bf16[2,272,128]{2,1,0:T(8,128)(2,1)S(1)}, u32[]{:S(2)}, u32[]{:S(2)}) collective-permute-start(bf16[2,272,128]{2,1,0:T(8,128)(2,1)S(1)} %get-tuple-element.35), channel_id=1, source_target_pairs={{0,8},{1,9},{2,10},{3,11},{4,12},{5,13},{6,14},{7,15},{8,0},{9,1},... | collective-permute-start | bytes 417800 | tf_op jit(solution)/shard_map/ppermute | solution.py:186
  22.4 21.1 %all-to-all-start = ((f32[128,1,256]{2,1,0:T(1,128)}), f32[128,1,256]{2,1,0:T(1,128)S(1)}, u32[]{:S(2)}, u32[]{:S(2)}) async-start(f32[128,1,256]{2,1,0:T(1,128)} %get-tuple-element.39), calls=%async_computation | async-start | bytes 262144 | tf_op jit(solution)/shard_map/all_to_all | solution.py:216

commit v4 on v3

--- a/solution.py
+++ b/solution.py
@@ -15,6 +15,7 @@
 ROW_Q, ROW_D, ROW_N, ROWS = 0, 128, 256, 272
 
 HBM = pl.BlockSpec(memory_space=pltpu.HBM)
+ANY = pl.BlockSpec(memory_space=pl.ANY)
 VMEM = pl.BlockSpec(memory_space=pltpu.VMEM)
 SMEM = pl.BlockSpec(memory_space=pltpu.SMEM)
 NT = (((1,), (1,)), ((), ()))
@@ -44,67 +45,78 @@
     return (rows.astype(jnp.float32) * gain).astype(jnp.bfloat16)
 
 
-def copy_blocks(offsets, sources, outs, sems):
+def pack_kernel(offsets_in, k_in, v_in, q_in, d_in, norm_in, *refs):
+    outs, (offsets, k, v, q, d, norm, sems) = refs[:8], refs[8:]
     copies = []
+    for i, (source, target) in enumerate(
+        ((offsets_in, offsets), (k_in, k), (v_in, v), (q_in, q), (d_in, d), (norm_in, norm))
+    ):
+        copies.append(pltpu.make_async_copy(source, target, sems.at[i]))
+        copies[-1].start()
+    for copy in copies[:3]:
+        copy.wait()
+    spots = [(level, head, offsets[head, level] & 1) for level in range(1, LEVELS) for head in range(HEADS)]
+    for level, head, block in spots:
+        at, out = block_rows(block), outs[level - 1]
+        out[head, :BLOCK] = k[at, cols(head)]
+        out[head, BLOCK:] = v[at, cols(head)]
+    for copy in copies[3:]:
+        copy.wait()
+    row = lax.broadcasted_iota(jnp.int32, (16, BLOCK), 0)
+    for level, head, block in spots:
+        at, out = block_rows(block), outs[LEVELS - 1 + level - 1]
+        out[head, ROW_Q : ROW_Q + BLOCK] = q[at, cols(head)]
+        out[head, ROW_D : ROW_D + BLOCK] = d[at, cols(head)]
+        whole = jnp.where(block == 0, norm[head : head + 1, :BLOCK], norm[head : head + 1, BLOCK:])
+        high = whole.astype(jnp.bfloat16).astype(jnp.float32)
+        rest = whole - high
+        mid = rest.astype(jnp.bfloat16).astype(jnp.float32)
+        low = rest - mid
+        parts = jnp.where(row == 0, high, jnp.where(row == 1, mid, jnp.where(row == 2, low, 0.0)))
+        out[head, ROW_N:ROWS] = parts.astype(jnp.bfloat16)
+
+
+def block_counts(offsets, head):
+    me = lax.axis_index("ctx")
+    count = [jnp.float32(1.0), jnp.float32(1.0)]
     for level in range(1, LEVELS):
-        for head in range(HEADS):
-            at = block_rows(offsets[head, level] & 1)
-            for i, source in enumerate(sources):
-                copies.append(
-                    pltpu.make_async_copy(
-                        source.at[at, cols(head)],
-                        outs[level - 1].at[head, i * BLOCK : (i + 1) * BLOCK],
-                        sems.at[level - 1, head, i],
-                    )
-                )
-    for copy in copies:
-        copy.start()
-    return copies
-
-
-def pack_kv_kernel(offsets, k, v, *refs):
-    for copy in copy_blocks(offsets, (k, v), refs[:-1], refs[-1]):
-        copy.wait()
-
-
-def pack_qd_kernel(offsets, q, d, norm, *refs):
-    outs, sems = refs[:-1], refs[-1]
-    copies = copy_blocks(offsets, (q, d), outs, sems)
-    row = lax.broadcasted_iota(jnp.int32, (16, BLOCK), 0)
-    for head in range(HEADS):
-        for level in range(1, LEVELS):
-            block = offsets[head, level] & 1
-            whole = jnp.where(block == 0, norm[head : head + 1, :BLOCK], norm[head : head + 1, BLOCK:])
-            high = whole.astype(jnp.bfloat16).astype(jnp.float32)
-            rest = whole - high
-            mid = rest.astype(jnp.bfloat16).astype(jnp.float32)
-            low = rest - mid
-            parts = jnp.where(row == 0, high, jnp.where(row == 1, mid, jnp.where(row == 2, low, 0.0)))
-            outs[level - 1][head, ROW_N:ROWS] = parts.astype(jnp.bfloat16)
-    for copy in copies:
-        copy.wait()
-
-
-def local_kernel(offsets, gain, q, k, v, d, norm, dq, dk, dv, norm_cols, scaled):
-    me = lax.axis_index("ctx")
+        active, block = place(offsets, me, head, level)
+        for b in range(2):
+            count[b] = count[b] + jnp.where(active & (block == b), 1.0, 0.0)
+    return count
+
+
+def both_blocks(b):
+    return slice(b * BLOCK, (b + 1) * BLOCK), slice((1 - b) * BLOCK, (2 - b) * BLOCK)
+
+
+def local_q_kernel(offsets, gain, q, k, v, d, norm, dq, norm_cols, scaled):
     for head in range(HEADS):
         c = cols(head)
-        count = [jnp.float32(1.0), jnp.float32(1.0)]
-        for level in range(1, LEVELS):
-            active, block = place(offsets, me, head, level)
-            for b in range(2):
-                count[b] = count[b] + jnp.where(active & (block == b), 1.0, 0.0)
+        count = block_counts(offsets, head)
         query, key, value, dout = scale_rows(q[:, c], gain[:, c]), k[:, c], v[:, c], d[:, c]
         scaled[:, c] = query
+        column = jnp.transpose(jnp.broadcast_to(norm[head : head + 1, :], (BLOCK, 2 * BLOCK)))
+        norm_cols[head] = column
+        probs = jnp.exp(dot(query, key, NT) * SCALE - jnp.concatenate([column, column], axis=1))
+        grads = (probs * dot(dout, value, NT)).astype(jnp.bfloat16)
+        for b in range(2):
+            own, other = both_blocks(b)
+            dq[own, c] = count[b] * dot(grads[own, own], key[own], NN) + dot(grads[own, other], key[other], NN)
+
+
+def local_kv_kernel(offsets, scaled, k, v, d, norm, dk, dv):
+    for head in range(HEADS):
+        c = cols(head)
+        count = block_counts(offsets, head)
+        query, key, value, dout = scaled[:, c], k[:, c], v[:, c], d[:, c]
         probs = jnp.exp(dot(key, query, NT) * SCALE - norm[head : head + 1, :])
         grads = (probs * dot(value, dout, NT)).astype(jnp.bfloat16)
         probs = probs.astype(jnp.bfloat16)
         for b in range(2):
-            own, other = slice(b * BLOCK, (b + 1) * BLOCK), slice((1 - b) * BLOCK, (2 - b) * BLOCK)
-            dq[own, c] = count[b] * dot(grads[own, own], key[own], TN) + dot(grads[other, own], key[other], TN)
+            own, other = both_blocks(b)
             dk[own, c] = count[b] * dot(grads[own, own], query[own], NN) + dot(grads[own, other], query[other], NN)
             dv[own, c] = count[b] * dot(probs[own, own], dout[own], NN) + dot(probs[own, other], dout[other], NN)
-        norm_cols[head] = jnp.transpose(jnp.broadcast_to(norm[head : head + 1, :], (BLOCK, 2 * BLOCK)))
 
 
 def for_each_level(offsets, fn):
@@ -165,14 +177,15 @@
     grad_v[...] = dv[...].astype(jnp.bfloat16)
 
 
-def call(kernel, name, outs, in_specs, scratch=()):
+def call(kernel, name, outs, in_specs, scratch=(), out_specs=None, aliases=None):
     return pl.pallas_call(
         kernel,
         name=name,
         out_shape=outs,
         in_specs=in_specs,
-        out_specs=[VMEM] * len(outs),
+        out_specs=out_specs or [VMEM] * len(outs),
         scratch_shapes=list(scratch),
+        input_output_aliases=aliases or {},
         compiler_params=pltpu.CompilerParams(vmem_limit_bytes=32 * 1024 * 1024),
     )
 
@@ -193,19 +206,28 @@
     gain = q_gain.reshape(1, width)
     f32 = functools.partial(jax.ShapeDtypeStruct, dtype=jnp.float32)
     bf16 = functools.partial(jax.ShapeDtypeStruct, dtype=jnp.bfloat16)
-    sems = pltpu.SemaphoreType.DMA((LEVELS - 1, HEADS, 2))
-    sent = call(pack_kv_kernel, "pack_kv", [bf16((HEADS, 2 * BLOCK, HD))] * (LEVELS - 1), [SMEM, HBM, HBM], [sems])(
-        offsets, in_hbm(k), in_hbm(v)
-    )
-    got_kv = swap(sent)
-    sent = call(pack_qd_kernel, "pack_qd", [bf16((HEADS, ROWS, HD))] * (LEVELS - 1), [SMEM, HBM, HBM, VMEM], [sems])(
-        offsets, in_hbm(q), in_hbm(d), norm
-    )
-    got_qd = swap(sent)
-    dq, dk, dv, norm_cols, scaled = call(
-        local_kernel,
-        "local",
-        [f32((tokens, width))] * 3 + [f32((HEADS, tokens, HD)), bf16((tokens, width))],
+    many = LEVELS - 1
+    raw = pltpu.VMEM((tokens, width), jnp.bfloat16)
+    sent = call(
+        pack_kernel,
+        "pack",
+        [bf16((HEADS, 2 * BLOCK, HD))] * many + [bf16((HEADS, ROWS, HD))] * many,
+        [HBM] * 6,
+        [
+            pltpu.SMEM(offsets.shape, jnp.int32),
+            raw,
+            raw,
+            raw,
+            raw,
+            pltpu.VMEM(norm.shape, jnp.float32),
+            pltpu.SemaphoreType.DMA((6,)),
+        ],
+    )(*map(in_hbm, (offsets, k, v, q, d, norm)))
+    got_kv, got_qd = swap(sent[:many]), swap(sent[many:])
+    dq, norm_cols, scaled = call(
+        local_q_kernel,
+        "local_q",
+        [f32((tokens, width)), f32((HEADS, tokens, HD)), bf16((tokens, width))],
         [SMEM] + [VMEM] * 6,
     )(offsets, gain, q, k, v, d, norm)
     axes = ("dp", "ctx")
@@ -214,6 +236,9 @@
         query_kernel, "remote_q", [f32((tokens, width)), f32((everyone, 1, width))], [SMEM] + [VMEM] * 9
     )(offsets, scaled, q, d, norm_cols, dq, *got_kv)
     parts = lax.all_to_all(partial, axes, 0, 0, tiled=True)
+    dk, dv = call(local_kv_kernel, "local_kv", [f32((tokens, width))] * 2, [SMEM] + [VMEM] * 5)(
+        offsets, scaled, k, v, d, norm
+    )
     acc = pltpu.VMEM((tokens, width), jnp.float32)
     grad_q, grad_k, grad_v = call(
         key_kernel, "remote_kv", [bf16((tokens, width))] * 3, [SMEM] + [VMEM] * 10, [acc, acc]

time: 44.5 us -> 40.6 us (0.912); the launches traced: 44.2 us -> 40.9 us
  Pallas kernels: 10.2 us -> 8.16 us
  local copies, waits for them, and re-layouts: 1.37 us -> 0.03 us
  starting transfers between devices: 23.7 us -> 24.5 us
  waiting for transfers between devices: 7.4 us -> 6.67 us
    ppermute x8, starting transfers between devices: 12.8 us -> 15.2 us  [swap(): lax.ppermute(p, 'ctx', [(i, i ^ 1 << n) for i in range(count)])]
    all_to_all x1, starting transfers between devices: 10.9 us -> 9.32 us  [body(): parts = lax.all_to_all(partial, axes, 0, 0, tiled=True)]
    unnamed x14, local copies, waits for them, and re-layouts: 1.37 us -> 0.03 us
    pallas_call x3, Pallas kernels: 4.81 us -> 3.65 us  [the longest x1 1.33 us: body(): call(pack_kernel, 'pack', [bf16((HEADS, 2 * BLOCK, HD))] * many + [bf16((...]
    all_to_all x1, waiting for transfers between devices: 7.38 us -> 6.65 us  [body(): parts = lax.all_to_all(partial, axes, 0, 0, tiled=True)]
    pallas_call x1, Pallas kernels: 2.79 us -> 2.3 us  [body(): call(key_kernel, 'remote_kv', [bf16((tokens, width))] * 3, [SMEM] + [VMEM...]
  transfers between devices with their start and end apart: 9 -> 9, of which waited for: 1 -> 1; matrix products, arithmetic and copies ran while one was open for 0% -> 0% of each run, Pallas kernels for 19% -> 17%
where the time goes in v4:
time: 40.6 us; the launch traced here: 40.9 us
  starting transfers between devices  24.5 us (60%)
  Pallas kernels  8.16 us (20%)
  waiting for transfers between devices  6.67 us (16%)
  between operations  0.77 us (2%)
  other arithmetic  0.71 us (2%)
    ppermute x8, starting transfers between devices, swap(): lax.ppermute(p, 'ctx', [(i, i ^ 1 << n) for i in range(count)])  15.2 us
    all_to_all x1, starting transfers between devices, body(): parts = lax.all_to_all(partial, axes, 0, 0, tiled=True)  9.32 us
    all_to_all x1, waiting for transfers between devices, body(): parts = lax.all_to_all(partial, axes, 0, 0, tiled=True)  6.65 us
    pallas_call x1, Pallas kernels, body(): call(key_kernel, 'remote_kv', [bf16((tokens, width))] * 3, [SMEM] + [VMEM...  2.3 us
    pallas_call x1, Pallas kernels, body(): call(query_kernel, 'remote_q', [f32((tokens, width)), f32((everyone, 1, w...  2.21 us
    pallas_call x1, Pallas kernels, body(): call(pack_kernel, 'pack', [bf16((HEADS, 2 * BLOCK, HD))] * many + [bf16((...  1.33 us
    pallas_call x1, Pallas kernels, body(): call(local_kv_kernel, 'local_kv', [f32((tokens, width))] * 2, [SMEM] + [V...  1.2 us
    pallas_call x1, Pallas kernels, body(): call(local_q_kernel, 'local_q', [f32((tokens, width)), f32((HEADS, tokens...  1.12 us
  transfers between devices with their start and end apart: 9, of which 1 were waited for; matrix products, arithmetic and copies ran while one was open for 0% of the time, Pallas kernels for 17%

profile of v4, /device:TPU:1, one launch (start us, length us, event | category | flops | bytes accessed | tf_op | source)
XLA Modules:
  0.0 40.9 jit_solution(70034090781879770)
XLA Ops:
  0.7 1.3 %pack.1 = (bf16[2,256,128]{2,1,0:T(8,128)(2,1)S(1)}, bf16[2,256,128]{2,1,0:T(8,128)(2,1)S(1)}, bf16[2,256,128]{2,1,0:T(8,128)(2,1)S(1)}, bf16[2,256,128]{2,1,0:T...) custom-call(s32[2,5]{1,0:T(2,128)} %offsets.7, ...), custom_call_target="tpu_custom_call" | custom-call | tf_op jit(solution)/shard_map/pack/pallas_call | solution.py:211
  2.0 2.1 %collective-permute-start = (bf16[2,256,128]{2,1,0:T(8,128)(2,1)S(1)}, bf16[2,256,128]{2,1,0:T(8,128)(2,1)S(1)}, u32[]{:S(2)}, u32[]{:S(2)}) collective-permute-start(bf16[2,256,128]{2,1,0:T(8,128)(2,1)S(1)} %get-tuple-element.25), channel_id=1, source_target_pairs={{0,1},{1,0},{2,3},{3,2},{4,5},{5,4},{6,7},{7,6},{8,9},{9,8},{10,11... | collective-permute-start | bytes 393224 | tf_op jit(solution)/shard_map/ppermute | solution.py:199
  4.1 2.5 %collective-permute-start.1 = (bf16[2,256,128]{2,1,0:T(8,128)(2,1)S(1)}, bf16[2,256,128]{2,1,0:T(8,128)(2,1)S(1)}, u32[]{:S(2)}, u32[]{:S(2)}) collective-permute-start(bf16[2,256,128]{2,1,0:T(8,128)(2,1)S(1)} %get-tuple-element.26), channel_id=1, source_target_pairs={{0,2},{1,3},{2,0},{3,1},{4,6},{5,7},{6,4},{7,5},{8,10},{9,11},{10,... | collective-permute-start | bytes 393224 | tf_op jit(solution)/shard_map/ppermute | solution.py:199
  6.6 1.6 %collective-permute-start.2 = (bf16[2,256,128]{2,1,0:T(8,128)(2,1)S(1)}, bf16[2,256,128]{2,1,0:T(8,128)(2,1)S(1)}, u32[]{:S(2)}, u32[]{:S(2)}) collective-permute-start(bf16[2,256,128]{2,1,0:T(8,128)(2,1)S(1)} %get-tuple-element.27), channel_id=1, source_target_pairs={{0,4},{1,5},{2,6},{3,7},{4,0},{5,1},{6,2},{7,3},{8,12},{9,13},{10,... | collective-permute-start | bytes 393224 | tf_op jit(solution)/shard_map/ppermute | solution.py:199
  8.2 3.3 %collective-permute-start.3 = (bf16[2,256,128]{2,1,0:T(8,128)(2,1)S(1)}, bf16[2,256,128]{2,1,0:T(8,128)(2,1)S(1)}, u32[]{:S(2)}, u32[]{:S(2)}) collective-permute-start(bf16[2,256,128]{2,1,0:T(8,128)(2,1)S(1)} %get-tuple-element.28), channel_id=1, source_target_pairs={{0,8},{1,9},{2,10},{3,11},{4,12},{5,13},{6,14},{7,15},{8,0},{9,1},... | collective-permute-start | bytes 393224 | tf_op jit(solution)/shard_map/ppermute | solution.py:199
  11.5 0.0 collective-permute-start.4
  11.5 0.0 collective-permute-done.r1
  11.5 1.4 %collective-permute-start.5 = (bf16[2,272,128]{2,1,0:T(8,128)(2,1)S(1)}, bf16[2,272,128]{2,1,0:T(8,128)(2,1)S(1)}, u32[]{:S(2)}, u32[]{:S(2)}) collective-permute-start(bf16[2,272,128]{2,1,0:T(8,128)(2,1)S(1)} %get-tuple-element.33), channel_id=1, source_target_pairs={{0,2},{1,3},{2,0},{3,1},{4,6},{5,7},{6,4},{7,5},{8,10},{9,11},{10,... | collective-permute-start | bytes 417800 | tf_op jit(solution)/shard_map/ppermute | solution.py:199
  12.9 0.0 collective-permute-done.1.r2
  12.9 1.0 %collective-permute-start.6 = (bf16[2,272,128]{2,1,0:T(8,128)(2,1)S(1)}, bf16[2,272,128]{2,1,0:T(8,128)(2,1)S(1)}, u32[]{:S(2)}, u32[]{:S(2)}) collective-permute-start(bf16[2,272,128]{2,1,0:T(8,128)(2,1)S(1)} %get-tuple-element.34), channel_id=1, source_target_pairs={{0,4},{1,5},{2,6},{3,7},{4,0},{5,1},{6,2},{7,3},{8,12},{9,13},{10,... | collective-permute-start | bytes 417800 | tf_op jit(solution)/shard_map/ppermute | solution.py:199
  13.9 0.0 collective-permute-done.2.r3
  13.9 3.3 %collective-permute-start.7 = (bf16[2,272,128]{2,1,0:T(8,128)(2,1)S(1)}, bf16[2,272,128]{2,1,0:T(8,128)(2,1)S(1)}, u32[]{:S(2)}, u32[]{:S(2)}) collective-permute-start(bf16[2,272,128]{2,1,0:T(8,128)(2,1)S(1)} %get-tuple-element.35), channel_id=1, source_target_pairs={{0,8},{1,9},{2,10},{3,11},{4,12},{5,13},{6,14},{7,15},{8,0},{9,1},... | collective-permute-start | bytes 417800 | tf_op jit(solution)/shard_map/ppermute | solution.py:199
  17.3 1.1 %local_q.1 = (f32[256,256]{1,0:T(8,128)S(1)}, f32[2,256,128]{2,1,0:T(8,128)S(1)}, bf16[256,256]{1,0:T(8,128)(2,1)S(1)}) custom-call(s32[2,5]{1,0:T(2,128)S(1)} %copy-done.4, f32[1,256]{1,0:T(1,128)S(1)} %bitcast.27, bf16[256,256]{1,0:T(8,128)(2,1)S(1)} %bitcast.22, bf16[256,256]{1,0:T(8,128)(2,1)S(1)} %bitcast.14, bf16[256,256]{1,0:T(8,128)(2,1)S(1)} %bitcast.18, ...), custom_call_target="tpu_custom_call" | custom-call | tf_op jit(solution)/shard_map/local_q/pallas_call | solution.py:227
  18.4 0.0 collective-permute-done.3.r4
  18.4 2.2 %remote_q.1 = (f32[256,256]{1,0:T(8,128)S(1)}, f32[128,1,256]{2,1,0:T(1,128)}) custom-call(s32[2,5]{1,0:T(2,128)S(1)} %copy-done.4, bf16[256,256]{1,0:T(8,128)(2,1)S(1)} %get-tuple-element.22.scaled, bf16[256,256]{1,0:T(8,128)(2,1)S(1)} %bitcast.23, bf16[256,256]{1,0:T(8,128)(2,1)S(1)} %bitcast.11, f32[2,256,128]{2,1,0:T(8,128)S(1)} %get-tuple-element.23.norm_cols, ...), custom_call_target="tpu_custom_call" | custom-call | tf_op jit(solution)/shard_map/remote_q/pallas_call | solution.py:235
  20.6 9.3 %all-to-all-start = ((f32[128,1,256]{2,1,0:T(1,128)}), f32[128,1,256]{2,1,0:T(1,128)S(1)}, u32[]{:S(2)}, u32[]{:S(2)}) async-start(f32[128,1,256]{2,1,0:T(1,128)} %get-tuple-element.39), calls=%async_computation | async-start | bytes 262144 | tf_op jit(solution)/shard_map/all_to_all | solution.py:238
  30.0 1.2 %local_kv.1 = (f32[256,256]{1,0:T(8,128)S(1)}, f32[256,256]{1,0:T(8,128)S(1)}) custom-call(s32[2,5]{1,0:T(2,128)S(1)} %copy-done.4, bf16[256,256]{1,0:T(8,128)(2,1)S(1)} %get-tuple-element.22.scaled, bf16[256,256]{1,0:T(8,128)(2,1)S(1)} %bitcast.15, bf16[256,256]{1,0:T(8,128)(2,1)S(1)} %bitcast.19, bf16[256,256]{1,0:T(8,128)(2,1)S(1)} %bitcast.12, ...), custom_call_target="tpu_custom_call" | custom-call | tf_op jit(solution)/shard_map/local_kv/pallas_call | solution.py:239
  31.2 0.0 collective-permute-done.4.r1
  31.2 0.0 collective-permute-done.5.r2
  31.2 0.0 collective-permute-done.6.r3
  31.2 0.0 collective-permute-done.7.r4
  31.2 2.3 %remote_kv.1 = (bf16[256,256]{1,0:T(8,128)(2,1)}, bf16[256,256]{1,0:T(8,128)(2,1)}, bf16[256,256]{1,0:T(8,128)(2,1)}) custom-call(s32[2,5]{1,0:T(2,128)S(1)} %copy-done.4, f32[1,256]{1,0:T(1,128)S(1)} %bitcast.28, bf16[256,256]{1,0:T(8,128)(2,1)S(1)} %bitcast.16, bf16[256,256]{1,0:T(8,128)(2,1)S(1)} %bitcast.20, f32[256,256]{1,0:T(8,128)S(1)} %get-tuple-element.29.dq, ...), custom_call_target="tpu_custom_call" | custom-call | tf_op jit(solution)/shard_map/remote_kv/pallas_call | solution.py:243
  33.5 6.6 %all-to-all-done = f32[128,1,256]{2,1,0:T(1,128)S(1)} async-done(((f32[128,1,256]{2,1,0:T(1,128)}), f32[128,1,256]{2,1,0:T(1,128)S(1)}, u32[]{:S(2)}, u32[]{:S(2)}) %all-to-all-start) | async-done | bytes 131104 | tf_op jit(solution)/shard_map/all_to_all | solution.py:238
  40.2 0.7 %reduce_sum.9 = f32[256]{0:T(256)} reduce(f32[128,1,256]{2,1,0:T(1,128)S(1)} %all-to-all-done, f32[]{:T(128)} %constant.0.clone.1), dimensions={0,1}, to_apply=%region_0.0 | reduce | flops 32512 | bytes 132100 | tf_op jit(solution)/shard_map/reduce_sum | solution.py:246
  (14 shorter events, 0.0 us)
Async XLA Ops:
  0.6 16.6 %copy-start = (bf16[1,256,256]{2,1,0:T(8,128)(2,1)S(1)}, bf16[1,256,256]{2,1,0:T(8,128)(2,1)}, u32[]{:S(2)}) copy-start(bf16[1,256,256]{2,1,0:T(8,128)(2,1)} %param.10) | copy-start | bytes 393220
  0.6 16.6 %copy-start.1 = (bf16[1,256,256]{2,1,0:T(8,128)(2,1)S(1)}, bf16[1,256,256]{2,1,0:T(8,128)(2,1)}, u32[]{:S(2)}) copy-start(bf16[1,256,256]{2,1,0:T(8,128)(2,1)} %param.8) | copy-start | bytes 393220
  0.7 16.6 %copy-start.2 = (bf16[1,256,256]{2,1,0:T(8,128)(2,1)S(1)}, bf16[1,256,256]{2,1,0:T(8,128)(2,1)}, u32[]{:S(2)}) copy-start(bf16[1,256,256]{2,1,0:T(8,128)(2,1)} %param.9) | copy-start | bytes 393220
  0.7 16.6 %copy-start.3 = (bf16[1,256,256]{2,1,0:T(8,128)(2,1)S(1)}, bf16[1,256,256]{2,1,0:T(8,128)(2,1)}, u32[]{:S(2)}) copy-start(bf16[1,256,256]{2,1,0:T(8,128)(2,1)} %param.7) | copy-start | bytes 393220
  2.0 9.5 %collective-permute-start = (bf16[2,256,128]{2,1,0:T(8,128)(2,1)S(1)}, bf16[2,256,128]{2,1,0:T(8,128)(2,1)S(1)}, u32[]{:S(2)}, u32[]{:S(2)}) collective-permute-start(bf16[2,256,128]{2,1,0:T(8,128)(2,1)S(1)} %get-tuple-element.25), channel_id=1, source_target_pairs={{0,1},{1,0},{2,3},{3,2},{4,5},{5,4},{6,7},{7,6},{8,9},{9,8},{10,11... | collective-permute-start | bytes 393224 | tf_op jit(solution)/shard_map/ppermute | solution.py:199
  4.1 8.8 %collective-permute-start.1 = (bf16[2,256,128]{2,1,0:T(8,128)(2,1)S(1)}, bf16[2,256,128]{2,1,0:T(8,128)(2,1)S(1)}, u32[]{:S(2)}, u32[]{:S(2)}) collective-permute-start(bf16[2,256,128]{2,1,0:T(8,128)(2,1)S(1)} %get-tuple-element.26), channel_id=1, source_target_pairs={{0,2},{1,3},{2,0},{3,1},{4,6},{5,7},{6,4},{7,5},{8,10},{9,11},{10,... | collective-permute-start | bytes 393224 | tf_op jit(solution)/shard_map/ppermute | solution.py:199
  6.6 7.4 %collective-permute-start.2 = (bf16[2,256,128]{2,1,0:T(8,128)(2,1)S(1)}, bf16[2,256,128]{2,1,0:T(8,128)(2,1)S(1)}, u32[]{:S(2)}, u32[]{:S(2)}) collective-permute-start(bf16[2,256,128]{2,1,0:T(8,128)(2,1)S(1)} %get-tuple-element.27), channel_id=1, source_target_pairs={{0,4},{1,5},{2,6},{3,7},{4,0},{5,1},{6,2},{7,3},{8,12},{9,13},{10,... | collective-permute-start | bytes 393224 | tf_op jit(solution)/shard_map/ppermute | solution.py:199
  8.2 10.2 %collective-permute-start.3 = (bf16[2,256,128]{2,1,0:T(8,128)(2,1)S(1)}, bf16[2,256,128]{2,1,0:T(8,128)(2,1)S(1)}, u32[]{:S(2)}, u32[]{:S(2)}) collective-permute-start(bf16[2,256,128]{2,1,0:T(8,128)(2,1)S(1)} %get-tuple-element.28), channel_id=1, source_target_pairs={{0,8},{1,9},{2,10},{3,11},{4,12},{5,13},{6,14},{7,15},{8,0},{9,1},... | collective-permute-start | bytes 393224 | tf_op jit(solution)/shard_map/ppermute | solution.py:199
  11.5 5.7 %copy-start.6 = (f32[256]{0:T(256)S(1)}, f32[256]{0:T(256)}, u32[]{:S(2)}) copy-start(f32[256]{0:T(256)} %param.13) | copy-start | bytes 3076
  11.5 19.6 %collective-permute-start.4 = (bf16[2,272,128]{2,1,0:T(8,128)(2,1)S(1)}, bf16[2,272,128]{2,1,0:T(8,128)(2,1)S(1)}, u32[]{:S(2)}, u32[]{:S(2)}) collective-permute-start(bf16[2,272,128]{2,1,0:T(8,128)(2,1)S(1)} %get-tuple-element.32), channel_id=1, source_target_pairs={{0,1},{1,0},{2,3},{3,2},{4,5},{5,4},{6,7},{7,6},{8,9},{9,8},{10,11... | collective-permute-start | bytes 417800 | tf_op jit(solution)/shard_map/ppermute | solution.py:199
  11.5 19.6 %collective-permute-start.5 = (bf16[2,272,128]{2,1,0:T(8,128)(2,1)S(1)}, bf16[2,272,128]{2,1,0:T(8,128)(2,1)S(1)}, u32[]{:S(2)}, u32[]{:S(2)}) collective-permute-start(bf16[2,272,128]{2,1,0:T(8,128)(2,1)S(1)} %get-tuple-element.33), channel_id=1, source_target_pairs={{0,2},{1,3},{2,0},{3,1},{4,6},{5,7},{6,4},{7,5},{8,10},{9,11},{10,... | collective-permute-start | bytes 417800 | tf_op jit(solution)/shard_map/ppermute | solution.py:199
  12.9 4.4 %copy-start.5 = (f32[1,2,256]{2,1,0:T(2,128)S(1)}, f32[1,2,256]{2,1,0:T(2,128)}, u32[]{:S(2)}) copy-start(f32[1,2,256]{2,1,0:T(2,128)} %param.11) | copy-start | bytes 6148
  12.9 18.3 %collective-permute-start.6 = (bf16[2,272,128]{2,1,0:T(8,128)(2,1)S(1)}, bf16[2,272,128]{2,1,0:T(8,128)(2,1)S(1)}, u32[]{:S(2)}, u32[]{:S(2)}) collective-permute-start(bf16[2,272,128]{2,1,0:T(8,128)(2,1)S(1)} %get-tuple-element.34), channel_id=1, source_target_pairs={{0,4},{1,5},{2,6},{3,7},{4,0},{5,1},{6,2},{7,3},{8,12},{9,13},{10,... | collective-permute-start | bytes 417800 | tf_op jit(solution)/shard_map/ppermute | solution.py:199
  13.9 3.3 %copy-start.4 = (s32[2,5]{1,0:T(2,128)S(1)}, s32[2,5]{1,0:T(2,128)}, u32[]{:S(2)}) copy-start(s32[2,5]{1,0:T(2,128)} %offsets.7) | copy-start | bytes 124
  13.9 17.3 %collective-permute-start.7 = (bf16[2,272,128]{2,1,0:T(8,128)(2,1)S(1)}, bf16[2,272,128]{2,1,0:T(8,128)(2,1)S(1)}, u32[]{:S(2)}, u32[]{:S(2)}) collective-permute-start(bf16[2,272,128]{2,1,0:T(8,128)(2,1)S(1)} %get-tuple-element.35), channel_id=1, source_target_pairs={{0,8},{1,9},{2,10},{3,11},{4,12},{5,13},{6,14},{7,15},{8,0},{9,1},... | collective-permute-start | bytes 417800 | tf_op jit(solution)/shard_map/ppermute | solution.py:199
  20.6 19.5 %all-to-all-start = ((f32[128,1,256]{2,1,0:T(1,128)}), f32[128,1,256]{2,1,0:T(1,128)S(1)}, u32[]{:S(2)}, u32[]{:S(2)}) async-start(f32[128,1,256]{2,1,0:T(1,128)} %get-tuple-element.39), calls=%async_computation | async-start | bytes 262144 | tf_op jit(solution)/shard_map/all_to_all | solution.py:238

commit v5 on v4

--- a/solution.py
+++ b/solution.py
@@ -12,7 +12,8 @@
 HEADS = 2
 HD = 128
 SCALE = HD**-0.5
-ROW_Q, ROW_D, ROW_N, ROWS = 0, 128, 256, 272
+EARLY = 16
+PARTS, TAIL, FIRST, SECOND = 2 * BLOCK, 2 * BLOCK + 16, 2 * BLOCK + 16 + EARLY, 2 * BLOCK - EARLY
 
 HBM = pl.BlockSpec(memory_space=pltpu.HBM)
 ANY = pl.BlockSpec(memory_space=pl.ANY)
@@ -49,31 +50,32 @@
     outs, (offsets, k, v, q, d, norm, sems) = refs[:8], refs[8:]
     copies = []
     for i, (source, target) in enumerate(
-        ((offsets_in, offsets), (k_in, k), (v_in, v), (q_in, q), (d_in, d), (norm_in, norm))
+        ((offsets_in, offsets), (k_in, k), (v_in, v), (norm_in, norm), (d_in, d), (q_in, q))
     ):
         copies.append(pltpu.make_async_copy(source, target, sems.at[i]))
         copies[-1].start()
-    for copy in copies[:3]:
+    for copy in copies[:5]:
         copy.wait()
     spots = [(level, head, offsets[head, level] & 1) for level in range(1, LEVELS) for head in range(HEADS)]
+    row = lax.broadcasted_iota(jnp.int32, (16, BLOCK), 0)
     for level, head, block in spots:
         at, out = block_rows(block), outs[level - 1]
         out[head, :BLOCK] = k[at, cols(head)]
-        out[head, BLOCK:] = v[at, cols(head)]
-    for copy in copies[3:]:
-        copy.wait()
-    row = lax.broadcasted_iota(jnp.int32, (16, BLOCK), 0)
-    for level, head, block in spots:
-        at, out = block_rows(block), outs[LEVELS - 1 + level - 1]
-        out[head, ROW_Q : ROW_Q + BLOCK] = q[at, cols(head)]
-        out[head, ROW_D : ROW_D + BLOCK] = d[at, cols(head)]
+        out[head, BLOCK:PARTS] = v[at, cols(head)]
+        out[head, TAIL:] = d[pl.ds(pl.multiple_of(block * BLOCK + BLOCK - EARLY, EARLY), EARLY), cols(head)]
         whole = jnp.where(block == 0, norm[head : head + 1, :BLOCK], norm[head : head + 1, BLOCK:])
         high = whole.astype(jnp.bfloat16).astype(jnp.float32)
         rest = whole - high
         mid = rest.astype(jnp.bfloat16).astype(jnp.float32)
         low = rest - mid
         parts = jnp.where(row == 0, high, jnp.where(row == 1, mid, jnp.where(row == 2, low, 0.0)))
-        out[head, ROW_N:ROWS] = parts.astype(jnp.bfloat16)
+        out[head, PARTS:TAIL] = parts.astype(jnp.bfloat16)
+    for copy in copies[5:]:
+        copy.wait()
+    for level, head, block in spots:
+        at, out = block_rows(block), outs[LEVELS - 1 + level - 1]
+        out[head, :BLOCK] = q[at, cols(head)]
+        out[head, BLOCK:] = d[pl.ds(pl.multiple_of(block * BLOCK, BLOCK), BLOCK - EARLY), cols(head)]
 
 
 def block_counts(offsets, head):
@@ -133,7 +135,7 @@
             pl.when(spots[0][0] | spots[1][0])(both)
 
 
-def query_kernel(offsets, scaled, q, d, norm_cols, dq_in, r1, r2, r3, r4, dq, partial):
+def query_kernel(offsets, scaled, q, d, norm_cols, dq_in, r1, r2, r3, r4, p1, p2, p3, p4, dq, partial, *passed):
     received = (r1, r2, r3, r4)
     dq[...] = dq_in[...]
 
@@ -142,7 +144,7 @@
         for head in range(HEADS):
             active, block = spots[head]
             c, at = cols(head), block_rows(block)
-            key, value = got[head, :BLOCK], got[head, BLOCK:]
+            key, value = got[head, :BLOCK], got[head, BLOCK:PARTS]
             probs = jnp.exp(dot(scaled[at, c], key, NT) * SCALE - norm_cols[head, at, :])
             grads = (probs * dot(d[at, c], value, NT)).astype(jnp.bfloat16)
             dq[at, c] += jnp.where(active, dot(grads, key, NN), 0.0)
@@ -152,8 +154,8 @@
     partial[...] = jnp.broadcast_to(total[None], partial.shape)
 
 
-def key_kernel(offsets, gain, k, v, dq, dk_in, dv_in, r1, r2, r3, r4, grad_q, grad_k, grad_v, dk, dv):
-    received = (r1, r2, r3, r4)
+def key_kernel(offsets, gain, k, v, dq, dk_in, dv_in, f1, f2, f3, f4, r1, r2, r3, r4, grad_q, grad_k, grad_v, dk, dv):
+    received, firsts = (r1, r2, r3, r4), (f1, f2, f3, f4)
     dk[...] = dk_in[...]
     dv[...] = dv_in[...]
     grad_q[...] = (dq[...] * SCALE * gain[...]).astype(jnp.bfloat16)
@@ -163,9 +165,10 @@
         for head in range(HEADS):
             active, block = spots[head]
             c, at = cols(head), block_rows(block)
-            query = scale_rows(got[head, ROW_Q : ROW_Q + BLOCK], gain[:, c])
-            dout = got[head, ROW_D : ROW_D + BLOCK]
-            parts = got[head, ROW_N:ROWS].astype(jnp.float32)
+            query = scale_rows(got[head, :BLOCK], gain[:, c])
+            first = firsts[level - 1]
+            dout = jnp.concatenate([got[head, BLOCK:], first[head, TAIL:]], axis=0)
+            parts = first[head, PARTS:TAIL].astype(jnp.float32)
             norm = parts[0:1] + parts[1:2] + parts[2:3]
             probs = jnp.exp(dot(k[at, c], query, NT) * SCALE - norm)
             grads = (probs * dot(v[at, c], dout, NT)).astype(jnp.bfloat16)
@@ -211,7 +214,7 @@
     sent = call(
         pack_kernel,
         "pack",
-        [bf16((HEADS, 2 * BLOCK, HD))] * many + [bf16((HEADS, ROWS, HD))] * many,
+        [bf16((HEADS, FIRST, HD))] * many + [bf16((HEADS, SECOND, HD))] * many,
         [HBM] * 6,
         [
             pltpu.SMEM(offsets.shape, jnp.int32),
@@ -223,7 +226,7 @@
             pltpu.SemaphoreType.DMA((6,)),
         ],
     )(*map(in_hbm, (offsets, k, v, q, d, norm)))
-    got_kv, got_qd = swap(sent[:many]), swap(sent[many:])
+    got_kv = swap(sent[:many])
     dq, norm_cols, scaled = call(
         local_q_kernel,
         "local_q",
@@ -232,17 +235,23 @@
     )(offsets, gain, q, k, v, d, norm)
     axes = ("dp", "ctx")
     everyone = lax.axis_size(axes)
-    dq, partial = call(
-        query_kernel, "remote_q", [f32((tokens, width)), f32((everyone, 1, width))], [SMEM] + [VMEM] * 9
-    )(offsets, scaled, q, d, norm_cols, dq, *got_kv)
+    dq, partial, *later = call(
+        query_kernel,
+        "remote_q",
+        [f32((tokens, width)), f32((everyone, 1, width))] + [bf16((HEADS, SECOND, HD))] * many,
+        [SMEM] + [VMEM] * 9 + [ANY] * many,
+        out_specs=[VMEM] * 2 + [ANY] * many,
+        aliases={10 + i: 2 + i for i in range(many)},
+    )(offsets, scaled, q, d, norm_cols, dq, *got_kv, *sent[many:])
     parts = lax.all_to_all(partial, axes, 0, 0, tiled=True)
     dk, dv = call(local_kv_kernel, "local_kv", [f32((tokens, width))] * 2, [SMEM] + [VMEM] * 5)(
         offsets, scaled, k, v, d, norm
     )
+    got_qd = swap(later)
     acc = pltpu.VMEM((tokens, width), jnp.float32)
     grad_q, grad_k, grad_v = call(
-        key_kernel, "remote_kv", [bf16((tokens, width))] * 3, [SMEM] + [VMEM] * 10, [acc, acc]
-    )(offsets, gain, k, v, dq, dk, dv, *got_qd)
+        key_kernel, "remote_kv", [bf16((tokens, width))] * 3, [SMEM] + [VMEM] * 14, [acc, acc]
+    )(offsets, gain, k, v, dq, dk, dv, *got_kv, *got_qd)
     return (grad_q[None], grad_k[None], grad_v[None], jnp.sum(parts, axis=(0, 1)))
 
 

time: 40.6 us -> 44.2 us (1.089)
  Pallas kernels: 8.16 us -> 10.1 us
  waiting for transfers between devices: 6.67 us -> 8.5 us
    ppermute x8, waiting for transfers between devices: 0.02 us -> 8.5 us  [swap(): lax.ppermute(p, 'ctx', [(i, i ^ 1 << n) for i in range(count)])]
    all_to_all x1, waiting for transfers between devices: 6.65 us -> 0.01 us  [body(): parts = lax.all_to_all(partial, axes, 0, 0, tiled=True)]
    all_to_all x1, starting transfers between devices: 9.32 us -> 6.51 us  [body(): parts = lax.all_to_all(partial, axes, 0, 0, tiled=True)]
    ppermute x8, starting transfers between devices: 15.2 us -> 17.7 us  [swap(): lax.ppermute(p, 'ctx', [(i, i ^ 1 << n) for i in range(count)])]
    pallas_call x1, Pallas kernels: 2.3 us -> 3.28 us  [body(): call(key_kernel, 'remote_kv', [bf16((tokens, width))] * 3, [SMEM] + [VMEM...]
    pallas_call x1, Pallas kernels: 2.21 us -> 3.09 us  [body(): call(query_kernel, 'remote_q', [f32((tokens, width)), f32((everyone, 1, w...]
  transfers between devices with their start and end apart: 9 -> 9, of which waited for: 1 -> 4; matrix products, arithmetic and copies ran while one was open for 0% -> 0% of each run, Pallas kernels for 17% -> 13%
where the time goes in v5:
time: 44.2 us
  starting transfers between devices  24.2 us (55%)
  Pallas kernels  10.1 us (23%)
  waiting for transfers between devices  8.5 us (19%)
  between operations  0.76 us (2%)
  other arithmetic  0.72 us (2%)
    ppermute x8, starting transfers between devices, swap(): lax.ppermute(p, 'ctx', [(i, i ^ 1 << n) for i in range(count)])  17.7 us
    ppermute x8, waiting for transfers between devices, swap(): lax.ppermute(p, 'ctx', [(i, i ^ 1 << n) for i in range(count)])  8.5 us
    all_to_all x1, starting transfers between devices, body(): parts = lax.all_to_all(partial, axes, 0, 0, tiled=True)  6.51 us
    pallas_call x1, Pallas kernels, body(): call(key_kernel, 'remote_kv', [bf16((tokens, width))] * 3, [SMEM] + [VMEM...  3.28 us
    pallas_call x1, Pallas kernels, body(): call(query_kernel, 'remote_q', [f32((tokens, width)), f32((everyone, 1, w...  3.09 us
    pallas_call x1, Pallas kernels, body(): call(pack_kernel, 'pack', [bf16((HEADS, FIRST, HD))] * many + [bf16((HEAD...  1.38 us
    pallas_call x1, Pallas kernels, body(): call(local_kv_kernel, 'local_kv', [f32((tokens, width))] * 2, [SMEM] + [V...  1.2 us
    pallas_call x1, Pallas kernels, body(): call(local_q_kernel, 'local_q', [f32((tokens, width)), f32((HEADS, tokens...  1.12 us
  transfers between devices with their start and end apart: 9, of which 4 were waited for; matrix products, arithmetic and copies ran while one was open for 0% of the time, Pallas kernels for 13%

profile of v5, /device:TPU:1, one launch (start us, length us, event | category | flops | bytes accessed | tf_op | source)
XLA Modules:
  0.0 44.2 jit_solution(4076890494502537639)
XLA Ops:
  0.7 1.4 %pack.1 = (bf16[2,288,128]{2,1,0:T(8,128)(2,1)S(1)}, bf16[2,288,128]{2,1,0:T(8,128)(2,1)S(1)}, bf16[2,288,128]{2,1,0:T(8,128)(2,1)S(1)}, bf16[2,288,128]{2,1,0:T...) custom-call(s32[2,5]{1,0:T(2,128)} %offsets.7, ...), custom_call_target="tpu_custom_call" | custom-call | tf_op jit(solution)/shard_map/pack/pallas_call | solution.py:214
  2.1 0.0 copy-start.6
  2.1 2.1 %collective-permute-start = (bf16[2,288,128]{2,1,0:T(8,128)(2,1)S(1)}, bf16[2,288,128]{2,1,0:T(8,128)(2,1)S(1)}, u32[]{:S(2)}, u32[]{:S(2)}) collective-permute-start(bf16[2,288,128]{2,1,0:T(8,128)(2,1)S(1)} %get-tuple-element.29), channel_id=1, source_target_pairs={{0,1},{1,0},{2,3},{3,2},{4,5},{5,4},{6,7},{7,6},{8,9},{9,8},{10,11... | collective-permute-start | bytes 442376 | tf_op jit(solution)/shard_map/ppermute | solution.py:202
  4.2 2.5 %collective-permute-start.1 = (bf16[2,288,128]{2,1,0:T(8,128)(2,1)S(1)}, bf16[2,288,128]{2,1,0:T(8,128)(2,1)S(1)}, u32[]{:S(2)}, u32[]{:S(2)}) collective-permute-start(bf16[2,288,128]{2,1,0:T(8,128)(2,1)S(1)} %get-tuple-element.30), channel_id=1, source_target_pairs={{0,2},{1,3},{2,0},{3,1},{4,6},{5,7},{6,4},{7,5},{8,10},{9,11},{10,... | collective-permute-start | bytes 442376 | tf_op jit(solution)/shard_map/ppermute | solution.py:202
  6.6 1.6 %collective-permute-start.2 = (bf16[2,288,128]{2,1,0:T(8,128)(2,1)S(1)}, bf16[2,288,128]{2,1,0:T(8,128)(2,1)S(1)}, u32[]{:S(2)}, u32[]{:S(2)}) collective-permute-start(bf16[2,288,128]{2,1,0:T(8,128)(2,1)S(1)} %get-tuple-element.31), channel_id=1, source_target_pairs={{0,4},{1,5},{2,6},{3,7},{4,0},{5,1},{6,2},{7,3},{8,12},{9,13},{10,... | collective-permute-start | bytes 442376 | tf_op jit(solution)/shard_map/ppermute | solution.py:202
  8.3 3.3 %collective-permute-start.3 = (bf16[2,288,128]{2,1,0:T(8,128)(2,1)S(1)}, bf16[2,288,128]{2,1,0:T(8,128)(2,1)S(1)}, u32[]{:S(2)}, u32[]{:S(2)}) collective-permute-start(bf16[2,288,128]{2,1,0:T(8,128)(2,1)S(1)} %get-tuple-element.32), channel_id=1, source_target_pairs={{0,8},{1,9},{2,10},{3,11},{4,12},{5,13},{6,14},{7,15},{8,0},{9,1},... | collective-permute-start | bytes 442376 | tf_op jit(solution)/shard_map/ppermute | solution.py:202
  11.6 1.1 %local_q.1 = (f32[256,256]{1,0:T(8,128)S(1)}, f32[2,256,128]{2,1,0:T(8,128)S(1)}, bf16[256,256]{1,0:T(8,128)(2,1)S(1)}) custom-call(s32[2,5]{1,0:T(2,128)S(1)} %copy-done.4, f32[1,256]{1,0:T(1,128)S(1)} %bitcast.27, bf16[256,256]{1,0:T(8,128)(2,1)S(1)} %bitcast.22, bf16[256,256]{1,0:T(8,128)(2,1)S(1)} %bitcast.14, bf16[256,256]{1,0:T(8,128)(2,1)S(1)} %bitcast.18, ...), custom_call_target="tpu_custom_call" | custom-call | tf_op jit(solution)/shard_map/local_q/pallas_call | solution.py:230
  12.8 0.0 collective-permute-done.r1.f1
  12.8 0.3 collective-permute-done.1.r2.f2
  13.1 0.0 collective-permute-done.2.r3.f3
  13.1 4.0 %collective-permute-done.3.r4.f4 = bf16[2,288,128]{2,1,0:T(8,128)(2,1)S(1)} collective-permute-done((bf16[2,288,128]{2,1,0:T(8,128)(2,1)S(1)}, bf16[2,288,128]{2,1,0:T(8,128)(2,1)S(1)}, u32[]{:S(2)}, u32[]{:S(2)}) %collective-permute-start.3) | collective-permute-done | bytes 147488 | tf_op jit(solution)/shard_map/ppermute | solution.py:202
  17.1 3.1 %remote_q.1 = (f32[256,256]{1,0:T(8,128)S(1)}, f32[128,1,256]{2,1,0:T(1,128)}, bf16[2,240,128]{2,1,0:T(8,128)(2,1)S(1)}, bf16[2,240,128]{2,1,0:T(8,128)(2,1)S(1)...) custom-call(s32[2,5]{1,0:T(2,128)S(1)} %copy-done.4, ...), custom_call_target="tpu_custom_call", output_to_operand_aliasing={{2}: (10, {}), {3}: (11, {}), {4}: (12, {}), {5}: (13, {})} | custom-call | tf_op jit(solution)/shard_map/remote_q/pallas_call | solution.py:238
  20.2 6.5 %all-to-all-start = ((f32[128,1,256]{2,1,0:T(1,128)}), f32[128,1,256]{2,1,0:T(1,128)S(1)}, u32[]{:S(2)}, u32[]{:S(2)}) async-start(f32[128,1,256]{2,1,0:T(1,128)} %get-tuple-element.47), calls=%async_computation | async-start | bytes 262144 | tf_op jit(solution)/shard_map/all_to_all | solution.py:246
  26.7 1.5 %collective-permute-start.4 = (bf16[2,240,128]{2,1,0:T(8,128)(2,1)S(1)}, bf16[2,240,128]{2,1,0:T(8,128)(2,1)S(1)}, u32[]{:S(2)}, u32[]{:S(2)}) collective-permute-start(bf16[2,240,128]{2,1,0:T(8,128)(2,1)S(1)} %get-tuple-element.40), channel_id=1, source_target_pairs={{0,1},{1,0},{2,3},{3,2},{4,5},{5,4},{6,7},{7,6},{8,9},{9,8},{10,11... | collective-permute-start | bytes 368648 | tf_op jit(solution)/shard_map/ppermute | solution.py:202
  28.2 2.4 %collective-permute-start.5 = (bf16[2,240,128]{2,1,0:T(8,128)(2,1)S(1)}, bf16[2,240,128]{2,1,0:T(8,128)(2,1)S(1)}, u32[]{:S(2)}, u32[]{:S(2)}) collective-permute-start(bf16[2,240,128]{2,1,0:T(8,128)(2,1)S(1)} %get-tuple-element.41), channel_id=1, source_target_pairs={{0,2},{1,3},{2,0},{3,1},{4,6},{5,7},{6,4},{7,5},{8,10},{9,11},{10,... | collective-permute-start | bytes 368648 | tf_op jit(solution)/shard_map/ppermute | solution.py:202
  30.6 1.4 %collective-permute-start.6 = (bf16[2,240,128]{2,1,0:T(8,128)(2,1)S(1)}, bf16[2,240,128]{2,1,0:T(8,128)(2,1)S(1)}, u32[]{:S(2)}, u32[]{:S(2)}) collective-permute-start(bf16[2,240,128]{2,1,0:T(8,128)(2,1)S(1)} %get-tuple-element.42), channel_id=1, source_target_pairs={{0,4},{1,5},{2,6},{3,7},{4,0},{5,1},{6,2},{7,3},{8,12},{9,13},{10,... | collective-permute-start | bytes 368648 | tf_op jit(solution)/shard_map/ppermute | solution.py:202
  31.9 2.9 %collective-permute-start.7 = (bf16[2,240,128]{2,1,0:T(8,128)(2,1)S(1)}, bf16[2,240,128]{2,1,0:T(8,128)(2,1)S(1)}, u32[]{:S(2)}, u32[]{:S(2)}) collective-permute-start(bf16[2,240,128]{2,1,0:T(8,128)(2,1)S(1)} %get-tuple-element.43), channel_id=1, source_target_pairs={{0,8},{1,9},{2,10},{3,11},{4,12},{5,13},{6,14},{7,15},{8,0},{9,1},... | collective-permute-start | bytes 368648 | tf_op jit(solution)/shard_map/ppermute | solution.py:202
  34.8 1.2 %local_kv.1 = (f32[256,256]{1,0:T(8,128)S(1)}, f32[256,256]{1,0:T(8,128)S(1)}) custom-call(s32[2,5]{1,0:T(2,128)S(1)} %copy-done.4, bf16[256,256]{1,0:T(8,128)(2,1)S(1)} %get-tuple-element.26.scaled, bf16[256,256]{1,0:T(8,128)(2,1)S(1)} %bitcast.15, bf16[256,256]{1,0:T(8,128)(2,1)S(1)} %bitcast.19, bf16[256,256]{1,0:T(8,128)(2,1)S(1)} %bitcast.12, ...), custom_call_target="tpu_custom_call" | custom-call | tf_op jit(solution)/shard_map/local_kv/pallas_call | solution.py:247
  36.0 0.0 collective-permute-done.4.r1
  36.1 0.2 collective-permute-done.5.r2
  36.3 0.0 collective-permute-done.6.r3
  36.3 4.0 %collective-permute-done.7.r4 = bf16[2,240,128]{2,1,0:T(8,128)(2,1)S(1)} collective-permute-done((bf16[2,240,128]{2,1,0:T(8,128)(2,1)S(1)}, bf16[2,240,128]{2,1,0:T(8,128)(2,1)S(1)}, u32[]{:S(2)}, u32[]{:S(2)}) %collective-permute-start.7) | collective-permute-done | bytes 122912 | tf_op jit(solution)/shard_map/ppermute | solution.py:202
  40.2 3.3 %remote_kv.1 = (bf16[256,256]{1,0:T(8,128)(2,1)}, bf16[256,256]{1,0:T(8,128)(2,1)}, bf16[256,256]{1,0:T(8,128)(2,1)}) custom-call(s32[2,5]{1,0:T(2,128)S(1)} %copy-done.4, f32[1,256]{1,0:T(1,128)S(1)} %bitcast.28, bf16[256,256]{1,0:T(8,128)(2,1)S(1)} %bitcast.16, bf16[256,256]{1,0:T(8,128)(2,1)S(1)} %bitcast.20, f32[256,256]{1,0:T(8,128)S(1)} %get-tuple-element.37.dq, ...), custom_call_target="tpu_custom_call" | custom-call | tf_op jit(solution)/shard_map/remote_kv/pallas_call | solution.py:252
  43.5 0.7 %reduce_sum.9 = f32[256]{0:T(256)} reduce(f32[128,1,256]{2,1,0:T(1,128)S(1)} %all-to-all-done, f32[]{:T(128)} %constant.0.clone.1), dimensions={0,1}, to_apply=%region_0.0 | reduce | flops 32512 | bytes 132100 | tf_op jit(solution)/shard_map/reduce_sum | solution.py:255
  (14 shorter events, 0.0 us)
Async XLA Ops:
  0.6 11.0 %copy-start = (bf16[1,256,256]{2,1,0:T(8,128)(2,1)S(1)}, bf16[1,256,256]{2,1,0:T(8,128)(2,1)}, u32[]{:S(2)}) copy-start(bf16[1,256,256]{2,1,0:T(8,128)(2,1)} %param.10) | copy-start | bytes 393220
  0.6 11.0 %copy-start.1 = (bf16[1,256,256]{2,1,0:T(8,128)(2,1)S(1)}, bf16[1,256,256]{2,1,0:T(8,128)(2,1)}, u32[]{:S(2)}) copy-start(bf16[1,256,256]{2,1,0:T(8,128)(2,1)} %param.8) | copy-start | bytes 393220
  0.7 10.9 %copy-start.2 = (bf16[1,256,256]{2,1,0:T(8,128)(2,1)S(1)}, bf16[1,256,256]{2,1,0:T(8,128)(2,1)}, u32[]{:S(2)}) copy-start(bf16[1,256,256]{2,1,0:T(8,128)(2,1)} %param.9) | copy-start | bytes 393220
  0.7 10.9 %copy-start.3 = (bf16[1,256,256]{2,1,0:T(8,128)(2,1)S(1)}, bf16[1,256,256]{2,1,0:T(8,128)(2,1)}, u32[]{:S(2)}) copy-start(bf16[1,256,256]{2,1,0:T(8,128)(2,1)} %param.7) | copy-start | bytes 393220
  2.1 9.5 %copy-start.6 = (f32[256]{0:T(256)S(1)}, f32[256]{0:T(256)}, u32[]{:S(2)}) copy-start(f32[256]{0:T(256)} %param.13) | copy-start | bytes 3076
  2.1 10.7 %collective-permute-start = (bf16[2,288,128]{2,1,0:T(8,128)(2,1)S(1)}, bf16[2,288,128]{2,1,0:T(8,128)(2,1)S(1)}, u32[]{:S(2)}, u32[]{:S(2)}) collective-permute-start(bf16[2,288,128]{2,1,0:T(8,128)(2,1)S(1)} %get-tuple-element.29), channel_id=1, source_target_pairs={{0,1},{1,0},{2,3},{3,2},{4,5},{5,4},{6,7},{7,6},{8,9},{9,8},{10,11... | collective-permute-start | bytes 442376 | tf_op jit(solution)/shard_map/ppermute | solution.py:202
  4.2 8.9 %collective-permute-start.1 = (bf16[2,288,128]{2,1,0:T(8,128)(2,1)S(1)}, bf16[2,288,128]{2,1,0:T(8,128)(2,1)S(1)}, u32[]{:S(2)}, u32[]{:S(2)}) collective-permute-start(bf16[2,288,128]{2,1,0:T(8,128)(2,1)S(1)} %get-tuple-element.30), channel_id=1, source_target_pairs={{0,2},{1,3},{2,0},{3,1},{4,6},{5,7},{6,4},{7,5},{8,10},{9,11},{10,... | collective-permute-start | bytes 442376 | tf_op jit(solution)/shard_map/ppermute | solution.py:202
  6.6 5.0 %copy-start.5 = (f32[1,2,256]{2,1,0:T(2,128)S(1)}, f32[1,2,256]{2,1,0:T(2,128)}, u32[]{:S(2)}) copy-start(f32[1,2,256]{2,1,0:T(2,128)} %param.11) | copy-start | bytes 6148
  6.6 6.4 %collective-permute-start.2 = (bf16[2,288,128]{2,1,0:T(8,128)(2,1)S(1)}, bf16[2,288,128]{2,1,0:T(8,128)(2,1)S(1)}, u32[]{:S(2)}, u32[]{:S(2)}) collective-permute-start(bf16[2,288,128]{2,1,0:T(8,128)(2,1)S(1)} %get-tuple-element.31), channel_id=1, source_target_pairs={{0,4},{1,5},{2,6},{3,7},{4,0},{5,1},{6,2},{7,3},{8,12},{9,13},{10,... | collective-permute-start | bytes 442376 | tf_op jit(solution)/shard_map/ppermute | solution.py:202
  8.3 3.3 %copy-start.4 = (s32[2,5]{1,0:T(2,128)S(1)}, s32[2,5]{1,0:T(2,128)}, u32[]{:S(2)}) copy-start(s32[2,5]{1,0:T(2,128)} %offsets.7) | copy-start | bytes 124
  8.3 8.8 %collective-permute-start.3 = (bf16[2,288,128]{2,1,0:T(8,128)(2,1)S(1)}, bf16[2,288,128]{2,1,0:T(8,128)(2,1)S(1)}, u32[]{:S(2)}, u32[]{:S(2)}) collective-permute-start(bf16[2,288,128]{2,1,0:T(8,128)(2,1)S(1)} %get-tuple-element.32), channel_id=1, source_target_pairs={{0,8},{1,9},{2,10},{3,11},{4,12},{5,13},{6,14},{7,15},{8,0},{9,1},... | collective-permute-start | bytes 442376 | tf_op jit(solution)/shard_map/ppermute | solution.py:202
  20.2 23.3 %all-to-all-start = ((f32[128,1,256]{2,1,0:T(1,128)}), f32[128,1,256]{2,1,0:T(1,128)S(1)}, u32[]{:S(2)}, u32[]{:S(2)}) async-start(f32[128,1,256]{2,1,0:T(1,128)} %get-tuple-element.47), calls=%async_computation | async-start | bytes 262144 | tf_op jit(solution)/shard_map/all_to_all | solution.py:246
  26.7 9.4 %collective-permute-start.4 = (bf16[2,240,128]{2,1,0:T(8,128)(2,1)S(1)}, bf16[2,240,128]{2,1,0:T(8,128)(2,1)S(1)}, u32[]{:S(2)}, u32[]{:S(2)}) collective-permute-start(bf16[2,240,128]{2,1,0:T(8,128)(2,1)S(1)} %get-tuple-element.40), channel_id=1, source_target_pairs={{0,1},{1,0},{2,3},{3,2},{4,5},{5,4},{6,7},{7,6},{8,9},{9,8},{10,11... | collective-permute-start | bytes 368648 | tf_op jit(solution)/shard_map/ppermute | solution.py:202
  28.2 8.1 %collective-permute-start.5 = (bf16[2,240,128]{2,1,0:T(8,128)(2,1)S(1)}, bf16[2,240,128]{2,1,0:T(8,128)(2,1)S(1)}, u32[]{:S(2)}, u32[]{:S(2)}) collective-permute-start(bf16[2,240,128]{2,1,0:T(8,128)(2,1)S(1)} %get-tuple-element.41), channel_id=1, source_target_pairs={{0,2},{1,3},{2,0},{3,1},{4,6},{5,7},{6,4},{7,5},{8,10},{9,11},{10,... | collective-permute-start | bytes 368648 | tf_op jit(solution)/shard_map/ppermute | solution.py:202
  30.6 5.7 %collective-permute-start.6 = (bf16[2,240,128]{2,1,0:T(8,128)(2,1)S(1)}, bf16[2,240,128]{2,1,0:T(8,128)(2,1)S(1)}, u32[]{:S(2)}, u32[]{:S(2)}) collective-permute-start(bf16[2,240,128]{2,1,0:T(8,128)(2,1)S(1)} %get-tuple-element.42), channel_id=1, source_target_pairs={{0,4},{1,5},{2,6},{3,7},{4,0},{5,1},{6,2},{7,3},{8,12},{9,13},{10,... | collective-permute-start | bytes 368648 | tf_op jit(solution)/shard_map/ppermute | solution.py:202
  31.9 8.3 %collective-permute-start.7 = (bf16[2,240,128]{2,1,0:T(8,128)(2,1)S(1)}, bf16[2,240,128]{2,1,0:T(8,128)(2,1)S(1)}, u32[]{:S(2)}, u32[]{:S(2)}) collective-permute-start(bf16[2,240,128]{2,1,0:T(8,128)(2,1)S(1)} %get-tuple-element.43), channel_id=1, source_target_pairs={{0,8},{1,9},{2,10},{3,11},{4,12},{5,13},{6,14},{7,15},{8,0},{9,1},... | collective-permute-start | bytes 368648 | tf_op jit(solution)/shard_map/ppermute | solution.py:202

commit v6 on v4

--- a/solution.py
+++ b/solution.py
@@ -18,6 +18,7 @@
 ANY = pl.BlockSpec(memory_space=pl.ANY)
 VMEM = pl.BlockSpec(memory_space=pltpu.VMEM)
 SMEM = pl.BlockSpec(memory_space=pltpu.SMEM)
+ORDER = (4, 1, 2, 3)
 NT = (((1,), (1,)), ((), ()))
 TN = (((0,), (0,)), ((), ()))
 NN = (((1,), (0,)), ((), ()))
@@ -90,7 +91,7 @@
     return slice(b * BLOCK, (b + 1) * BLOCK), slice((1 - b) * BLOCK, (2 - b) * BLOCK)
 
 
-def local_q_kernel(offsets, gain, q, k, v, d, norm, dq, norm_cols, scaled):
+def local_q_kernel(offsets, gain, q, k, v, d, norm, dq, norm_cols, scaled, partial):
     for head in range(HEADS):
         c = cols(head)
         count = block_counts(offsets, head)
@@ -103,6 +104,7 @@
         for b in range(2):
             own, other = both_blocks(b)
             dq[own, c] = count[b] * dot(grads[own, own], key[own], NN) + dot(grads[own, other], key[other], NN)
+        partial[:, c] = jnp.sum(q[:, c].astype(jnp.float32) * dq[:, c], axis=0, keepdims=True)
 
 
 def local_kv_kernel(offsets, scaled, k, v, d, norm, dk, dv):
@@ -133,33 +135,34 @@
             pl.when(spots[0][0] | spots[1][0])(both)
 
 
-def query_kernel(offsets, scaled, q, d, norm_cols, dq_in, r1, r2, r3, r4, dq, partial):
-    received = (r1, r2, r3, r4)
-    dq[...] = dq_in[...]
+def query_kernel(offsets, scaled, q, d, norm_cols, partial_in, r1, r2, r3, r4, added, partial, total):
+    received = dict(zip(ORDER, (r1, r2, r3, r4)))
+    total[...] = partial_in[...]
 
     def one(level, spots):
-        got = received[level - 1]
+        got = received[level]
         for head in range(HEADS):
             active, block = spots[head]
             c, at = cols(head), block_rows(block)
             key, value = got[head, :BLOCK], got[head, BLOCK:]
             probs = jnp.exp(dot(scaled[at, c], key, NT) * SCALE - norm_cols[head, at, :])
             grads = (probs * dot(d[at, c], value, NT)).astype(jnp.bfloat16)
-            dq[at, c] += jnp.where(active, dot(grads, key, NN), 0.0)
+            more = jnp.where(active, dot(grads, key, NN), 0.0)
+            added[level - 1, head] = more
+            total[:, c] += jnp.sum(q[at, c].astype(jnp.float32) * more, axis=0, keepdims=True)
 
     for_each_level(offsets, one)
-    total = jnp.sum(q[...].astype(jnp.float32) * (dq[...] * SCALE), axis=0, keepdims=True)
-    partial[...] = jnp.broadcast_to(total[None], partial.shape)
-
-
-def key_kernel(offsets, gain, k, v, dq, dk_in, dv_in, r1, r2, r3, r4, grad_q, grad_k, grad_v, dk, dv):
-    received = (r1, r2, r3, r4)
+    partial[...] = jnp.broadcast_to((total[...] * SCALE)[None], partial.shape)
+
+
+def key_kernel(offsets, gain, k, v, dq_in, added, dk_in, dv_in, r1, r2, r3, r4, grad_q, grad_k, grad_v, dq, dk, dv):
+    received = dict(zip(ORDER, (r1, r2, r3, r4)))
+    dq[...] = dq_in[...]
     dk[...] = dk_in[...]
     dv[...] = dv_in[...]
-    grad_q[...] = (dq[...] * SCALE * gain[...]).astype(jnp.bfloat16)
 
     def one(level, spots):
-        got = received[level - 1]
+        got = received[level]
         for head in range(HEADS):
             active, block = spots[head]
             c, at = cols(head), block_rows(block)
@@ -169,10 +172,12 @@
             norm = parts[0:1] + parts[1:2] + parts[2:3]
             probs = jnp.exp(dot(k[at, c], query, NT) * SCALE - norm)
             grads = (probs * dot(v[at, c], dout, NT)).astype(jnp.bfloat16)
+            dq[at, c] += added[level - 1, head]
             dk[at, c] += jnp.where(active, dot(grads, query, NN), 0.0)
             dv[at, c] += jnp.where(active, dot(probs.astype(jnp.bfloat16), dout, NN), 0.0)
 
     for_each_level(offsets, one)
+    grad_q[...] = (dq[...] * SCALE * gain[...]).astype(jnp.bfloat16)
     grad_k[...] = (dk[...] * SCALE).astype(jnp.bfloat16)
     grad_v[...] = dv[...].astype(jnp.bfloat16)
 
@@ -194,9 +199,12 @@
     return pltpu.with_memory_space_constraint(array, pltpu.HBM)
 
 
-def swap(payloads):
-    count = lax.axis_size("ctx")
-    return [lax.ppermute(p, "ctx", [(i, i ^ (1 << n)) for i in range(count)]) for n, p in enumerate(payloads)]
+def swap(payloads, order=ORDER):
+    count, got = lax.axis_size("ctx"), {}
+    for level in order:
+        half = 1 << (level - 1)
+        got[level] = lax.ppermute(payloads[level - 1], "ctx", [(i, i ^ half) for i in range(count)])
+    return [got[level] for level in order]
 
 
 def body(queries, keys, values, grad_out, log_norm, offsets, q_gain):
@@ -224,25 +232,29 @@
         ],
     )(*map(in_hbm, (offsets, k, v, q, d, norm)))
     got_kv, got_qd = swap(sent[:many]), swap(sent[many:])
-    dq, norm_cols, scaled = call(
+    dq, norm_cols, scaled, partial = call(
         local_q_kernel,
         "local_q",
-        [f32((tokens, width)), f32((HEADS, tokens, HD)), bf16((tokens, width))],
+        [f32((tokens, width)), f32((HEADS, tokens, HD)), bf16((tokens, width)), f32((1, width))],
         [SMEM] + [VMEM] * 6,
     )(offsets, gain, q, k, v, d, norm)
     axes = ("dp", "ctx")
     everyone = lax.axis_size(axes)
-    dq, partial = call(
-        query_kernel, "remote_q", [f32((tokens, width)), f32((everyone, 1, width))], [SMEM] + [VMEM] * 9
-    )(offsets, scaled, q, d, norm_cols, dq, *got_kv)
+    added, partial = call(
+        query_kernel,
+        "remote_q",
+        [f32((many, HEADS, BLOCK, HD)), f32((everyone, 1, width))],
+        [SMEM] + [VMEM] * 9,
+        [pltpu.VMEM((1, width), jnp.float32)],
+    )(offsets, scaled, q, d, norm_cols, partial, *got_kv)
     parts = lax.all_to_all(partial, axes, 0, 0, tiled=True)
     dk, dv = call(local_kv_kernel, "local_kv", [f32((tokens, width))] * 2, [SMEM] + [VMEM] * 5)(
         offsets, scaled, k, v, d, norm
     )
     acc = pltpu.VMEM((tokens, width), jnp.float32)
     grad_q, grad_k, grad_v = call(
-        key_kernel, "remote_kv", [bf16((tokens, width))] * 3, [SMEM] + [VMEM] * 10, [acc, acc]
-    )(offsets, gain, k, v, dq, dk, dv, *got_qd)
+        key_kernel, "remote_kv", [bf16((tokens, width))] * 3, [SMEM] + [VMEM] * 11, [acc] * 3
+    )(offsets, gain, k, v, dq, added, dk, dv, *got_qd)
     return (grad_q[None], grad_k[None], grad_v[None], jnp.sum(parts, axis=(0, 1)))
 
 

time: 40.6 us -> 40 us (0.985); the launches traced: 40.9 us -> 39.8 us
  starting transfers between devices: 24.5 us -> 21.1 us
  waiting for transfers between devices: 6.67 us -> 8.02 us
  Pallas kernels: 8.16 us -> 9.12 us
    ppermute x8, starting transfers between devices: 15.2 us -> 12.1 us  [swap(): lax.ppermute(payloads[level - 1], 'ctx', [(i, i ^ half) for i in range(co...]
    ppermute x8, waiting for transfers between devices: 0.02 us -> 1.88 us  [swap(): lax.ppermute(payloads[level - 1], 'ctx', [(i, i ^ half) for i in range(co...]
    pallas_call x1, Pallas kernels: 2.3 us -> 2.81 us  [body(): call(key_kernel, 'remote_kv', [bf16((tokens, width))] * 3, [SMEM] + [VMEM...]
    all_to_all x1, waiting for transfers between devices: 6.65 us -> 6.14 us  [body(): parts = lax.all_to_all(partial, axes, 0, 0, tiled=True)]
    pallas_call x1, Pallas kernels: 2.21 us -> 2.64 us  [body(): call(query_kernel, 'remote_q', [f32((many, HEADS, BLOCK, HD)), f32((every...]
  transfers between devices with their start and end apart: 9 -> 9, of which waited for: 1 -> 2; matrix products, arithmetic and copies ran while one was open for 0% -> 0% of each run, Pallas kernels for 17% -> 20%
where the time goes in v6:
time: 40 us; the launch traced here: 39.8 us
  starting transfers between devices  21.1 us (53%)
  Pallas kernels  9.12 us (23%)
  waiting for transfers between devices  8.02 us (20%)
  between operations  0.78 us (2%)
  other arithmetic  0.71 us (2%)
    ppermute x8, starting transfers between devices, swap(): lax.ppermute(payloads[level - 1], 'ctx', [(i, i ^ half) for i in range(co...  12.1 us
    all_to_all x1, starting transfers between devices, body(): parts = lax.all_to_all(partial, axes, 0, 0, tiled=True)  9.01 us
    all_to_all x1, waiting for transfers between devices, body(): parts = lax.all_to_all(partial, axes, 0, 0, tiled=True)  6.14 us
    pallas_call x1, Pallas kernels, body(): call(key_kernel, 'remote_kv', [bf16((tokens, width))] * 3, [SMEM] + [VMEM...  2.81 us
    pallas_call x1, Pallas kernels, body(): call(query_kernel, 'remote_q', [f32((many, HEADS, BLOCK, HD)), f32((every...  2.64 us
    ppermute x8, waiting for transfers between devices, swap(): lax.ppermute(payloads[level - 1], 'ctx', [(i, i ^ half) for i in range(co...  1.88 us
    pallas_call x1, Pallas kernels, body(): call(pack_kernel, 'pack', [bf16((HEADS, 2 * BLOCK, HD))] * many + [bf16((...  1.33 us
    pallas_call x1, Pallas kernels, body(): call(local_kv_kernel, 'local_kv', [f32((tokens, width))] * 2, [SMEM] + [V...  1.2 us
  transfers between devices with their start and end apart: 9, of which 2 were waited for; matrix products, arithmetic and copies ran while one was open for 0% of the time, Pallas kernels for 20%

profile of v6, /device:TPU:1, one launch (start us, length us, event | category | flops | bytes accessed | tf_op | source)
XLA Modules:
  0.0 39.8 jit_solution(9962421697178584504)
XLA Ops:
  0.7 1.3 %pack.1 = (bf16[2,256,128]{2,1,0:T(8,128)(2,1)S(1)}, bf16[2,256,128]{2,1,0:T(8,128)(2,1)S(1)}, bf16[2,256,128]{2,1,0:T(8,128)(2,1)S(1)}, bf16[2,256,128]{2,1,0:T...) custom-call(s32[2,5]{1,0:T(2,128)} %offsets.7, ...), custom_call_target="tpu_custom_call" | custom-call | tf_op jit(solution)/shard_map/pack/pallas_call | solution.py:219
  2.0 4.5 %collective-permute-start = (bf16[2,256,128]{2,1,0:T(8,128)(2,1)S(1)}, bf16[2,256,128]{2,1,0:T(8,128)(2,1)S(1)}, u32[]{:S(2)}, u32[]{:S(2)}) collective-permute-start(bf16[2,256,128]{2,1,0:T(8,128)(2,1)S(1)} %get-tuple-element.27), channel_id=1, source_target_pairs={{0,8},{1,9},{2,10},{3,11},{4,12},{5,13},{6,14},{7,15},{8,0},{9,1},... | collective-permute-start | bytes 393224 | tf_op jit(solution)/shard_map/ppermute | solution.py:206
  6.5 1.2 %collective-permute-start.1 = (bf16[2,256,128]{2,1,0:T(8,128)(2,1)S(1)}, bf16[2,256,128]{2,1,0:T(8,128)(2,1)S(1)}, u32[]{:S(2)}, u32[]{:S(2)}) collective-permute-start(bf16[2,256,128]{2,1,0:T(8,128)(2,1)S(1)} %get-tuple-element.28), channel_id=1, source_target_pairs={{0,1},{1,0},{2,3},{3,2},{4,5},{5,4},{6,7},{7,6},{8,9},{9,8},{10,11... | collective-permute-start | bytes 393224 | tf_op jit(solution)/shard_map/ppermute | solution.py:206
  7.7 2.5 %collective-permute-start.2 = (bf16[2,256,128]{2,1,0:T(8,128)(2,1)S(1)}, bf16[2,256,128]{2,1,0:T(8,128)(2,1)S(1)}, u32[]{:S(2)}, u32[]{:S(2)}) collective-permute-start(bf16[2,256,128]{2,1,0:T(8,128)(2,1)S(1)} %get-tuple-element.29), channel_id=1, source_target_pairs={{0,2},{1,3},{2,0},{3,1},{4,6},{5,7},{6,4},{7,5},{8,10},{9,11},{10,... | collective-permute-start | bytes 393224 | tf_op jit(solution)/shard_map/ppermute | solution.py:206
  10.2 0.7 %collective-permute-start.3 = (bf16[2,256,128]{2,1,0:T(8,128)(2,1)S(1)}, bf16[2,256,128]{2,1,0:T(8,128)(2,1)S(1)}, u32[]{:S(2)}, u32[]{:S(2)}) collective-permute-start(bf16[2,256,128]{2,1,0:T(8,128)(2,1)S(1)} %get-tuple-element.30), channel_id=1, source_target_pairs={{0,4},{1,5},{2,6},{3,7},{4,0},{5,1},{6,2},{7,3},{8,12},{9,13},{10,... | collective-permute-start | bytes 393224 | tf_op jit(solution)/shard_map/ppermute | solution.py:206
  10.9 0.9 %collective-permute-start.4 = (bf16[2,272,128]{2,1,0:T(8,128)(2,1)S(1)}, bf16[2,272,128]{2,1,0:T(8,128)(2,1)S(1)}, u32[]{:S(2)}, u32[]{:S(2)}) collective-permute-start(bf16[2,272,128]{2,1,0:T(8,128)(2,1)S(1)} %get-tuple-element.34), channel_id=1, source_target_pairs={{0,8},{1,9},{2,10},{3,11},{4,12},{5,13},{6,14},{7,15},{8,0},{9,1},... | collective-permute-start | bytes 417800 | tf_op jit(solution)/shard_map/ppermute | solution.py:206
  11.8 0.0 collective-permute-done.r1
  11.8 0.0 collective-permute-start.5
  11.8 0.0 collective-permute-done.1.r2
  11.8 0.0 copy-start.5
  11.8 1.6 %collective-permute-start.6 = (bf16[2,272,128]{2,1,0:T(8,128)(2,1)S(1)}, bf16[2,272,128]{2,1,0:T(8,128)(2,1)S(1)}, u32[]{:S(2)}, u32[]{:S(2)}) collective-permute-start(bf16[2,272,128]{2,1,0:T(8,128)(2,1)S(1)} %get-tuple-element.36), channel_id=1, source_target_pairs={{0,2},{1,3},{2,0},{3,1},{4,6},{5,7},{6,4},{7,5},{8,10},{9,11},{10,... | collective-permute-start | bytes 417800 | tf_op jit(solution)/shard_map/ppermute | solution.py:206
  13.4 1.9 %collective-permute-done.2.r3 = bf16[2,256,128]{2,1,0:T(8,128)(2,1)S(1)} collective-permute-done((bf16[2,256,128]{2,1,0:T(8,128)(2,1)S(1)}, bf16[2,256,128]{2,1,0:T(8,128)(2,1)S(1)}, u32[]{:S(2)}, u32[]{:S(2)}) %collective-permute-start.2) | collective-permute-done | bytes 131104 | tf_op jit(solution)/shard_map/ppermute | solution.py:206
  15.3 0.7 %collective-permute-start.7 = (bf16[2,272,128]{2,1,0:T(8,128)(2,1)S(1)}, bf16[2,272,128]{2,1,0:T(8,128)(2,1)S(1)}, u32[]{:S(2)}, u32[]{:S(2)}) collective-permute-start(bf16[2,272,128]{2,1,0:T(8,128)(2,1)S(1)} %get-tuple-element.37), channel_id=1, source_target_pairs={{0,4},{1,5},{2,6},{3,7},{4,0},{5,1},{6,2},{7,3},{8,12},{9,13},{10,... | collective-permute-start | bytes 417800 | tf_op jit(solution)/shard_map/ppermute | solution.py:206
  16.1 1.1 %local_q.1 = (f32[256,256]{1,0:T(8,128)S(1)}, f32[2,256,128]{2,1,0:T(8,128)S(1)}, bf16[256,256]{1,0:T(8,128)(2,1)S(1)}, f32[1,256]{1,0:T(1,128)S(1)}) custom-call(s32[2,5]{1,0:T(2,128)S(1)} %copy-done.4, f32[1,256]{1,0:T(1,128)S(1)} %bitcast.27, bf16[256,256]{1,0:T(8,128)(2,1)S(1)} %bitcast.22, bf16[256,256]{1,0:T(8,128)(2,1)S(1)} %bitcast.14, ...), custom_call_target="tpu_custom_call" | custom-call | tf_op jit(solution)/shard_map/local_q/pallas_call | solution.py:235
  17.2 0.0 collective-permute-done.3.r4
  17.2 2.6 %remote_q.1 = (f32[4,2,128,128]{3,2,1,0:T(8,128)S(1)}, f32[128,1,256]{2,1,0:T(1,128)}) custom-call(s32[2,5]{1,0:T(2,128)S(1)} %copy-done.4, bf16[256,256]{1,0:T(8,128)(2,1)S(1)} %get-tuple-element.24.scaled, bf16[256,256]{1,0:T(8,128)(2,1)S(1)} %bitcast.23, bf16[256,256]{1,0:T(8,128)(2,1)S(1)} %bitcast.11, f32[2,256,128]{2,1,0:T(8,128)S(1)} %get-tuple-element.25.norm_cols, ...), custom_call_target="tpu_custom_call" | custom-call | tf_op jit(solution)/shard_map/remote_q/pallas_call | solution.py:243
  19.8 9.0 %all-to-all-start = ((f32[128,1,256]{2,1,0:T(1,128)}), f32[128,1,256]{2,1,0:T(1,128)S(1)}, u32[]{:S(2)}, u32[]{:S(2)}) async-start(f32[128,1,256]{2,1,0:T(1,128)} %get-tuple-element.41), calls=%async_computation | async-start | bytes 262144 | tf_op jit(solution)/shard_map/all_to_all | solution.py:250
  28.9 1.2 %local_kv.1 = (f32[256,256]{1,0:T(8,128)S(1)}, f32[256,256]{1,0:T(8,128)S(1)}) custom-call(s32[2,5]{1,0:T(2,128)S(1)} %copy-done.4, bf16[256,256]{1,0:T(8,128)(2,1)S(1)} %get-tuple-element.24.scaled, bf16[256,256]{1,0:T(8,128)(2,1)S(1)} %bitcast.15, bf16[256,256]{1,0:T(8,128)(2,1)S(1)} %bitcast.19, bf16[256,256]{1,0:T(8,128)(2,1)S(1)} %bitcast.12, ...), custom_call_target="tpu_custom_call" | custom-call | tf_op jit(solution)/shard_map/local_kv/pallas_call | solution.py:251
  30.1 0.0 collective-permute-done.4.r1
  30.1 0.0 collective-permute-done.5.r2
  30.1 0.0 collective-permute-done.7.r4
  30.1 2.8 %remote_kv.1 = (bf16[256,256]{1,0:T(8,128)(2,1)}, bf16[256,256]{1,0:T(8,128)(2,1)}, bf16[256,256]{1,0:T(8,128)(2,1)}) custom-call(s32[2,5]{1,0:T(2,128)S(1)} %copy-done.4, f32[1,256]{1,0:T(1,128)S(1)} %bitcast.28, bf16[256,256]{1,0:T(8,128)(2,1)S(1)} %bitcast.16, bf16[256,256]{1,0:T(8,128)(2,1)S(1)} %bitcast.20, f32[256,256]{1,0:T(8,128)S(1)} %get-tuple-element.23.dq_in, ...), custom_call_target="tpu_custom_call" | custom-call | tf_op jit(solution)/shard_map/remote_kv/pallas_call | solution.py:255
  32.9 6.1 %all-to-all-done = f32[128,1,256]{2,1,0:T(1,128)S(1)} async-done(((f32[128,1,256]{2,1,0:T(1,128)}), f32[128,1,256]{2,1,0:T(1,128)S(1)}, u32[]{:S(2)}, u32[]{:S(2)}) %all-to-all-start) | async-done | bytes 131104 | tf_op jit(solution)/shard_map/all_to_all | solution.py:250
  39.1 0.7 %reduce_sum.9 = f32[256]{0:T(256)} reduce(f32[128,1,256]{2,1,0:T(1,128)S(1)} %all-to-all-done, f32[]{:T(128)} %constant.0.clone.1), dimensions={0,1}, to_apply=%region_0.0 | reduce | flops 32512 | bytes 132100 | tf_op jit(solution)/shard_map/reduce_sum | solution.py:258
  (14 shorter events, 0.0 us)
Async XLA Ops:
  0.6 15.4 %copy-start = (bf16[1,256,256]{2,1,0:T(8,128)(2,1)S(1)}, bf16[1,256,256]{2,1,0:T(8,128)(2,1)}, u32[]{:S(2)}) copy-start(bf16[1,256,256]{2,1,0:T(8,128)(2,1)} %param.10) | copy-start | bytes 393220
  0.6 15.4 %copy-start.1 = (bf16[1,256,256]{2,1,0:T(8,128)(2,1)S(1)}, bf16[1,256,256]{2,1,0:T(8,128)(2,1)}, u32[]{:S(2)}) copy-start(bf16[1,256,256]{2,1,0:T(8,128)(2,1)} %param.8) | copy-start | bytes 393220
  0.7 15.4 %copy-start.2 = (bf16[1,256,256]{2,1,0:T(8,128)(2,1)S(1)}, bf16[1,256,256]{2,1,0:T(8,128)(2,1)}, u32[]{:S(2)}) copy-start(bf16[1,256,256]{2,1,0:T(8,128)(2,1)} %param.9) | copy-start | bytes 393220
  0.7 15.4 %copy-start.3 = (bf16[1,256,256]{2,1,0:T(8,128)(2,1)S(1)}, bf16[1,256,256]{2,1,0:T(8,128)(2,1)}, u32[]{:S(2)}) copy-start(bf16[1,256,256]{2,1,0:T(8,128)(2,1)} %param.7) | copy-start | bytes 393220
  2.0 9.8 %collective-permute-start = (bf16[2,256,128]{2,1,0:T(8,128)(2,1)S(1)}, bf16[2,256,128]{2,1,0:T(8,128)(2,1)S(1)}, u32[]{:S(2)}, u32[]{:S(2)}) collective-permute-start(bf16[2,256,128]{2,1,0:T(8,128)(2,1)S(1)} %get-tuple-element.27), channel_id=1, source_target_pairs={{0,8},{1,9},{2,10},{3,11},{4,12},{5,13},{6,14},{7,15},{8,0},{9,1},... | collective-permute-start | bytes 393224 | tf_op jit(solution)/shard_map/ppermute | solution.py:206
  6.5 5.3 %collective-permute-start.1 = (bf16[2,256,128]{2,1,0:T(8,128)(2,1)S(1)}, bf16[2,256,128]{2,1,0:T(8,128)(2,1)S(1)}, u32[]{:S(2)}, u32[]{:S(2)}) collective-permute-start(bf16[2,256,128]{2,1,0:T(8,128)(2,1)S(1)} %get-tuple-element.28), channel_id=1, source_target_pairs={{0,1},{1,0},{2,3},{3,2},{4,5},{5,4},{6,7},{7,6},{8,9},{9,8},{10,11... | collective-permute-start | bytes 393224 | tf_op jit(solution)/shard_map/ppermute | solution.py:206
  7.7 7.5 %collective-permute-start.2 = (bf16[2,256,128]{2,1,0:T(8,128)(2,1)S(1)}, bf16[2,256,128]{2,1,0:T(8,128)(2,1)S(1)}, u32[]{:S(2)}, u32[]{:S(2)}) collective-permute-start(bf16[2,256,128]{2,1,0:T(8,128)(2,1)S(1)} %get-tuple-element.29), channel_id=1, source_target_pairs={{0,2},{1,3},{2,0},{3,1},{4,6},{5,7},{6,4},{7,5},{8,10},{9,11},{10,... | collective-permute-start | bytes 393224 | tf_op jit(solution)/shard_map/ppermute | solution.py:206
  10.2 7.0 %collective-permute-start.3 = (bf16[2,256,128]{2,1,0:T(8,128)(2,1)S(1)}, bf16[2,256,128]{2,1,0:T(8,128)(2,1)S(1)}, u32[]{:S(2)}, u32[]{:S(2)}) collective-permute-start(bf16[2,256,128]{2,1,0:T(8,128)(2,1)S(1)} %get-tuple-element.30), channel_id=1, source_target_pairs={{0,4},{1,5},{2,6},{3,7},{4,0},{5,1},{6,2},{7,3},{8,12},{9,13},{10,... | collective-permute-start | bytes 393224 | tf_op jit(solution)/shard_map/ppermute | solution.py:206
  10.9 5.1 %copy-start.6 = (f32[256]{0:T(256)S(1)}, f32[256]{0:T(256)}, u32[]{:S(2)}) copy-start(f32[256]{0:T(256)} %param.13) | copy-start | bytes 3076
  10.9 19.2 %collective-permute-start.4 = (bf16[2,272,128]{2,1,0:T(8,128)(2,1)S(1)}, bf16[2,272,128]{2,1,0:T(8,128)(2,1)S(1)}, u32[]{:S(2)}, u32[]{:S(2)}) collective-permute-start(bf16[2,272,128]{2,1,0:T(8,128)(2,1)S(1)} %get-tuple-element.34), channel_id=1, source_target_pairs={{0,8},{1,9},{2,10},{3,11},{4,12},{5,13},{6,14},{7,15},{8,0},{9,1},... | collective-permute-start | bytes 417800 | tf_op jit(solution)/shard_map/ppermute | solution.py:206
  11.8 18.3 %collective-permute-start.5 = (bf16[2,272,128]{2,1,0:T(8,128)(2,1)S(1)}, bf16[2,272,128]{2,1,0:T(8,128)(2,1)S(1)}, u32[]{:S(2)}, u32[]{:S(2)}) collective-permute-start(bf16[2,272,128]{2,1,0:T(8,128)(2,1)S(1)} %get-tuple-element.35), channel_id=1, source_target_pairs={{0,1},{1,0},{2,3},{3,2},{4,5},{5,4},{6,7},{7,6},{8,9},{9,8},{10,11... | collective-permute-start | bytes 417800 | tf_op jit(solution)/shard_map/ppermute | solution.py:206
  11.8 4.2 %copy-start.5 = (f32[1,2,256]{2,1,0:T(2,128)S(1)}, f32[1,2,256]{2,1,0:T(2,128)}, u32[]{:S(2)}) copy-start(f32[1,2,256]{2,1,0:T(2,128)} %param.11) | copy-start | bytes 6148
  11.8 18.3 %collective-permute-start.6 = (bf16[2,272,128]{2,1,0:T(8,128)(2,1)S(1)}, bf16[2,272,128]{2,1,0:T(8,128)(2,1)S(1)}, u32[]{:S(2)}, u32[]{:S(2)}) collective-permute-start(bf16[2,272,128]{2,1,0:T(8,128)(2,1)S(1)} %get-tuple-element.36), channel_id=1, source_target_pairs={{0,2},{1,3},{2,0},{3,1},{4,6},{5,7},{6,4},{7,5},{8,10},{9,11},{10,... | collective-permute-start | bytes 417800 | tf_op jit(solution)/shard_map/ppermute | solution.py:206
  15.3 0.8 %copy-start.4 = (s32[2,5]{1,0:T(2,128)S(1)}, s32[2,5]{1,0:T(2,128)}, u32[]{:S(2)}) copy-start(s32[2,5]{1,0:T(2,128)} %offsets.7) | copy-start | bytes 124
  15.3 14.8 %collective-permute-start.7 = (bf16[2,272,128]{2,1,0:T(8,128)(2,1)S(1)}, bf16[2,272,128]{2,1,0:T(8,128)(2,1)S(1)}, u32[]{:S(2)}, u32[]{:S(2)}) collective-permute-start(bf16[2,272,128]{2,1,0:T(8,128)(2,1)S(1)} %get-tuple-element.37), channel_id=1, source_target_pairs={{0,4},{1,5},{2,6},{3,7},{4,0},{5,1},{6,2},{7,3},{8,12},{9,13},{10,... | collective-permute-start | bytes 417800 | tf_op jit(solution)/shard_map/ppermute | solution.py:206
  19.8 19.2 %all-to-all-start = ((f32[128,1,256]{2,1,0:T(1,128)}), f32[128,1,256]{2,1,0:T(1,128)S(1)}, u32[]{:S(2)}, u32[]{:S(2)}) async-start(f32[128,1,256]{2,1,0:T(1,128)} %get-tuple-element.41), calls=%async_computation | async-start | bytes 262144 | tf_op jit(solution)/shard_map/all_to_all | solution.py:250

commit v7 on v6

v7 whole, which is shorter than its diff:
```python
import functools

import jax
import jax.numpy as jnp
from jax import lax
from jax.experimental import pallas as pl
from jax.experimental.pallas import tpu as pltpu
from jax.sharding import PartitionSpec as P

BLOCK = 128
LEVELS = 5
HEADS = 2
HD = 128
SCALE = HD**-0.5
LATE, EARLY, PARTS = (4,), 16, 16

HBM = pl.BlockSpec(memory_space=pltpu.HBM)
ANY = pl.BlockSpec(memory_space=pl.ANY)
VMEM = pl.BlockSpec(memory_space=pltpu.VMEM)
SMEM = pl.BlockSpec(memory_space=pltpu.SMEM)
ORDER = (4, 1, 2, 3)
SOON = tuple(level for level in ORDER if level not in LATE)
NT = (((1,), (1,)), ((), ()))
TN = (((0,), (0,)), ((), ()))
NN = (((1,), (0,)), ((), ()))


def dot(left, right, dims):
    return lax.dot_general(left, right, dims, preferred_element_type=jnp.float32)


def cols(head):
    return slice(head * HD, (head + 1) * HD)


def place(offsets, me, head, level):
    half = 1 << (level - 1)
    shift = offsets[head, level] & (2 * half - 1)
    return (me & (half - 1)) == (shift >> 1), shift & 1


def block_rows(block):
    return pl.ds(pl.multiple_of(block * BLOCK, BLOCK), BLOCK)


def scale_rows(rows, gain):
    return (rows.astype(jnp.float32) * gain).astype(jnp.bfloat16)


def pack_kernel(offsets_in, k_in, v_in, q_in, d_in, norm_in, gain_in, *refs):
    outs, (norm, gain, table), (offsets, k, v, q, d, sems) = refs[:8], refs[8:11], refs[11:]
    copies = []
    moves = ((offsets_in, offsets), (k_in, k), (v_in, v), (q_in, q), (d_in, d))
    for i, (source, target) in enumerate(moves + ((norm_in, norm), (gain_in, gain), (offsets_in, table))):
        copies.append(pltpu.make_async_copy(source, target, sems.at[i]))
        copies[-1].start()
    for copy in copies:
        copy.wait()
    row = lax.broadcasted_iota(jnp.int32, (PARTS, BLOCK), 0)
    for level in range(1, LEVELS):
        first, second = outs[level - 1], outs[LEVELS - 1 + level - 1]
        for head in range(HEADS):
            block, c = offsets[head, level] & 1, cols(head)
            at = block_rows(block)
            first[head, :BLOCK] = k[at, c]
            first[head, BLOCK : 2 * BLOCK] = v[at, c]
            second[head, :BLOCK] = q[at, c]
            whole = jnp.where(block == 0, norm[head : head + 1, :BLOCK], norm[head : head + 1, BLOCK:])
            high = whole.astype(jnp.bfloat16).astype(jnp.float32)
            rest = whole - high
            mid = rest.astype(jnp.bfloat16).astype(jnp.float32)
            low = rest - mid
            parts = jnp.where(row == 0, high, jnp.where(row == 1, mid, jnp.where(row == 2, low, 0.0)))
            parts = parts.astype(jnp.bfloat16)
            if level in LATE:
                start = pl.multiple_of(block * BLOCK, BLOCK)
                first[head, 2 * BLOCK : 2 * BLOCK + PARTS] = parts
                first[head, 2 * BLOCK + PARTS :] = d[pl.ds(start + BLOCK - EARLY, EARLY), c]
                second[head, BLOCK:] = d[pl.ds(start, BLOCK - EARLY), c]
            else:
                second[head, BLOCK : 2 * BLOCK] = d[at, c]
                second[head, 2 * BLOCK :] = parts


def block_counts(offsets, head):
    me = lax.axis_index("ctx")
    count = [jnp.float32(1.0), jnp.float32(1.0)]
    for level in range(1, LEVELS):
        active, block = place(offsets, me, head, level)
        for b in range(2):
            count[b] = count[b] + jnp.where(active & (block == b), 1.0, 0.0)
    return count


def both_blocks(b):
    return slice(b * BLOCK, (b + 1) * BLOCK), slice((1 - b) * BLOCK, (2 - b) * BLOCK)


def local_q_kernel(offsets, gain, q, k, v, d, norm, *refs):
    dq, norm_cols, scaled, partial = refs[LEVELS - 1 - len(LATE) :][:4]
    for head in range(HEADS):
        c = cols(head)
        count = block_counts(offsets, head)
        query, key, value, dout = scale_rows(q[:, c], gain[:, c]), k[:, c], v[:, c], d[:, c]
        scaled[:, c] = query
        column = jnp.transpose(jnp.broadcast_to(norm[head : head + 1, :], (BLOCK, 2 * BLOCK)))
        norm_cols[head] = column
        probs = jnp.exp(dot(query, key, NT) * SCALE - jnp.concatenate([column, column], axis=1))
        grads = (probs * dot(dout, value, NT)).astype(jnp.bfloat16)
        for b in range(2):
            own, other = both_blocks(b)
            dq[own, c] = count[b] * dot(grads[own, own], key[own], NN) + dot(grads[own, other], key[other], NN)
        partial[:, c] = jnp.sum(q[:, c].astype(jnp.float32) * dq[:, c], axis=0, keepdims=True)


def for_each_level(offsets, levels, fn):
    me = lax.axis_index("ctx")
    for level in levels:
        spots = [place(offsets, me, head, level) for head in range(HEADS)]

        def both(level=level, spots=spots):
            fn(level, spots)

        if level == 1:
            both()
        else:
            pl.when(spots[0][0] | spots[1][0])(both)


def query_kernel(offsets, scaled, q, d, norm_cols, partial_in, r1, r2, r3, r4, *refs):
    added, partial, total = refs[len(LATE)], refs[len(LATE) + 1], refs[-1]
    received = dict(zip(ORDER, (r1, r2, r3, r4)))
    total[...] = partial_in[...]

    def one(level, spots):
        got = received[level]
        for head in range(HEADS):
            active, block = spots[head]
            c, at = cols(head), block_rows(block)
            key, value = got[head, :BLOCK], got[head, BLOCK : 2 * BLOCK]
            probs = jnp.exp(dot(scaled[at, c], key, NT) * SCALE - norm_cols[head, at, :])
            grads = (probs * dot(d[at, c], value, NT)).astype(jnp.bfloat16)
            more = jnp.where(active, dot(grads, key, NN), 0.0)
            added[level - 1, head] = more
            total[:, c] += jnp.sum(q[at, c].astype(jnp.float32) * more, axis=0, keepdims=True)

    for_each_level(offsets, range(1, LEVELS), one)
    partial[...] = jnp.broadcast_to((total[...] * SCALE)[None], partial.shape)


def add_keys(level, spots, got, first, gain, k, v, dk, dv):
    for head in range(HEADS):
        active, block = spots[head]
        c, at = cols(head), block_rows(block)
        query = scale_rows(got[head, :BLOCK], gain[:, c])
        if level in LATE:
            parts = first[head, 2 * BLOCK : 2 * BLOCK + PARTS]
            dout = jnp.concatenate([got[head, BLOCK:], first[head, 2 * BLOCK + PARTS :]], axis=0)
        else:
            parts, dout = got[head, 2 * BLOCK :], got[head, BLOCK : 2 * BLOCK]
        parts = parts.astype(jnp.float32)
        norm = parts[0:1] + parts[1:2] + parts[2:3]
        probs = jnp.exp(dot(k[at, c], query, NT) * SCALE - norm)
        grads = (probs * dot(v[at, c], dout, NT)).astype(jnp.bfloat16)
        dk[at, c] += jnp.where(active, dot(grads, query, NN), 0.0)
        dv[at, c] += jnp.where(active, dot(probs.astype(jnp.bfloat16), dout, NN), 0.0)


def most_kernel(offsets, gain, scaled, k, v, d, norm, dq_in, added, r1, r2, r3, grad_q, dk, dv, dq):
    received = dict(zip(SOON, (r1, r2, r3)))
    for head in range(HEADS):
        c = cols(head)
        count = block_counts(offsets, head)
        query, key, value, dout = scaled[:, c], k[:, c], v[:, c], d[:, c]
        probs = jnp.exp(dot(key, query, NT) * SCALE - norm[head : head + 1, :])
        grads = (probs * dot(value, dout, NT)).astype(jnp.bfloat16)
        probs = probs.astype(jnp.bfloat16)
        for b in range(2):
            own, other = both_blocks(b)
            dk[own, c] = count[b] * dot(grads[own, own], query[own], NN) + dot(grads[own, other], query[other], NN)
            dv[own, c] = count[b] * dot(probs[own, own], dout[own], NN) + dot(probs[own, other], dout[other], NN)
    dq[...] = dq_in[...]

    def add_queries(level, spots):
        for head in range(HEADS):
            dq[block_rows(spots[head][1]), cols(head)] += added[level - 1, head]

    for_each_level(offsets, range(1, LEVELS), add_queries)
    grad_q[...] = (dq[...] * SCALE * gain[...]).astype(jnp.bfloat16)
    for_each_level(
        offsets, SOON, lambda level, spots: add_keys(level, spots, received[level], None, gain, k, v, dk, dv)
    )


def last_kernel(offsets, gain, k, v, dk_in, dv_in, got, first, grad_k, grad_v, dk, dv):
    dk[...] = dk_in[...]
    dv[...] = dv_in[...]
    for_each_level(offsets, LATE, lambda level, spots: add_keys(level, spots, got, first, gain, k, v, dk, dv))
    grad_k[...] = (dk[...] * SCALE).astype(jnp.bfloat16)
    grad_v[...] = dv[...].astype(jnp.bfloat16)


def call(kernel, name, outs, in_specs, scratch=(), out_specs=None, aliases=None):
    return pl.pallas_call(
        kernel,
        name=name,
        out_shape=outs,
        in_specs=in_specs,
        out_specs=out_specs or [VMEM] * len(outs),
        scratch_shapes=list(scratch),
        input_output_aliases=aliases or {},
        compiler_params=pltpu.CompilerParams(vmem_limit_bytes=32 * 1024 * 1024),
    )


def in_hbm(array):
    return pltpu.with_memory_space_constraint(array, pltpu.HBM)


def swap(payloads):
    count, got = lax.axis_size("ctx"), {}
    for level, payload in payloads.items():
        half = 1 << (level - 1)
        got[level] = lax.ppermute(payload, "ctx", [(i, i ^ half) for i in range(count)])
    return got


def body(queries, keys, values, grad_out, log_norm, offsets, q_gain):
    q, k, v, d = queries[0], keys[0], values[0], grad_out[0]
    norm = log_norm[0]
    tokens, width = q.shape
    gain = q_gain.reshape(1, width)
    f32 = functools.partial(jax.ShapeDtypeStruct, dtype=jnp.float32)
    bf16 = functools.partial(jax.ShapeDtypeStruct, dtype=jnp.bfloat16)
    many = LEVELS - 1
    raw = pltpu.VMEM((tokens, width), jnp.bfloat16)
    *sent, norm, gain, table = call(
        pack_kernel,
        "pack",
        [bf16((HEADS, 2 * BLOCK + (PARTS + EARLY) * (level in LATE), HD)) for level in range(1, LEVELS)]
        + [bf16((HEADS, 2 * BLOCK + (-EARLY if level in LATE else PARTS), HD)) for level in range(1, LEVELS)]
        + [f32(norm.shape), f32(gain.shape), jax.ShapeDtypeStruct(offsets.shape, jnp.int32)],
        [HBM] * 7,
        [pltpu.SMEM(offsets.shape, jnp.int32), raw, raw, raw, raw, pltpu.SemaphoreType.DMA((8,))],
    )(*map(in_hbm, (offsets, k, v, q, d, norm, gain)))
    offsets = table
    second = dict(zip(range(1, LEVELS), sent[many:]))
    got_kv = swap({level: sent[level - 1] for level in ORDER})
    early = {level: second[level] for level in ORDER if level not in LATE}
    dq, norm_cols, scaled, partial, *passed = call(
        local_q_kernel,
        "local_q",
        [f32((tokens, width)), f32((HEADS, tokens, HD)), bf16((tokens, width)), f32((1, width))]
        + [bf16(p.shape) for p in early.values()],
        [SMEM] + [VMEM] * 6 + [ANY] * len(early),
        out_specs=[VMEM] * 4 + [ANY] * len(early),
        aliases={7 + i: 4 + i for i in range(len(early))},
    )(offsets, gain, q, k, v, d, norm, *early.values())
    got_qd = swap(dict(zip(early, passed)))
    axes = ("dp", "ctx")
    everyone = lax.axis_size(axes)
    late = [second[level] for level in LATE]
    added, partial, *late = call(
        query_kernel,
        "remote_q",
        [f32((many, HEADS, BLOCK, HD)), f32((everyone, 1, width))] + [bf16(p.shape) for p in late],
        [SMEM] + [VMEM] * 9 + [ANY] * len(late),
        [pltpu.VMEM((1, width), jnp.float32)],
        [VMEM] * 2 + [ANY] * len(late),
        {10 + i: 2 + i for i in range(len(late))},
    )(offsets, scaled, q, d, norm_cols, partial, *(got_kv[level] for level in ORDER), *late)
    got_qd.update(swap(dict(zip(LATE, late))))
    parts = lax.all_to_all(partial, axes, 0, 0, tiled=True)
    acc = pltpu.VMEM((tokens, width), jnp.float32)
    grad_q, dk, dv = call(
        most_kernel,
        "most_kv",
        [bf16((tokens, width)), f32((tokens, width)), f32((tokens, width))],
        [SMEM] + [VMEM] * 11,
        [acc],
    )(offsets, gain, scaled, k, v, d, norm, dq, added, *(got_qd[level] for level in SOON))
    grad_k, grad_v = call(
        last_kernel, "last_kv", [bf16((tokens, width))] * 2, [SMEM] + [VMEM] * 7, [acc, acc]
    )(offsets, gain, k, v, dk, dv, got_qd[LATE[0]], got_kv[LATE[0]])
    return (grad_q[None], grad_k[None], grad_v[None], jnp.sum(parts, axis=(0, 1)))


def solution(mesh):
    rows = P("dp", "ctx", None)
    in_specs = (rows, rows, rows, rows, P("dp", None, "ctx"), P(), P())
    out_specs = (rows, rows, rows, P())
    return jax.shard_map(body, mesh=mesh, in_specs=in_specs, out_specs=out_specs, check_vma=False)
```

time: 40 us -> 38.6 us (0.965)
  waiting for transfers between devices: 8.02 us -> 4.37 us
  starting transfers between devices: 21.1 us -> 23.6 us
    all_to_all x1, waiting for transfers between devices: 6.14 us -> 1.64 us  [body(): parts = lax.all_to_all(partial, axes, 0, 0, tiled=True)]
    ppermute x8, starting transfers between devices: 12.1 us -> 14.4 us  [swap(): lax.ppermute(payload, 'ctx', [(i, i ^ half) for i in range(count)])]
    ppermute x8, waiting for transfers between devices: 1.88 us -> 2.73 us  [swap(): lax.ppermute(payload, 'ctx', [(i, i ^ half) for i in range(count)])]
    pallas_call x1, Pallas kernels: 2.64 us -> 2.19 us  [body(): call(query_kernel, 'remote_q', [f32((many, HEADS, BLOCK, HD)), f32((every...]
  transfers between devices with their start and end apart: 9 -> 9, of which waited for: 2 -> 3; matrix products, arithmetic and copies ran while one was open for 0% -> 0% of each run, Pallas kernels for 20% -> 20%
where the time goes in v7:
time: 38.6 us; the launch traced here: 38.4 us
  starting transfers between devices  23.6 us (61%)
  Pallas kernels  8.98 us (23%)
  waiting for transfers between devices  4.37 us (11%)
  between operations  0.72 us (2%)
  other arithmetic  0.71 us (2%)
    ppermute x8, starting transfers between devices, swap(): lax.ppermute(payload, 'ctx', [(i, i ^ half) for i in range(count)])  14.4 us
    all_to_all x1, starting transfers between devices, body(): parts = lax.all_to_all(partial, axes, 0, 0, tiled=True)  9.18 us
    ppermute x8, waiting for transfers between devices, swap(): lax.ppermute(payload, 'ctx', [(i, i ^ half) for i in range(count)])  2.73 us
    pallas_call x1, Pallas kernels, body(): call(most_kernel, 'most_kv', [bf16((tokens, width)), f32((tokens, width))...  2.42 us
    pallas_call x1, Pallas kernels, body(): call(query_kernel, 'remote_q', [f32((many, HEADS, BLOCK, HD)), f32((every...  2.19 us
    pallas_call x1, Pallas kernels, body(): call(last_kernel, 'last_kv', [bf16((tokens, width))] * 2, [SMEM] + [VMEM]...  1.79 us
    all_to_all x1, waiting for transfers between devices, body(): parts = lax.all_to_all(partial, axes, 0, 0, tiled=True)  1.64 us
    pallas_call x1, Pallas kernels, body(): call(pack_kernel, 'pack', [bf16((HEADS, 2 * BLOCK + (PARTS + EARLY) * (le...  1.44 us
  transfers between devices with their start and end apart: 9, of which 3 were waited for; matrix products, arithmetic and copies ran while one was open for 0% of the time, Pallas kernels for 20%

profile of v7, /device:TPU:1, one launch (start us, length us, event | category | flops | bytes accessed | tf_op | source)
XLA Modules:
  0.0 38.4 jit_solution(16243068928635170314)
XLA Ops:
  0.7 1.4 %pack.1 = (bf16[2,256,128]{2,1,0:T(8,128)(2,1)S(1)}, bf16[2,256,128]{2,1,0:T(8,128)(2,1)S(1)}, bf16[2,256,128]{2,1,0:T(8,128)(2,1)S(1)}, bf16[2,288,128]{2,1,0:T...) custom-call(s32[2,5]{1,0:T(2,128)} %offsets_in.1, ...), custom_call_target="tpu_custom_call" | custom-call | tf_op jit(solution)/shard_map/pack/pallas_call | solution.py:237
  2.1 4.5 %collective-permute-start = (bf16[2,288,128]{2,1,0:T(8,128)(2,1)S(1)}, bf16[2,288,128]{2,1,0:T(8,128)(2,1)S(1)}, u32[]{:S(2)}, u32[]{:S(2)}) collective-permute-start(bf16[2,288,128]{2,1,0:T(8,128)(2,1)S(1)} %get-tuple-element.40), channel_id=1, source_target_pairs={{0,8},{1,9},{2,10},{3,11},{4,12},{5,13},{6,14},{7,15},{8,0},{9,1},... | collective-permute-start | bytes 442376 | tf_op jit(solution)/shard_map/ppermute | solution.py:224
  6.6 1.2 %collective-permute-start.1 = (bf16[2,256,128]{2,1,0:T(8,128)(2,1)S(1)}, bf16[2,256,128]{2,1,0:T(8,128)(2,1)S(1)}, u32[]{:S(2)}, u32[]{:S(2)}) collective-permute-start(bf16[2,256,128]{2,1,0:T(8,128)(2,1)S(1)} %get-tuple-element.41), channel_id=1, source_target_pairs={{0,1},{1,0},{2,3},{3,2},{4,5},{5,4},{6,7},{7,6},{8,9},{9,8},{10,11... | collective-permute-start | bytes 393224 | tf_op jit(solution)/shard_map/ppermute | solution.py:224
  7.8 2.5 %collective-permute-start.2 = (bf16[2,256,128]{2,1,0:T(8,128)(2,1)S(1)}, bf16[2,256,128]{2,1,0:T(8,128)(2,1)S(1)}, u32[]{:S(2)}, u32[]{:S(2)}) collective-permute-start(bf16[2,256,128]{2,1,0:T(8,128)(2,1)S(1)} %get-tuple-element.42), channel_id=1, source_target_pairs={{0,2},{1,3},{2,0},{3,1},{4,6},{5,7},{6,4},{7,5},{8,10},{9,11},{10,... | collective-permute-start | bytes 393224 | tf_op jit(solution)/shard_map/ppermute | solution.py:224
  10.3 0.7 %collective-permute-start.3 = (bf16[2,256,128]{2,1,0:T(8,128)(2,1)S(1)}, bf16[2,256,128]{2,1,0:T(8,128)(2,1)S(1)}, u32[]{:S(2)}, u32[]{:S(2)}) collective-permute-start(bf16[2,256,128]{2,1,0:T(8,128)(2,1)S(1)} %get-tuple-element.43), channel_id=1, source_target_pairs={{0,4},{1,5},{2,6},{3,7},{4,0},{5,1},{6,2},{7,3},{8,12},{9,13},{10,... | collective-permute-start | bytes 393224 | tf_op jit(solution)/shard_map/ppermute | solution.py:224
  11.0 1.1 %local_q.1 = (f32[256,256]{1,0:T(8,128)S(1)}, f32[2,256,128]{2,1,0:T(8,128)S(1)}, bf16[256,256]{1,0:T(8,128)(2,1)S(1)}, f32[1,256]{1,0:T(1,128)S(1)}, bf16[2,272...) custom-call(s32[2,5]{1,0:T(2,128)S(1)} %get-tuple-element.30.offsets, ...), custom_call_target="tpu_custom_call", output_to_operand_aliasing={{4}: (7, {}), {5}: (8, {}), {6}: (9, {})} | custom-call | tf_op jit(solution)/shard_map/local_q/pallas_call | solution.py:250
  12.2 0.1 collective-permute-start.4
  12.3 0.0 collective-permute-done.1.r2
  12.3 1.4 %collective-permute-start.5 = (bf16[2,272,128]{2,1,0:T(8,128)(2,1)S(1)}, bf16[2,272,128]{2,1,0:T(8,128)(2,1)S(1)}, u32[]{:S(2)}, u32[]{:S(2)}) collective-permute-start(bf16[2,272,128]{2,1,0:T(8,128)(2,1)S(1)} %get-tuple-element.47), channel_id=1, source_target_pairs={{0,2},{1,3},{2,0},{3,1},{4,6},{5,7},{6,4},{7,5},{8,10},{9,11},{10,... | collective-permute-start | bytes 417800 | tf_op jit(solution)/shard_map/ppermute | solution.py:224
  13.6 1.7 %collective-permute-done.2.r3 = bf16[2,256,128]{2,1,0:T(8,128)(2,1)S(1)} collective-permute-done((bf16[2,256,128]{2,1,0:T(8,128)(2,1)S(1)}, bf16[2,256,128]{2,1,0:T(8,128)(2,1)S(1)}, u32[]{:S(2)}, u32[]{:S(2)}) %collective-permute-start.2) | collective-permute-done | bytes 131104 | tf_op jit(solution)/shard_map/ppermute | solution.py:224
  15.4 0.7 %collective-permute-start.6 = (bf16[2,272,128]{2,1,0:T(8,128)(2,1)S(1)}, bf16[2,272,128]{2,1,0:T(8,128)(2,1)S(1)}, u32[]{:S(2)}, u32[]{:S(2)}) collective-permute-start(bf16[2,272,128]{2,1,0:T(8,128)(2,1)S(1)} %get-tuple-element.48), channel_id=1, source_target_pairs={{0,4},{1,5},{2,6},{3,7},{4,0},{5,1},{6,2},{7,3},{8,12},{9,13},{10,... | collective-permute-start | bytes 417800 | tf_op jit(solution)/shard_map/ppermute | solution.py:224
  16.1 0.0 collective-permute-done.3.r4
  16.1 0.0 collective-permute-done.r1.first
  16.1 2.2 %remote_q.1 = (f32[4,2,128,128]{3,2,1,0:T(8,128)S(1)}, f32[128,1,256]{2,1,0:T(1,128)}, bf16[2,240,128]{2,1,0:T(8,128)(2,1)S(1)}) custom-call(s32[2,5]{1,0:T(2,128)S(1)} %get-tuple-element.30.offsets, bf16[256,256]{1,0:T(8,128)(2,1)S(1)} %get-tuple-element.36.scaled, bf16[256,256]{1,0:T(8,128)(2,1)S(1)} %bitcast.23, ...), custom_call_target="tpu_custom_call", output_to_operand_aliasing={{2}: (10, {})} | custom-call | tf_op jit(solution)/shard_map/remote_q/pallas_call | solution.py:263
  18.3 9.2 %all-to-all-start = ((f32[128,1,256]{2,1,0:T(1,128)}), f32[128,1,256]{2,1,0:T(1,128)S(1)}, u32[]{:S(2)}, u32[]{:S(2)}) async-start(f32[128,1,256]{2,1,0:T(1,128)} %get-tuple-element.55), calls=%async_computation | async-start | bytes 262144 | tf_op jit(solution)/shard_map/all_to_all | solution.py:273
  27.5 3.4 %collective-permute-start.7 = (bf16[2,240,128]{2,1,0:T(8,128)(2,1)S(1)}, bf16[2,240,128]{2,1,0:T(8,128)(2,1)S(1)}, u32[]{:S(2)}, u32[]{:S(2)}) collective-permute-start(bf16[2,240,128]{2,1,0:T(8,128)(2,1)S(1)} %get-tuple-element.52), channel_id=1, source_target_pairs={{0,8},{1,9},{2,10},{3,11},{4,12},{5,13},{6,14},{7,15},{8,0},{9,1},... | collective-permute-start | bytes 368648 | tf_op jit(solution)/shard_map/ppermute | solution.py:224
  30.9 0.0 collective-permute-done.4.r1
  30.9 0.0 collective-permute-done.5.r2
  30.9 0.0 collective-permute-done.6.r3
  30.9 2.4 %most_kv.1 = (bf16[256,256]{1,0:T(8,128)(2,1)}, f32[256,256]{1,0:T(8,128)S(1)}, f32[256,256]{1,0:T(8,128)S(1)}) custom-call(s32[2,5]{1,0:T(2,128)S(1)} %get-tuple-element.30.offsets, f32[1,256]{1,0:T(1,128)S(1)} %get-tuple-element.31.gain, bf16[256,256]{1,0:T(8,128)(2,1)S(1)} %get-tuple-element.36.scaled, bf16[256,256]{1,0:T(8,128)(2,1)S(1)} %bitcast.15, ...), custom_call_target="tpu_custom_call" | custom-call | tf_op jit(solution)/shard_map/most_kv/pallas_call | solution.py:275
  33.3 1.0 %collective-permute-done.7.got = bf16[2,240,128]{2,1,0:T(8,128)(2,1)S(1)} collective-permute-done((bf16[2,240,128]{2,1,0:T(8,128)(2,1)S(1)}, bf16[2,240,128]{2,1,0:T(8,128)(2,1)S(1)}, u32[]{:S(2)}, u32[]{:S(2)}) %collective-permute-start.7) | collective-permute-done | bytes 122912 | tf_op jit(solution)/shard_map/ppermute | solution.py:224
  34.3 1.8 %last_kv.1 = (bf16[256,256]{1,0:T(8,128)(2,1)}, bf16[256,256]{1,0:T(8,128)(2,1)}) custom-call(s32[2,5]{1,0:T(2,128)S(1)} %get-tuple-element.30.offsets, f32[1,256]{1,0:T(1,128)S(1)} %get-tuple-element.31.gain, bf16[256,256]{1,0:T(8,128)(2,1)S(1)} %bitcast.16, bf16[256,256]{1,0:T(8,128)(2,1)S(1)} %bitcast.20, f32[256,256]{1,0:T(8,128)S(1)} %get-tuple-element.50.dk_in, ...), custom_call_target="tpu_custom_call" | custom-call | tf_op jit(solution)/shard_map/last_kv/pallas_call | solution.py:282
  36.1 1.6 %all-to-all-done = f32[128,1,256]{2,1,0:T(1,128)S(1)} async-done(((f32[128,1,256]{2,1,0:T(1,128)}), f32[128,1,256]{2,1,0:T(1,128)S(1)}, u32[]{:S(2)}, u32[]{:S(2)}) %all-to-all-start) | async-done | bytes 131104 | tf_op jit(solution)/shard_map/all_to_all | solution.py:273
  37.7 0.7 %reduce_sum.9 = f32[256]{0:T(256)} reduce(f32[128,1,256]{2,1,0:T(1,128)S(1)} %all-to-all-done, f32[]{:T(128)} %constant.0.clone.1), dimensions={0,1}, to_apply=%region_0.0 | reduce | flops 32512 | bytes 132100 | tf_op jit(solution)/shard_map/reduce_sum | solution.py:285
  (8 shorter events, 0.0 us)
Async XLA Ops:
  0.6 10.4 %copy-start = (bf16[1,256,256]{2,1,0:T(8,128)(2,1)S(1)}, bf16[1,256,256]{2,1,0:T(8,128)(2,1)}, u32[]{:S(2)}) copy-start(bf16[1,256,256]{2,1,0:T(8,128)(2,1)} %param.10) | copy-start | bytes 393220
  0.6 10.4 %copy-start.1 = (bf16[1,256,256]{2,1,0:T(8,128)(2,1)S(1)}, bf16[1,256,256]{2,1,0:T(8,128)(2,1)}, u32[]{:S(2)}) copy-start(bf16[1,256,256]{2,1,0:T(8,128)(2,1)} %param.8) | copy-start | bytes 393220
  0.7 10.4 %copy-start.2 = (bf16[1,256,256]{2,1,0:T(8,128)(2,1)S(1)}, bf16[1,256,256]{2,1,0:T(8,128)(2,1)}, u32[]{:S(2)}) copy-start(bf16[1,256,256]{2,1,0:T(8,128)(2,1)} %param.9) | copy-start | bytes 393220
  0.7 10.4 %copy-start.3 = (bf16[1,256,256]{2,1,0:T(8,128)(2,1)S(1)}, bf16[1,256,256]{2,1,0:T(8,128)(2,1)}, u32[]{:S(2)}) copy-start(bf16[1,256,256]{2,1,0:T(8,128)(2,1)} %param.7) | copy-start | bytes 393220
  2.1 14.0 %collective-permute-start = (bf16[2,288,128]{2,1,0:T(8,128)(2,1)S(1)}, bf16[2,288,128]{2,1,0:T(8,128)(2,1)S(1)}, u32[]{:S(2)}, u32[]{:S(2)}) collective-permute-start(bf16[2,288,128]{2,1,0:T(8,128)(2,1)S(1)} %get-tuple-element.40), channel_id=1, source_target_pairs={{0,8},{1,9},{2,10},{3,11},{4,12},{5,13},{6,14},{7,15},{8,0},{9,1},... | collective-permute-start | bytes 442376 | tf_op jit(solution)/shard_map/ppermute | solution.py:224
  6.6 5.6 %collective-permute-start.1 = (bf16[2,256,128]{2,1,0:T(8,128)(2,1)S(1)}, bf16[2,256,128]{2,1,0:T(8,128)(2,1)S(1)}, u32[]{:S(2)}, u32[]{:S(2)}) collective-permute-start(bf16[2,256,128]{2,1,0:T(8,128)(2,1)S(1)} %get-tuple-element.41), channel_id=1, source_target_pairs={{0,1},{1,0},{2,3},{3,2},{4,5},{5,4},{6,7},{7,6},{8,9},{9,8},{10,11... | collective-permute-start | bytes 393224 | tf_op jit(solution)/shard_map/ppermute | solution.py:224
  7.8 7.5 %collective-permute-start.2 = (bf16[2,256,128]{2,1,0:T(8,128)(2,1)S(1)}, bf16[2,256,128]{2,1,0:T(8,128)(2,1)S(1)}, u32[]{:S(2)}, u32[]{:S(2)}) collective-permute-start(bf16[2,256,128]{2,1,0:T(8,128)(2,1)S(1)} %get-tuple-element.42), channel_id=1, source_target_pairs={{0,2},{1,3},{2,0},{3,1},{4,6},{5,7},{6,4},{7,5},{8,10},{9,11},{10,... | collective-permute-start | bytes 393224 | tf_op jit(solution)/shard_map/ppermute | solution.py:224
  10.3 5.8 %collective-permute-start.3 = (bf16[2,256,128]{2,1,0:T(8,128)(2,1)S(1)}, bf16[2,256,128]{2,1,0:T(8,128)(2,1)S(1)}, u32[]{:S(2)}, u32[]{:S(2)}) collective-permute-start(bf16[2,256,128]{2,1,0:T(8,128)(2,1)S(1)} %get-tuple-element.43), channel_id=1, source_target_pairs={{0,4},{1,5},{2,6},{3,7},{4,0},{5,1},{6,2},{7,3},{8,12},{9,13},{10,... | collective-permute-start | bytes 393224 | tf_op jit(solution)/shard_map/ppermute | solution.py:224
  12.2 18.7 %collective-permute-start.4 = (bf16[2,272,128]{2,1,0:T(8,128)(2,1)S(1)}, bf16[2,272,128]{2,1,0:T(8,128)(2,1)S(1)}, u32[]{:S(2)}, u32[]{:S(2)}) collective-permute-start(bf16[2,272,128]{2,1,0:T(8,128)(2,1)S(1)} %get-tuple-element.46), channel_id=1, source_target_pairs={{0,1},{1,0},{2,3},{3,2},{4,5},{5,4},{6,7},{7,6},{8,9},{9,8},{10,11... | collective-permute-start | bytes 417800 | tf_op jit(solution)/shard_map/ppermute | solution.py:224
  12.3 18.6 %collective-permute-start.5 = (bf16[2,272,128]{2,1,0:T(8,128)(2,1)S(1)}, bf16[2,272,128]{2,1,0:T(8,128)(2,1)S(1)}, u32[]{:S(2)}, u32[]{:S(2)}) collective-permute-start(bf16[2,272,128]{2,1,0:T(8,128)(2,1)S(1)} %get-tuple-element.47), channel_id=1, source_target_pairs={{0,2},{1,3},{2,0},{3,1},{4,6},{5,7},{6,4},{7,5},{8,10},{9,11},{10,... | collective-permute-start | bytes 417800 | tf_op jit(solution)/shard_map/ppermute | solution.py:224
  15.4 15.5 %collective-permute-start.6 = (bf16[2,272,128]{2,1,0:T(8,128)(2,1)S(1)}, bf16[2,272,128]{2,1,0:T(8,128)(2,1)S(1)}, u32[]{:S(2)}, u32[]{:S(2)}) collective-permute-start(bf16[2,272,128]{2,1,0:T(8,128)(2,1)S(1)} %get-tuple-element.48), channel_id=1, source_target_pairs={{0,4},{1,5},{2,6},{3,7},{4,0},{5,1},{6,2},{7,3},{8,12},{9,13},{10,... | collective-permute-start | bytes 417800 | tf_op jit(solution)/shard_map/ppermute | solution.py:224
  18.3 19.4 %all-to-all-start = ((f32[128,1,256]{2,1,0:T(1,128)}), f32[128,1,256]{2,1,0:T(1,128)S(1)}, u32[]{:S(2)}, u32[]{:S(2)}) async-start(f32[128,1,256]{2,1,0:T(1,128)} %get-tuple-element.55), calls=%async_computation | async-start | bytes 262144 | tf_op jit(solution)/shard_map/all_to_all | solution.py:273
  27.5 6.8 %collective-permute-start.7 = (bf16[2,240,128]{2,1,0:T(8,128)(2,1)S(1)}, bf16[2,240,128]{2,1,0:T(8,128)(2,1)S(1)}, u32[]{:S(2)}, u32[]{:S(2)}) collective-permute-start(bf16[2,240,128]{2,1,0:T(8,128)(2,1)S(1)} %get-tuple-element.52), channel_id=1, source_target_pairs={{0,8},{1,9},{2,10},{3,11},{4,12},{5,13},{6,14},{7,15},{8,0},{9,1},... | collective-permute-start | bytes 368648 | tf_op jit(solution)/shard_map/ppermute | solution.py:224

commit v8 on v7

--- a/solution.py
+++ b/solution.py
@@ -18,8 +18,8 @@
 ANY = pl.BlockSpec(memory_space=pl.ANY)
 VMEM = pl.BlockSpec(memory_space=pltpu.VMEM)
 SMEM = pl.BlockSpec(memory_space=pltpu.SMEM)
-ORDER = (4, 1, 2, 3)
-SOON = tuple(level for level in ORDER if level not in LATE)
+ORDER = (4,1,2,3)
+SOON = (3,2,1,)
 NT = (((1,), (1,)), ((), ()))
 TN = (((0,), (0,)), ((), ()))
 NN = (((1,), (0,)), ((), ()))
@@ -166,8 +166,8 @@
         dv[at, c] += jnp.where(active, dot(probs.astype(jnp.bfloat16), dout, NN), 0.0)
 
 
-def most_kernel(offsets, gain, scaled, k, v, d, norm, dq_in, added, r1, r2, r3, grad_q, dk, dv, dq):
-    received = dict(zip(SOON, (r1, r2, r3)))
+def most_kernel(offsets, gain, scaled, k, v, d, norm, dq_in, added, *refs):
+    received, (grad_q, dk, dv, dq) = dict(zip(SOON, refs)), refs[len(SOON) :]
     for head in range(HEADS):
         c = cols(head)
         count = block_counts(offsets, head)
@@ -192,10 +192,14 @@
     )
 
 
-def last_kernel(offsets, gain, k, v, dk_in, dv_in, got, first, grad_k, grad_v, dk, dv):
+def last_kernel(offsets, gain, k, v, dk_in, dv_in, *refs):
+    got, first = dict(zip(LATE, refs)), dict(zip(LATE, refs[len(LATE) :]))
+    grad_k, grad_v, dk, dv = refs[2 * len(LATE) :]
     dk[...] = dk_in[...]
     dv[...] = dv_in[...]
-    for_each_level(offsets, LATE, lambda level, spots: add_keys(level, spots, got, first, gain, k, v, dk, dv))
+    for_each_level(
+        offsets, LATE, lambda level, spots: add_keys(level, spots, got[level], first[level], gain, k, v, dk, dv)
+    )
     grad_k[...] = (dk[...] * SCALE).astype(jnp.bfloat16)
     grad_v[...] = dv[...].astype(jnp.bfloat16)
 
@@ -246,7 +250,7 @@
     offsets = table
     second = dict(zip(range(1, LEVELS), sent[many:]))
     got_kv = swap({level: sent[level - 1] for level in ORDER})
-    early = {level: second[level] for level in ORDER if level not in LATE}
+    early = {level: second[level] for level in SOON}
     dq, norm_cols, scaled, partial, *passed = call(
         local_q_kernel,
         "local_q",
@@ -276,12 +280,12 @@
         most_kernel,
         "most_kv",
         [bf16((tokens, width)), f32((tokens, width)), f32((tokens, width))],
-        [SMEM] + [VMEM] * 11,
+        [SMEM] + [VMEM] * (8 + len(SOON)),
         [acc],
     )(offsets, gain, scaled, k, v, d, norm, dq, added, *(got_qd[level] for level in SOON))
     grad_k, grad_v = call(
-        last_kernel, "last_kv", [bf16((tokens, width))] * 2, [SMEM] + [VMEM] * 7, [acc, acc]
-    )(offsets, gain, k, v, dk, dv, got_qd[LATE[0]], got_kv[LATE[0]])
+        last_kernel, "last_kv", [bf16((tokens, width))] * 2, [SMEM] + [VMEM] * (5 + 2 * len(LATE)), [acc, acc]
+    )(offsets, gain, k, v, dk, dv, *(got_qd[level] for level in LATE), *(got_kv[level] for level in LATE))
     return (grad_q[None], grad_k[None], grad_v[None], jnp.sum(parts, axis=(0, 1)))
 
 

time: 38.6 us -> 37.2 us (0.964)
  starting transfers between devices: 23.6 us -> 21.6 us
  Pallas kernels: 8.98 us -> 9.72 us
    all_to_all x1, starting transfers between devices: 9.18 us -> 8.05 us  [body(): parts = lax.all_to_all(partial, axes, 0, 0, tiled=True)]
    ppermute x8, starting transfers between devices: 14.4 us -> 13.6 us  [swap(): lax.ppermute(payload, 'ctx', [(i, i ^ half) for i in range(count)])]
    pallas_call x1, Pallas kernels: 2.42 us -> 3.21 us  [body(): call(most_kernel, 'most_kv', [bf16((tokens, width)), f32((tokens, width))...]
    ppermute x8, waiting for transfers between devices: 2.73 us -> 2.07 us  [swap(): lax.ppermute(payload, 'ctx', [(i, i ^ half) for i in range(count)])]
    pallas_call x1, Pallas kernels: 1.79 us -> 1.3 us  [body(): call(last_kernel, 'last_kv', [bf16((tokens, width))] * 2, [SMEM] + [VMEM]...]
    all_to_all x1, waiting for transfers between devices: 1.64 us -> 2.13 us  [body(): parts = lax.all_to_all(partial, axes, 0, 0, tiled=True)]
    pallas_call x1, Pallas kernels: 2.19 us -> 2.63 us  [body(): call(query_kernel, 'remote_q', [f32((many, HEADS, BLOCK, HD)), f32((every...]
  transfers between devices with their start and end apart: 9 -> 9, of which waited for: 3 -> 3; matrix products, arithmetic and copies ran while one was open for 0% -> 0% of each run, Pallas kernels for 20% -> 22%
where the time goes in v8:
time: 37.2 us; the launch traced here: 37 us
  starting transfers between devices  21.6 us (58%)
  Pallas kernels  9.72 us (26%)
  waiting for transfers between devices  4.2 us (11%)
  other arithmetic  0.71 us (2%)
  between operations  0.7 us (2%)
    ppermute x8, starting transfers between devices, swap(): lax.ppermute(payload, 'ctx', [(i, i ^ half) for i in range(count)])  13.6 us
    all_to_all x1, starting transfers between devices, body(): parts = lax.all_to_all(partial, axes, 0, 0, tiled=True)  8.05 us
    pallas_call x1, Pallas kernels, body(): call(most_kernel, 'most_kv', [bf16((tokens, width)), f32((tokens, width))...  3.21 us
    pallas_call x1, Pallas kernels, body(): call(query_kernel, 'remote_q', [f32((many, HEADS, BLOCK, HD)), f32((every...  2.63 us
    all_to_all x1, waiting for transfers between devices, body(): parts = lax.all_to_all(partial, axes, 0, 0, tiled=True)  2.13 us
    ppermute x8, waiting for transfers between devices, swap(): lax.ppermute(payload, 'ctx', [(i, i ^ half) for i in range(count)])  2.07 us
    pallas_call x1, Pallas kernels, body(): call(pack_kernel, 'pack', [bf16((HEADS, 2 * BLOCK + (PARTS + EARLY) * (le...  1.44 us
    pallas_call x1, Pallas kernels, body(): call(last_kernel, 'last_kv', [bf16((tokens, width))] * 2, [SMEM] + [VMEM]...  1.3 us
  transfers between devices with their start and end apart: 9, of which 3 were waited for; matrix products, arithmetic and copies ran while one was open for 0% of the time, Pallas kernels for 22%

profile of v8, /device:TPU:1, one launch (start us, length us, event | category | flops | bytes accessed | tf_op | source)
XLA Modules:
  0.0 37.0 jit_solution(1241307796200079630)
XLA Ops:
  0.7 1.4 %pack.1 = (bf16[2,256,128]{2,1,0:T(8,128)(2,1)S(1)}, bf16[2,256,128]{2,1,0:T(8,128)(2,1)S(1)}, bf16[2,256,128]{2,1,0:T(8,128)(2,1)S(1)}, bf16[2,288,128]{2,1,0:T...) custom-call(s32[2,5]{1,0:T(2,128)} %offsets_in.1, ...), custom_call_target="tpu_custom_call" | custom-call | tf_op jit(solution)/shard_map/pack/pallas_call | solution.py:241
  2.1 4.5 %collective-permute-start = (bf16[2,288,128]{2,1,0:T(8,128)(2,1)S(1)}, bf16[2,288,128]{2,1,0:T(8,128)(2,1)S(1)}, u32[]{:S(2)}, u32[]{:S(2)}) collective-permute-start(bf16[2,288,128]{2,1,0:T(8,128)(2,1)S(1)} %get-tuple-element.40), channel_id=1, source_target_pairs={{0,8},{1,9},{2,10},{3,11},{4,12},{5,13},{6,14},{7,15},{8,0},{9,1},... | collective-permute-start | bytes 442376 | tf_op jit(solution)/shard_map/ppermute | solution.py:228
  6.6 1.2 %collective-permute-start.1 = (bf16[2,256,128]{2,1,0:T(8,128)(2,1)S(1)}, bf16[2,256,128]{2,1,0:T(8,128)(2,1)S(1)}, u32[]{:S(2)}, u32[]{:S(2)}) collective-permute-start(bf16[2,256,128]{2,1,0:T(8,128)(2,1)S(1)} %get-tuple-element.41), channel_id=1, source_target_pairs={{0,1},{1,0},{2,3},{3,2},{4,5},{5,4},{6,7},{7,6},{8,9},{9,8},{10,11... | collective-permute-start | bytes 393224 | tf_op jit(solution)/shard_map/ppermute | solution.py:228
  7.8 2.5 %collective-permute-start.2 = (bf16[2,256,128]{2,1,0:T(8,128)(2,1)S(1)}, bf16[2,256,128]{2,1,0:T(8,128)(2,1)S(1)}, u32[]{:S(2)}, u32[]{:S(2)}) collective-permute-start(bf16[2,256,128]{2,1,0:T(8,128)(2,1)S(1)} %get-tuple-element.42), channel_id=1, source_target_pairs={{0,2},{1,3},{2,0},{3,1},{4,6},{5,7},{6,4},{7,5},{8,10},{9,11},{10,... | collective-permute-start | bytes 393224 | tf_op jit(solution)/shard_map/ppermute | solution.py:228
  10.3 0.7 %collective-permute-start.3 = (bf16[2,256,128]{2,1,0:T(8,128)(2,1)S(1)}, bf16[2,256,128]{2,1,0:T(8,128)(2,1)S(1)}, u32[]{:S(2)}, u32[]{:S(2)}) collective-permute-start(bf16[2,256,128]{2,1,0:T(8,128)(2,1)S(1)} %get-tuple-element.43), channel_id=1, source_target_pairs={{0,4},{1,5},{2,6},{3,7},{4,0},{5,1},{6,2},{7,3},{8,12},{9,13},{10,... | collective-permute-start | bytes 393224 | tf_op jit(solution)/shard_map/ppermute | solution.py:228
  11.0 1.1 %local_q.1 = (f32[256,256]{1,0:T(8,128)S(1)}, f32[2,256,128]{2,1,0:T(8,128)S(1)}, bf16[256,256]{1,0:T(8,128)(2,1)S(1)}, f32[1,256]{1,0:T(1,128)S(1)}, bf16[2,272...) custom-call(s32[2,5]{1,0:T(2,128)S(1)} %get-tuple-element.30.offsets, ...), custom_call_target="tpu_custom_call", output_to_operand_aliasing={{4}: (7, {}), {5}: (8, {}), {6}: (9, {})} | custom-call | tf_op jit(solution)/shard_map/local_q/pallas_call | solution.py:254
  12.2 0.8 %collective-permute-start.4 = (bf16[2,272,128]{2,1,0:T(8,128)(2,1)S(1)}, bf16[2,272,128]{2,1,0:T(8,128)(2,1)S(1)}, u32[]{:S(2)}, u32[]{:S(2)}) collective-permute-start(bf16[2,272,128]{2,1,0:T(8,128)(2,1)S(1)} %get-tuple-element.46), channel_id=1, source_target_pairs={{0,4},{1,5},{2,6},{3,7},{4,0},{5,1},{6,2},{7,3},{8,12},{9,13},{10,... | collective-permute-start | bytes 417800 | tf_op jit(solution)/shard_map/ppermute | solution.py:228
  13.0 0.0 collective-permute-done.1.r2
  13.0 0.5 %collective-permute-start.5 = (bf16[2,272,128]{2,1,0:T(8,128)(2,1)S(1)}, bf16[2,272,128]{2,1,0:T(8,128)(2,1)S(1)}, u32[]{:S(2)}, u32[]{:S(2)}) collective-permute-start(bf16[2,272,128]{2,1,0:T(8,128)(2,1)S(1)} %get-tuple-element.47), channel_id=1, source_target_pairs={{0,2},{1,3},{2,0},{3,1},{4,6},{5,7},{6,4},{7,5},{8,10},{9,11},{10,... | collective-permute-start | bytes 417800 | tf_op jit(solution)/shard_map/ppermute | solution.py:228
  13.5 1.9 %collective-permute-done.2.r3 = bf16[2,256,128]{2,1,0:T(8,128)(2,1)S(1)} collective-permute-done((bf16[2,256,128]{2,1,0:T(8,128)(2,1)S(1)}, bf16[2,256,128]{2,1,0:T(8,128)(2,1)S(1)}, u32[]{:S(2)}, u32[]{:S(2)}) %collective-permute-start.2) | collective-permute-done | bytes 131104 | tf_op jit(solution)/shard_map/ppermute | solution.py:228
  15.4 0.0 collective-permute-start.6
  15.4 0.0 collective-permute-done.3.r4
  15.4 0.0 collective-permute-done.r1.refs_1_
  15.4 2.6 %remote_q.1 = (f32[4,2,128,128]{3,2,1,0:T(8,128)S(1)}, f32[128,1,256]{2,1,0:T(1,128)}, bf16[2,240,128]{2,1,0:T(8,128)(2,1)S(1)}) custom-call(s32[2,5]{1,0:T(2,128)S(1)} %get-tuple-element.30.offsets, bf16[256,256]{1,0:T(8,128)(2,1)S(1)} %get-tuple-element.36.scaled, bf16[256,256]{1,0:T(8,128)(2,1)S(1)} %bitcast.23, ...), custom_call_target="tpu_custom_call", output_to_operand_aliasing={{2}: (10, {})} | custom-call | tf_op jit(solution)/shard_map/remote_q/pallas_call | solution.py:267
  18.0 8.1 %all-to-all-start = ((f32[128,1,256]{2,1,0:T(1,128)}), f32[128,1,256]{2,1,0:T(1,128)S(1)}, u32[]{:S(2)}, u32[]{:S(2)}) async-start(f32[128,1,256]{2,1,0:T(1,128)} %get-tuple-element.55), calls=%async_computation | async-start | bytes 262144 | tf_op jit(solution)/shard_map/all_to_all | solution.py:277
  26.1 3.4 %collective-permute-start.7 = (bf16[2,240,128]{2,1,0:T(8,128)(2,1)S(1)}, bf16[2,240,128]{2,1,0:T(8,128)(2,1)S(1)}, u32[]{:S(2)}, u32[]{:S(2)}) collective-permute-start(bf16[2,240,128]{2,1,0:T(8,128)(2,1)S(1)} %get-tuple-element.52), channel_id=1, source_target_pairs={{0,8},{1,9},{2,10},{3,11},{4,12},{5,13},{6,14},{7,15},{8,0},{9,1},... | collective-permute-start | bytes 368648 | tf_op jit(solution)/shard_map/ppermute | solution.py:228
  29.4 0.0 collective-permute-done.4.refs_0_
  29.4 0.0 collective-permute-done.5.refs_1_
  29.5 0.0 collective-permute-done.6.refs_2_
  29.5 3.2 %most_kv.1 = (bf16[256,256]{1,0:T(8,128)(2,1)}, f32[256,256]{1,0:T(8,128)S(1)}, f32[256,256]{1,0:T(8,128)S(1)}) custom-call(s32[2,5]{1,0:T(2,128)S(1)} %get-tuple-element.30.offsets, f32[1,256]{1,0:T(1,128)S(1)} %get-tuple-element.31.gain, bf16[256,256]{1,0:T(8,128)(2,1)S(1)} %get-tuple-element.36.scaled, bf16[256,256]{1,0:T(8,128)(2,1)S(1)} %bitcast.15, ...), custom_call_target="tpu_custom_call" | custom-call | tf_op jit(solution)/shard_map/most_kv/pallas_call | solution.py:279
  32.7 0.2 collective-permute-done.7.refs_0_
  32.9 1.3 %last_kv.1 = (bf16[256,256]{1,0:T(8,128)(2,1)}, bf16[256,256]{1,0:T(8,128)(2,1)}) custom-call(s32[2,5]{1,0:T(2,128)S(1)} %get-tuple-element.30.offsets, f32[1,256]{1,0:T(1,128)S(1)} %get-tuple-element.31.gain, bf16[256,256]{1,0:T(8,128)(2,1)S(1)} %bitcast.16, bf16[256,256]{1,0:T(8,128)(2,1)S(1)} %bitcast.20, f32[256,256]{1,0:T(8,128)S(1)} %get-tuple-element.50.dk_in, ...), custom_call_target="tpu_custom_call" | custom-call | tf_op jit(solution)/shard_map/last_kv/pallas_call | solution.py:286
  34.2 2.1 %all-to-all-done = f32[128,1,256]{2,1,0:T(1,128)S(1)} async-done(((f32[128,1,256]{2,1,0:T(1,128)}), f32[128,1,256]{2,1,0:T(1,128)S(1)}, u32[]{:S(2)}, u32[]{:S(2)}) %all-to-all-start) | async-done | bytes 131104 | tf_op jit(solution)/shard_map/all_to_all | solution.py:277
  36.3 0.7 %reduce_sum.9 = f32[256]{0:T(256)} reduce(f32[128,1,256]{2,1,0:T(1,128)S(1)} %all-to-all-done, f32[]{:T(128)} %constant.0.clone.1), dimensions={0,1}, to_apply=%region_0.0 | reduce | flops 32512 | bytes 132100 | tf_op jit(solution)/shard_map/reduce_sum | solution.py:289
  (8 shorter events, 0.0 us)
Async XLA Ops:
  0.6 10.4 %copy-start = (bf16[1,256,256]{2,1,0:T(8,128)(2,1)S(1)}, bf16[1,256,256]{2,1,0:T(8,128)(2,1)}, u32[]{:S(2)}) copy-start(bf16[1,256,256]{2,1,0:T(8,128)(2,1)} %param.10) | copy-start | bytes 393220
  0.6 10.4 %copy-start.1 = (bf16[1,256,256]{2,1,0:T(8,128)(2,1)S(1)}, bf16[1,256,256]{2,1,0:T(8,128)(2,1)}, u32[]{:S(2)}) copy-start(bf16[1,256,256]{2,1,0:T(8,128)(2,1)} %param.8) | copy-start | bytes 393220
  0.7 10.4 %copy-start.2 = (bf16[1,256,256]{2,1,0:T(8,128)(2,1)S(1)}, bf16[1,256,256]{2,1,0:T(8,128)(2,1)}, u32[]{:S(2)}) copy-start(bf16[1,256,256]{2,1,0:T(8,128)(2,1)} %param.9) | copy-start | bytes 393220
  0.7 10.4 %copy-start.3 = (bf16[1,256,256]{2,1,0:T(8,128)(2,1)S(1)}, bf16[1,256,256]{2,1,0:T(8,128)(2,1)}, u32[]{:S(2)}) copy-start(bf16[1,256,256]{2,1,0:T(8,128)(2,1)} %param.7) | copy-start | bytes 393220
  2.1 13.3 %collective-permute-start = (bf16[2,288,128]{2,1,0:T(8,128)(2,1)S(1)}, bf16[2,288,128]{2,1,0:T(8,128)(2,1)S(1)}, u32[]{:S(2)}, u32[]{:S(2)}) collective-permute-start(bf16[2,288,128]{2,1,0:T(8,128)(2,1)S(1)} %get-tuple-element.40), channel_id=1, source_target_pairs={{0,8},{1,9},{2,10},{3,11},{4,12},{5,13},{6,14},{7,15},{8,0},{9,1},... | collective-permute-start | bytes 442376 | tf_op jit(solution)/shard_map/ppermute | solution.py:228
  6.6 6.4 %collective-permute-start.1 = (bf16[2,256,128]{2,1,0:T(8,128)(2,1)S(1)}, bf16[2,256,128]{2,1,0:T(8,128)(2,1)S(1)}, u32[]{:S(2)}, u32[]{:S(2)}) collective-permute-start(bf16[2,256,128]{2,1,0:T(8,128)(2,1)S(1)} %get-tuple-element.41), channel_id=1, source_target_pairs={{0,1},{1,0},{2,3},{3,2},{4,5},{5,4},{6,7},{7,6},{8,9},{9,8},{10,11... | collective-permute-start | bytes 393224 | tf_op jit(solution)/shard_map/ppermute | solution.py:228
  7.8 7.5 %collective-permute-start.2 = (bf16[2,256,128]{2,1,0:T(8,128)(2,1)S(1)}, bf16[2,256,128]{2,1,0:T(8,128)(2,1)S(1)}, u32[]{:S(2)}, u32[]{:S(2)}) collective-permute-start(bf16[2,256,128]{2,1,0:T(8,128)(2,1)S(1)} %get-tuple-element.42), channel_id=1, source_target_pairs={{0,2},{1,3},{2,0},{3,1},{4,6},{5,7},{6,4},{7,5},{8,10},{9,11},{10,... | collective-permute-start | bytes 393224 | tf_op jit(solution)/shard_map/ppermute | solution.py:228
  10.3 5.1 %collective-permute-start.3 = (bf16[2,256,128]{2,1,0:T(8,128)(2,1)S(1)}, bf16[2,256,128]{2,1,0:T(8,128)(2,1)S(1)}, u32[]{:S(2)}, u32[]{:S(2)}) collective-permute-start(bf16[2,256,128]{2,1,0:T(8,128)(2,1)S(1)} %get-tuple-element.43), channel_id=1, source_target_pairs={{0,4},{1,5},{2,6},{3,7},{4,0},{5,1},{6,2},{7,3},{8,12},{9,13},{10,... | collective-permute-start | bytes 393224 | tf_op jit(solution)/shard_map/ppermute | solution.py:228
  12.2 17.3 %collective-permute-start.4 = (bf16[2,272,128]{2,1,0:T(8,128)(2,1)S(1)}, bf16[2,272,128]{2,1,0:T(8,128)(2,1)S(1)}, u32[]{:S(2)}, u32[]{:S(2)}) collective-permute-start(bf16[2,272,128]{2,1,0:T(8,128)(2,1)S(1)} %get-tuple-element.46), channel_id=1, source_target_pairs={{0,4},{1,5},{2,6},{3,7},{4,0},{5,1},{6,2},{7,3},{8,12},{9,13},{10,... | collective-permute-start | bytes 417800 | tf_op jit(solution)/shard_map/ppermute | solution.py:228
  13.0 16.5 %collective-permute-start.5 = (bf16[2,272,128]{2,1,0:T(8,128)(2,1)S(1)}, bf16[2,272,128]{2,1,0:T(8,128)(2,1)S(1)}, u32[]{:S(2)}, u32[]{:S(2)}) collective-permute-start(bf16[2,272,128]{2,1,0:T(8,128)(2,1)S(1)} %get-tuple-element.47), channel_id=1, source_target_pairs={{0,2},{1,3},{2,0},{3,1},{4,6},{5,7},{6,4},{7,5},{8,10},{9,11},{10,... | collective-permute-start | bytes 417800 | tf_op jit(solution)/shard_map/ppermute | solution.py:228
  15.4 14.1 %collective-permute-start.6 = (bf16[2,272,128]{2,1,0:T(8,128)(2,1)S(1)}, bf16[2,272,128]{2,1,0:T(8,128)(2,1)S(1)}, u32[]{:S(2)}, u32[]{:S(2)}) collective-permute-start(bf16[2,272,128]{2,1,0:T(8,128)(2,1)S(1)} %get-tuple-element.48), channel_id=1, source_target_pairs={{0,1},{1,0},{2,3},{3,2},{4,5},{5,4},{6,7},{7,6},{8,9},{9,8},{10,11... | collective-permute-start | bytes 417800 | tf_op jit(solution)/shard_map/ppermute | solution.py:228
  18.0 18.3 %all-to-all-start = ((f32[128,1,256]{2,1,0:T(1,128)}), f32[128,1,256]{2,1,0:T(1,128)S(1)}, u32[]{:S(2)}, u32[]{:S(2)}) async-start(f32[128,1,256]{2,1,0:T(1,128)} %get-tuple-element.55), calls=%async_computation | async-start | bytes 262144 | tf_op jit(solution)/shard_map/all_to_all | solution.py:277
  26.1 6.8 %collective-permute-start.7 = (bf16[2,240,128]{2,1,0:T(8,128)(2,1)S(1)}, bf16[2,240,128]{2,1,0:T(8,128)(2,1)S(1)}, u32[]{:S(2)}, u32[]{:S(2)}) collective-permute-start(bf16[2,240,128]{2,1,0:T(8,128)(2,1)S(1)} %get-tuple-element.52), channel_id=1, source_target_pairs={{0,8},{1,9},{2,10},{3,11},{4,12},{5,13},{6,14},{7,15},{8,0},{9,1},... | collective-permute-start | bytes 368648 | tf_op jit(solution)/shard_map/ppermute | solution.py:228

commit v9 on v8

--- a/solution.py
+++ b/solution.py
@@ -132,19 +132,34 @@
     received = dict(zip(ORDER, (r1, r2, r3, r4)))
     total[...] = partial_in[...]
 
-    def one(level, spots):
-        got = received[level]
+    me = lax.axis_index("ctx")
+    spots = {level: [place(offsets, me, head, level) for head in range(HEADS)] for level in range(1, LEVELS)}
+
+    def any_active(level):
+        return spots[level][0][0] | spots[level][1][0]
+
+    def some(levels):
+        parts = []
+        for level in levels:
+            for head in range(HEADS):
+                got, (active, block) = received[level], spots[level][head]
+                c, at = cols(head), block_rows(block)
+                scores = dot(scaled[at, c], got[head, :BLOCK], NT)
+                parts.append((level, head, active, at, c, scores, dot(d[at, c], got[head, BLOCK : 2 * BLOCK], NT)))
+        grads = []
+        for level, head, active, at, c, scores, pull in parts:
+            probs = jnp.exp(scores * SCALE - norm_cols[head, at, :])
+            grads.append((probs * pull).astype(jnp.bfloat16))
+        mores = [dot(grad, received[p[0]][p[1], :BLOCK], NN) for grad, p in zip(grads, parts)]
+        sums = [0.0] * HEADS
+        for more, (level, head, active, at, c, _, _) in zip(mores, parts):
+            more = jnp.where(active, more, 0.0)
+            added[level - 1, head] = more
+            sums[head] = sums[head] + jnp.sum(q[at, c].astype(jnp.float32) * more, axis=0, keepdims=True)
         for head in range(HEADS):
-            active, block = spots[head]
-            c, at = cols(head), block_rows(block)
-            key, value = got[head, :BLOCK], got[head, BLOCK : 2 * BLOCK]
-            probs = jnp.exp(dot(scaled[at, c], key, NT) * SCALE - norm_cols[head, at, :])
-            grads = (probs * dot(d[at, c], value, NT)).astype(jnp.bfloat16)
-            more = jnp.where(active, dot(grads, key, NN), 0.0)
-            added[level - 1, head] = more
-            total[:, c] += jnp.sum(q[at, c].astype(jnp.float32) * more, axis=0, keepdims=True)
-
-    for_each_level(offsets, range(1, LEVELS), one)
+            total[:, cols(head)] += sums[head]
+
+    some((1, 2, 3, 4))
     partial[...] = jnp.broadcast_to((total[...] * SCALE)[None], partial.shape)
 
 

time: 37.2 us -> 36.5 us (0.981)
  Pallas kernels: 9.72 us -> 8.47 us
  waiting for transfers between devices: 4.2 us -> 4.7 us
    pallas_call x1, Pallas kernels: 2.63 us -> 1.88 us  [body(): call(query_kernel, 'remote_q', [f32((many, HEADS, BLOCK, HD)), f32((every...]
    pallas_call x1, Pallas kernels: 3.21 us -> 2.71 us  [body(): call(most_kernel, 'most_kv', [bf16((tokens, width)), f32((tokens, width))...]
    ppermute x8, waiting for transfers between devices: 2.07 us -> 2.57 us  [swap(): lax.ppermute(payload, 'ctx', [(i, i ^ half) for i in range(count)])]
  transfers between devices with their start and end apart: 9 -> 9, of which waited for: 3 -> 3; matrix products, arithmetic and copies ran while one was open for 0% -> 0% of each run, Pallas kernels for 22% -> 19%
where the time goes in v9:
time: 36.5 us; the launch traced here: 36.3 us
  starting transfers between devices  21.7 us (59%)
  Pallas kernels  8.47 us (23%)
  waiting for transfers between devices  4.7 us (13%)
  other arithmetic  0.71 us (2%)
  between operations  0.7 us (2%)
    ppermute x8, starting transfers between devices, swap(): lax.ppermute(payload, 'ctx', [(i, i ^ half) for i in range(count)])  13.6 us
    all_to_all x1, starting transfers between devices, body(): parts = lax.all_to_all(partial, axes, 0, 0, tiled=True)  8.13 us
    pallas_call x1, Pallas kernels, body(): call(most_kernel, 'most_kv', [bf16((tokens, width)), f32((tokens, width))...  2.71 us
    ppermute x8, waiting for transfers between devices, swap(): lax.ppermute(payload, 'ctx', [(i, i ^ half) for i in range(count)])  2.57 us
    all_to_all x1, waiting for transfers between devices, body(): parts = lax.all_to_all(partial, axes, 0, 0, tiled=True)  2.13 us
    pallas_call x1, Pallas kernels, body(): call(query_kernel, 'remote_q', [f32((many, HEADS, BLOCK, HD)), f32((every...  1.88 us
    pallas_call x1, Pallas kernels, body(): call(pack_kernel, 'pack', [bf16((HEADS, 2 * BLOCK + (PARTS + EARLY) * (le...  1.44 us
    pallas_call x1, Pallas kernels, body(): call(last_kernel, 'last_kv', [bf16((tokens, width))] * 2, [SMEM] + [VMEM]...  1.3 us
  transfers between devices with their start and end apart: 9, of which 3 were waited for; matrix products, arithmetic and copies ran while one was open for 0% of the time, Pallas kernels for 19%

profile of v9, /device:TPU:1, one launch (start us, length us, event | category | flops | bytes accessed | tf_op | source)
XLA Modules:
  0.0 36.3 jit_solution(5483097964007594188)
XLA Ops:
  0.7 1.4 %pack.1 = (bf16[2,256,128]{2,1,0:T(8,128)(2,1)S(1)}, bf16[2,256,128]{2,1,0:T(8,128)(2,1)S(1)}, bf16[2,256,128]{2,1,0:T(8,128)(2,1)S(1)}, bf16[2,288,128]{2,1,0:T...) custom-call(s32[2,5]{1,0:T(2,128)} %offsets_in.1, ...), custom_call_target="tpu_custom_call" | custom-call | tf_op jit(solution)/shard_map/pack/pallas_call | solution.py:256
  2.1 4.5 %collective-permute-start = (bf16[2,288,128]{2,1,0:T(8,128)(2,1)S(1)}, bf16[2,288,128]{2,1,0:T(8,128)(2,1)S(1)}, u32[]{:S(2)}, u32[]{:S(2)}) collective-permute-start(bf16[2,288,128]{2,1,0:T(8,128)(2,1)S(1)} %get-tuple-element.40), channel_id=1, source_target_pairs={{0,8},{1,9},{2,10},{3,11},{4,12},{5,13},{6,14},{7,15},{8,0},{9,1},... | collective-permute-start | bytes 442376 | tf_op jit(solution)/shard_map/ppermute | solution.py:243
  6.6 1.2 %collective-permute-start.1 = (bf16[2,256,128]{2,1,0:T(8,128)(2,1)S(1)}, bf16[2,256,128]{2,1,0:T(8,128)(2,1)S(1)}, u32[]{:S(2)}, u32[]{:S(2)}) collective-permute-start(bf16[2,256,128]{2,1,0:T(8,128)(2,1)S(1)} %get-tuple-element.41), channel_id=1, source_target_pairs={{0,1},{1,0},{2,3},{3,2},{4,5},{5,4},{6,7},{7,6},{8,9},{9,8},{10,11... | collective-permute-start | bytes 393224 | tf_op jit(solution)/shard_map/ppermute | solution.py:243
  7.8 2.5 %collective-permute-start.2 = (bf16[2,256,128]{2,1,0:T(8,128)(2,1)S(1)}, bf16[2,256,128]{2,1,0:T(8,128)(2,1)S(1)}, u32[]{:S(2)}, u32[]{:S(2)}) collective-permute-start(bf16[2,256,128]{2,1,0:T(8,128)(2,1)S(1)} %get-tuple-element.42), channel_id=1, source_target_pairs={{0,2},{1,3},{2,0},{3,1},{4,6},{5,7},{6,4},{7,5},{8,10},{9,11},{10,... | collective-permute-start | bytes 393224 | tf_op jit(solution)/shard_map/ppermute | solution.py:243
  10.3 0.7 %collective-permute-start.3 = (bf16[2,256,128]{2,1,0:T(8,128)(2,1)S(1)}, bf16[2,256,128]{2,1,0:T(8,128)(2,1)S(1)}, u32[]{:S(2)}, u32[]{:S(2)}) collective-permute-start(bf16[2,256,128]{2,1,0:T(8,128)(2,1)S(1)} %get-tuple-element.43), channel_id=1, source_target_pairs={{0,4},{1,5},{2,6},{3,7},{4,0},{5,1},{6,2},{7,3},{8,12},{9,13},{10,... | collective-permute-start | bytes 393224 | tf_op jit(solution)/shard_map/ppermute | solution.py:243
  11.0 1.1 %local_q.1 = (f32[256,256]{1,0:T(8,128)S(1)}, f32[2,256,128]{2,1,0:T(8,128)S(1)}, bf16[256,256]{1,0:T(8,128)(2,1)S(1)}, f32[1,256]{1,0:T(1,128)S(1)}, bf16[2,272...) custom-call(s32[2,5]{1,0:T(2,128)S(1)} %get-tuple-element.30.offsets, ...), custom_call_target="tpu_custom_call", output_to_operand_aliasing={{4}: (7, {}), {5}: (8, {}), {6}: (9, {})} | custom-call | tf_op jit(solution)/shard_map/local_q/pallas_call | solution.py:269
  12.2 0.8 %collective-permute-start.4 = (bf16[2,272,128]{2,1,0:T(8,128)(2,1)S(1)}, bf16[2,272,128]{2,1,0:T(8,128)(2,1)S(1)}, u32[]{:S(2)}, u32[]{:S(2)}) collective-permute-start(bf16[2,272,128]{2,1,0:T(8,128)(2,1)S(1)} %get-tuple-element.46), channel_id=1, source_target_pairs={{0,4},{1,5},{2,6},{3,7},{4,0},{5,1},{6,2},{7,3},{8,12},{9,13},{10,... | collective-permute-start | bytes 417800 | tf_op jit(solution)/shard_map/ppermute | solution.py:243
  13.0 0.0 collective-permute-done.1.r2
  13.0 0.5 %collective-permute-start.5 = (bf16[2,272,128]{2,1,0:T(8,128)(2,1)S(1)}, bf16[2,272,128]{2,1,0:T(8,128)(2,1)S(1)}, u32[]{:S(2)}, u32[]{:S(2)}) collective-permute-start(bf16[2,272,128]{2,1,0:T(8,128)(2,1)S(1)} %get-tuple-element.47), channel_id=1, source_target_pairs={{0,2},{1,3},{2,0},{3,1},{4,6},{5,7},{6,4},{7,5},{8,10},{9,11},{10,... | collective-permute-start | bytes 417800 | tf_op jit(solution)/shard_map/ppermute | solution.py:243
  13.5 1.9 %collective-permute-done.2.r3 = bf16[2,256,128]{2,1,0:T(8,128)(2,1)S(1)} collective-permute-done((bf16[2,256,128]{2,1,0:T(8,128)(2,1)S(1)}, bf16[2,256,128]{2,1,0:T(8,128)(2,1)S(1)}, u32[]{:S(2)}, u32[]{:S(2)}) %collective-permute-start.2) | collective-permute-done | bytes 131104 | tf_op jit(solution)/shard_map/ppermute | solution.py:243
  15.4 0.0 collective-permute-start.6
  15.4 0.0 collective-permute-done.3.r4
  15.4 0.0 collective-permute-done.r1.refs_1_
  15.4 1.9 %remote_q.1 = (f32[4,2,128,128]{3,2,1,0:T(8,128)S(1)}, f32[128,1,256]{2,1,0:T(1,128)}, bf16[2,240,128]{2,1,0:T(8,128)(2,1)S(1)}) custom-call(s32[2,5]{1,0:T(2,128)S(1)} %get-tuple-element.30.offsets, bf16[256,256]{1,0:T(8,128)(2,1)S(1)} %get-tuple-element.36.scaled, bf16[256,256]{1,0:T(8,128)(2,1)S(1)} %bitcast.23, ...), custom_call_target="tpu_custom_call", output_to_operand_aliasing={{2}: (10, {})} | custom-call | tf_op jit(solution)/shard_map/remote_q/pallas_call | solution.py:282
  17.3 8.1 %all-to-all-start = ((f32[128,1,256]{2,1,0:T(1,128)}), f32[128,1,256]{2,1,0:T(1,128)S(1)}, u32[]{:S(2)}, u32[]{:S(2)}) async-start(f32[128,1,256]{2,1,0:T(1,128)} %get-tuple-element.55), calls=%async_computation | async-start | bytes 262144 | tf_op jit(solution)/shard_map/all_to_all | solution.py:292
  25.4 3.4 %collective-permute-start.7 = (bf16[2,240,128]{2,1,0:T(8,128)(2,1)S(1)}, bf16[2,240,128]{2,1,0:T(8,128)(2,1)S(1)}, u32[]{:S(2)}, u32[]{:S(2)}) collective-permute-start(bf16[2,240,128]{2,1,0:T(8,128)(2,1)S(1)} %get-tuple-element.52), channel_id=1, source_target_pairs={{0,8},{1,9},{2,10},{3,11},{4,12},{5,13},{6,14},{7,15},{8,0},{9,1},... | collective-permute-start | bytes 368648 | tf_op jit(solution)/shard_map/ppermute | solution.py:243
  28.8 0.0 collective-permute-done.4.refs_0_
  28.8 0.0 collective-permute-done.5.refs_1_
  28.8 0.0 collective-permute-done.6.refs_2_
  28.8 2.7 %most_kv.1 = (bf16[256,256]{1,0:T(8,128)(2,1)}, f32[256,256]{1,0:T(8,128)S(1)}, f32[256,256]{1,0:T(8,128)S(1)}) custom-call(s32[2,5]{1,0:T(2,128)S(1)} %get-tuple-element.30.offsets, f32[1,256]{1,0:T(1,128)S(1)} %get-tuple-element.31.gain, bf16[256,256]{1,0:T(8,128)(2,1)S(1)} %get-tuple-element.36.scaled, bf16[256,256]{1,0:T(8,128)(2,1)S(1)} %bitcast.15, ...), custom_call_target="tpu_custom_call" | custom-call | tf_op jit(solution)/shard_map/most_kv/pallas_call | solution.py:294
  31.5 0.7 %collective-permute-done.7.refs_0_ = bf16[2,240,128]{2,1,0:T(8,128)(2,1)S(1)} collective-permute-done((bf16[2,240,128]{2,1,0:T(8,128)(2,1)S(1)}, bf16[2,240,128]{2,1,0:T(8,128)(2,1)S(1)}, u32[]{:S(2)}, u32[]{:S(2)}) %collective-permute-start.7) | collective-permute-done | bytes 122912 | tf_op jit(solution)/shard_map/ppermute | solution.py:243
  32.2 1.3 %last_kv.1 = (bf16[256,256]{1,0:T(8,128)(2,1)}, bf16[256,256]{1,0:T(8,128)(2,1)}) custom-call(s32[2,5]{1,0:T(2,128)S(1)} %get-tuple-element.30.offsets, f32[1,256]{1,0:T(1,128)S(1)} %get-tuple-element.31.gain, bf16[256,256]{1,0:T(8,128)(2,1)S(1)} %bitcast.16, bf16[256,256]{1,0:T(8,128)(2,1)S(1)} %bitcast.20, f32[256,256]{1,0:T(8,128)S(1)} %get-tuple-element.50.dk_in, ...), custom_call_target="tpu_custom_call" | custom-call | tf_op jit(solution)/shard_map/last_kv/pallas_call | solution.py:301
  33.5 2.1 %all-to-all-done = f32[128,1,256]{2,1,0:T(1,128)S(1)} async-done(((f32[128,1,256]{2,1,0:T(1,128)}), f32[128,1,256]{2,1,0:T(1,128)S(1)}, u32[]{:S(2)}, u32[]{:S(2)}) %all-to-all-start) | async-done | bytes 131104 | tf_op jit(solution)/shard_map/all_to_all | solution.py:292
  35.6 0.7 %reduce_sum.9 = f32[256]{0:T(256)} reduce(f32[128,1,256]{2,1,0:T(1,128)S(1)} %all-to-all-done, f32[]{:T(128)} %constant.0.clone.1), dimensions={0,1}, to_apply=%region_0.0 | reduce | flops 32512 | bytes 132100 | tf_op jit(solution)/shard_map/reduce_sum | solution.py:304
  (8 shorter events, 0.0 us)
Async XLA Ops:
  0.6 10.4 %copy-start = (bf16[1,256,256]{2,1,0:T(8,128)(2,1)S(1)}, bf16[1,256,256]{2,1,0:T(8,128)(2,1)}, u32[]{:S(2)}) copy-start(bf16[1,256,256]{2,1,0:T(8,128)(2,1)} %param.10) | copy-start | bytes 393220
  0.6 10.4 %copy-start.1 = (bf16[1,256,256]{2,1,0:T(8,128)(2,1)S(1)}, bf16[1,256,256]{2,1,0:T(8,128)(2,1)}, u32[]{:S(2)}) copy-start(bf16[1,256,256]{2,1,0:T(8,128)(2,1)} %param.8) | copy-start | bytes 393220
  0.7 10.4 %copy-start.2 = (bf16[1,256,256]{2,1,0:T(8,128)(2,1)S(1)}, bf16[1,256,256]{2,1,0:T(8,128)(2,1)}, u32[]{:S(2)}) copy-start(bf16[1,256,256]{2,1,0:T(8,128)(2,1)} %param.9) | copy-start | bytes 393220
  0.7 10.4 %copy-start.3 = (bf16[1,256,256]{2,1,0:T(8,128)(2,1)S(1)}, bf16[1,256,256]{2,1,0:T(8,128)(2,1)}, u32[]{:S(2)}) copy-start(bf16[1,256,256]{2,1,0:T(8,128)(2,1)} %param.7) | copy-start | bytes 393220
  2.1 13.3 %collective-permute-start = (bf16[2,288,128]{2,1,0:T(8,128)(2,1)S(1)}, bf16[2,288,128]{2,1,0:T(8,128)(2,1)S(1)}, u32[]{:S(2)}, u32[]{:S(2)}) collective-permute-start(bf16[2,288,128]{2,1,0:T(8,128)(2,1)S(1)} %get-tuple-element.40), channel_id=1, source_target_pairs={{0,8},{1,9},{2,10},{3,11},{4,12},{5,13},{6,14},{7,15},{8,0},{9,1},... | collective-permute-start | bytes 442376 | tf_op jit(solution)/shard_map/ppermute | solution.py:243
  6.6 6.4 %collective-permute-start.1 = (bf16[2,256,128]{2,1,0:T(8,128)(2,1)S(1)}, bf16[2,256,128]{2,1,0:T(8,128)(2,1)S(1)}, u32[]{:S(2)}, u32[]{:S(2)}) collective-permute-start(bf16[2,256,128]{2,1,0:T(8,128)(2,1)S(1)} %get-tuple-element.41), channel_id=1, source_target_pairs={{0,1},{1,0},{2,3},{3,2},{4,5},{5,4},{6,7},{7,6},{8,9},{9,8},{10,11... | collective-permute-start | bytes 393224 | tf_op jit(solution)/shard_map/ppermute | solution.py:243
  7.8 7.5 %collective-permute-start.2 = (bf16[2,256,128]{2,1,0:T(8,128)(2,1)S(1)}, bf16[2,256,128]{2,1,0:T(8,128)(2,1)S(1)}, u32[]{:S(2)}, u32[]{:S(2)}) collective-permute-start(bf16[2,256,128]{2,1,0:T(8,128)(2,1)S(1)} %get-tuple-element.42), channel_id=1, source_target_pairs={{0,2},{1,3},{2,0},{3,1},{4,6},{5,7},{6,4},{7,5},{8,10},{9,11},{10,... | collective-permute-start | bytes 393224 | tf_op jit(solution)/shard_map/ppermute | solution.py:243
  10.3 5.1 %collective-permute-start.3 = (bf16[2,256,128]{2,1,0:T(8,128)(2,1)S(1)}, bf16[2,256,128]{2,1,0:T(8,128)(2,1)S(1)}, u32[]{:S(2)}, u32[]{:S(2)}) collective-permute-start(bf16[2,256,128]{2,1,0:T(8,128)(2,1)S(1)} %get-tuple-element.43), channel_id=1, source_target_pairs={{0,4},{1,5},{2,6},{3,7},{4,0},{5,1},{6,2},{7,3},{8,12},{9,13},{10,... | collective-permute-start | bytes 393224 | tf_op jit(solution)/shard_map/ppermute | solution.py:243
  12.2 16.6 %collective-permute-start.4 = (bf16[2,272,128]{2,1,0:T(8,128)(2,1)S(1)}, bf16[2,272,128]{2,1,0:T(8,128)(2,1)S(1)}, u32[]{:S(2)}, u32[]{:S(2)}) collective-permute-start(bf16[2,272,128]{2,1,0:T(8,128)(2,1)S(1)} %get-tuple-element.46), channel_id=1, source_target_pairs={{0,4},{1,5},{2,6},{3,7},{4,0},{5,1},{6,2},{7,3},{8,12},{9,13},{10,... | collective-permute-start | bytes 417800 | tf_op jit(solution)/shard_map/ppermute | solution.py:243
  13.0 15.8 %collective-permute-start.5 = (bf16[2,272,128]{2,1,0:T(8,128)(2,1)S(1)}, bf16[2,272,128]{2,1,0:T(8,128)(2,1)S(1)}, u32[]{:S(2)}, u32[]{:S(2)}) collective-permute-start(bf16[2,272,128]{2,1,0:T(8,128)(2,1)S(1)} %get-tuple-element.47), channel_id=1, source_target_pairs={{0,2},{1,3},{2,0},{3,1},{4,6},{5,7},{6,4},{7,5},{8,10},{9,11},{10,... | collective-permute-start | bytes 417800 | tf_op jit(solution)/shard_map/ppermute | solution.py:243
  15.4 13.4 %collective-permute-start.6 = (bf16[2,272,128]{2,1,0:T(8,128)(2,1)S(1)}, bf16[2,272,128]{2,1,0:T(8,128)(2,1)S(1)}, u32[]{:S(2)}, u32[]{:S(2)}) collective-permute-start(bf16[2,272,128]{2,1,0:T(8,128)(2,1)S(1)} %get-tuple-element.48), channel_id=1, source_target_pairs={{0,1},{1,0},{2,3},{3,2},{4,5},{5,4},{6,7},{7,6},{8,9},{9,8},{10,11... | collective-permute-start | bytes 417800 | tf_op jit(solution)/shard_map/ppermute | solution.py:243
  17.3 18.3 %all-to-all-start = ((f32[128,1,256]{2,1,0:T(1,128)}), f32[128,1,256]{2,1,0:T(1,128)S(1)}, u32[]{:S(2)}, u32[]{:S(2)}) async-start(f32[128,1,256]{2,1,0:T(1,128)} %get-tuple-element.55), calls=%async_computation | async-start | bytes 262144 | tf_op jit(solution)/shard_map/all_to_all | solution.py:292
  25.4 6.8 %collective-permute-start.7 = (bf16[2,240,128]{2,1,0:T(8,128)(2,1)S(1)}, bf16[2,240,128]{2,1,0:T(8,128)(2,1)S(1)}, u32[]{:S(2)}, u32[]{:S(2)}) collective-permute-start(bf16[2,240,128]{2,1,0:T(8,128)(2,1)S(1)} %get-tuple-element.52), channel_id=1, source_target_pairs={{0,8},{1,9},{2,10},{3,11},{4,12},{5,13},{6,14},{7,15},{8,0},{9,1},... | collective-permute-start | bytes 368648 | tf_op jit(solution)/shard_map/ppermute | solution.py:243

commit v10 on v9

--- a/solution.py
+++ b/solution.py
@@ -47,39 +47,53 @@
     return (rows.astype(jnp.float32) * gain).astype(jnp.bfloat16)
 
 
-def pack_kernel(offsets_in, k_in, v_in, q_in, d_in, norm_in, gain_in, *refs):
-    outs, (norm, gain, table), (offsets, k, v, q, d, sems) = refs[:8], refs[8:11], refs[11:]
+def split_norm(norm, head, block):
+    whole = jnp.where(block == 0, norm[head : head + 1, :BLOCK], norm[head : head + 1, BLOCK:])
+    high = whole.astype(jnp.bfloat16).astype(jnp.float32)
+    rest = whole - high
+    mid = rest.astype(jnp.bfloat16).astype(jnp.float32)
+    low = rest - mid
+    row = lax.broadcasted_iota(jnp.int32, (PARTS, BLOCK), 0)
+    parts = jnp.where(row == 0, high, jnp.where(row == 1, mid, jnp.where(row == 2, low, 0.0)))
+    return parts.astype(jnp.bfloat16)
+
+
+def pack_kernel(offsets_in, k_in, v_in, d_in, norm_in, gain_in, q_in, *refs):
+    firsts, (norm, gain, table, q, k, v, d), (offsets, sems) = refs[:4], refs[4:11], refs[11:]
     copies = []
-    moves = ((offsets_in, offsets), (k_in, k), (v_in, v), (q_in, q), (d_in, d))
-    for i, (source, target) in enumerate(moves + ((norm_in, norm), (gain_in, gain), (offsets_in, table))):
+    moves = ((offsets_in, offsets), (k_in, k), (v_in, v), (d_in, d))
+    moves += ((norm_in, norm), (gain_in, gain), (offsets_in, table), (q_in, q))
+    for i, (source, target) in enumerate(moves):
         copies.append(pltpu.make_async_copy(source, target, sems.at[i]))
         copies[-1].start()
     for copy in copies:
         copy.wait()
-    row = lax.broadcasted_iota(jnp.int32, (PARTS, BLOCK), 0)
     for level in range(1, LEVELS):
-        first, second = outs[level - 1], outs[LEVELS - 1 + level - 1]
+        first = firsts[level - 1]
         for head in range(HEADS):
             block, c = offsets[head, level] & 1, cols(head)
             at = block_rows(block)
             first[head, :BLOCK] = k[at, c]
             first[head, BLOCK : 2 * BLOCK] = v[at, c]
-            second[head, :BLOCK] = q[at, c]
-            whole = jnp.where(block == 0, norm[head : head + 1, :BLOCK], norm[head : head + 1, BLOCK:])
-            high = whole.astype(jnp.bfloat16).astype(jnp.float32)
-            rest = whole - high
-            mid = rest.astype(jnp.bfloat16).astype(jnp.float32)
-            low = rest - mid
-            parts = jnp.where(row == 0, high, jnp.where(row == 1, mid, jnp.where(row == 2, low, 0.0)))
-            parts = parts.astype(jnp.bfloat16)
             if level in LATE:
                 start = pl.multiple_of(block * BLOCK, BLOCK)
-                first[head, 2 * BLOCK : 2 * BLOCK + PARTS] = parts
+                first[head, 2 * BLOCK : 2 * BLOCK + PARTS] = split_norm(norm, head, block)
                 first[head, 2 * BLOCK + PARTS :] = d[pl.ds(start + BLOCK - EARLY, EARLY), c]
+
+
+def pack_second(offsets, q, d, norm, seconds):
+    for level in range(1, LEVELS):
+        second = seconds[level - 1]
+        for head in range(HEADS):
+            block, c = offsets[head, level] & 1, cols(head)
+            at = block_rows(block)
+            second[head, :BLOCK] = q[at, c]
+            if level in LATE:
+                start = pl.multiple_of(block * BLOCK, BLOCK)
                 second[head, BLOCK:] = d[pl.ds(start, BLOCK - EARLY), c]
             else:
                 second[head, BLOCK : 2 * BLOCK] = d[at, c]
-                second[head, 2 * BLOCK :] = parts
+                second[head, 2 * BLOCK :] = split_norm(norm, head, block)
 
 
 def block_counts(offsets, head):
@@ -96,8 +110,8 @@
     return slice(b * BLOCK, (b + 1) * BLOCK), slice((1 - b) * BLOCK, (2 - b) * BLOCK)
 
 
-def local_q_kernel(offsets, gain, q, k, v, d, norm, *refs):
-    dq, norm_cols, scaled, partial = refs[LEVELS - 1 - len(LATE) :][:4]
+def local_q_kernel(offsets, gain, q, k, v, d, norm, dq, norm_cols, scaled, partial, *seconds):
+    pack_second(offsets, q, d, norm, seconds)
     for head in range(HEADS):
         c = cols(head)
         count = block_counts(offsets, head)
@@ -252,33 +266,28 @@
     f32 = functools.partial(jax.ShapeDtypeStruct, dtype=jnp.float32)
     bf16 = functools.partial(jax.ShapeDtypeStruct, dtype=jnp.bfloat16)
     many = LEVELS - 1
-    raw = pltpu.VMEM((tokens, width), jnp.bfloat16)
-    *sent, norm, gain, table = call(
+    *firsts, norm, gain, table, q, k, v, d = call(
         pack_kernel,
         "pack",
         [bf16((HEADS, 2 * BLOCK + (PARTS + EARLY) * (level in LATE), HD)) for level in range(1, LEVELS)]
-        + [bf16((HEADS, 2 * BLOCK + (-EARLY if level in LATE else PARTS), HD)) for level in range(1, LEVELS)]
-        + [f32(norm.shape), f32(gain.shape), jax.ShapeDtypeStruct(offsets.shape, jnp.int32)],
+        + [f32(norm.shape), f32(gain.shape), jax.ShapeDtypeStruct(offsets.shape, jnp.int32)]
+        + [bf16((tokens, width))] * 4,
         [HBM] * 7,
-        [pltpu.SMEM(offsets.shape, jnp.int32), raw, raw, raw, raw, pltpu.SemaphoreType.DMA((8,))],
-    )(*map(in_hbm, (offsets, k, v, q, d, norm, gain)))
+        [pltpu.SMEM(offsets.shape, jnp.int32), pltpu.SemaphoreType.DMA((8,))],
+    )(*map(in_hbm, (offsets, k, v, d, norm, gain, q)))
     offsets = table
-    second = dict(zip(range(1, LEVELS), sent[many:]))
-    got_kv = swap({level: sent[level - 1] for level in ORDER})
-    early = {level: second[level] for level in SOON}
-    dq, norm_cols, scaled, partial, *passed = call(
+    got_kv = swap({level: firsts[level - 1] for level in ORDER})
+    dq, norm_cols, scaled, partial, *second = call(
         local_q_kernel,
         "local_q",
         [f32((tokens, width)), f32((HEADS, tokens, HD)), bf16((tokens, width)), f32((1, width))]
-        + [bf16(p.shape) for p in early.values()],
-        [SMEM] + [VMEM] * 6 + [ANY] * len(early),
-        out_specs=[VMEM] * 4 + [ANY] * len(early),
-        aliases={7 + i: 4 + i for i in range(len(early))},
-    )(offsets, gain, q, k, v, d, norm, *early.values())
-    got_qd = swap(dict(zip(early, passed)))
+        + [bf16((HEADS, 2 * BLOCK + (-EARLY if level in LATE else PARTS), HD)) for level in range(1, LEVELS)],
+        [SMEM] + [VMEM] * 6,
+    )(offsets, gain, q, k, v, d, norm)
+    got_qd = swap({level: second[level - 1] for level in SOON})
     axes = ("dp", "ctx")
     everyone = lax.axis_size(axes)
-    late = [second[level] for level in LATE]
+    late = [second[level - 1] for level in LATE]
     added, partial, *late = call(
         query_kernel,
         "remote_q",

time: 36.5 us -> 36.3 us (level)
  Pallas kernels: 8.47 us -> 7.86 us
  waiting for transfers between devices: 4.7 us -> 5.2 us
    ppermute x8, waiting for transfers between devices: 2.57 us -> 3.07 us  [swap(): lax.ppermute(payload, 'ctx', [(i, i ^ half) for i in range(count)])]
    pallas_call x1, Pallas kernels: 2.71 us -> 2.22 us  [body(): call(most_kernel, 'most_kv', [bf16((tokens, width)), f32((tokens, width))...]
  transfers between devices with their start and end apart: 9 -> 9, of which waited for: 3 -> 3; matrix products, arithmetic and copies ran while one was open for 0% -> 0% of each run, Pallas kernels for 19% -> 18%
where the time goes in v10:
time: 36.3 us; the launch traced here: 36.2 us
  starting transfers between devices  21.7 us (60%)
  Pallas kernels  7.86 us (22%)
  waiting for transfers between devices  5.2 us (14%)
  other arithmetic  0.71 us (2%)
  between operations  0.67 us (2%)
    ppermute x8, starting transfers between devices, swap(): lax.ppermute(payload, 'ctx', [(i, i ^ half) for i in range(count)])  13.6 us
    all_to_all x1, starting transfers between devices, body(): parts = lax.all_to_all(partial, axes, 0, 0, tiled=True)  8.13 us
    ppermute x8, waiting for transfers between devices, swap(): lax.ppermute(payload, 'ctx', [(i, i ^ half) for i in range(count)])  3.07 us
    pallas_call x1, Pallas kernels, body(): call(most_kernel, 'most_kv', [bf16((tokens, width)), f32((tokens, width))...  2.22 us
    all_to_all x1, waiting for transfers between devices, body(): parts = lax.all_to_all(partial, axes, 0, 0, tiled=True)  2.13 us
    pallas_call x1, Pallas kernels, body(): call(query_kernel, 'remote_q', [f32((many, HEADS, BLOCK, HD)), f32((every...  1.87 us
    pallas_call x1, Pallas kernels, body(): call(pack_kernel, 'pack', [bf16((HEADS, 2 * BLOCK + (PARTS + EARLY) * (le...  1.33 us
    pallas_call x1, Pallas kernels, body(): call(last_kernel, 'last_kv', [bf16((tokens, width))] * 2, [SMEM] + [VMEM]...  1.3 us
  transfers between devices with their start and end apart: 9, of which 3 were waited for; matrix products, arithmetic and copies ran while one was open for 0% of the time, Pallas kernels for 18%

profile of v10, /device:TPU:1, one launch (start us, length us, event | category | flops | bytes accessed | tf_op | source)
XLA Modules:
  0.0 36.2 jit_solution(13733831488745064133)
XLA Ops:
  0.6 1.3 %pack.1 = (bf16[2,256,128]{2,1,0:T(8,128)(2,1)S(1)}, bf16[2,256,128]{2,1,0:T(8,128)(2,1)S(1)}, bf16[2,256,128]{2,1,0:T(8,128)(2,1)S(1)}, bf16[2,288,128]{2,1,0:T...) custom-call(s32[2,5]{1,0:T(2,128)} %offsets_in.1, ...), custom_call_target="tpu_custom_call" | custom-call | tf_op jit(solution)/shard_map/pack/pallas_call | solution.py:269
  2.0 4.5 %collective-permute-start = (bf16[2,288,128]{2,1,0:T(8,128)(2,1)S(1)}, bf16[2,288,128]{2,1,0:T(8,128)(2,1)S(1)}, u32[]{:S(2)}, u32[]{:S(2)}) collective-permute-start(bf16[2,288,128]{2,1,0:T(8,128)(2,1)S(1)} %get-tuple-element.42), channel_id=1, source_target_pairs={{0,8},{1,9},{2,10},{3,11},{4,12},{5,13},{6,14},{7,15},{8,0},{9,1},... | collective-permute-start | bytes 442376 | tf_op jit(solution)/shard_map/ppermute | solution.py:257
  6.5 1.2 %collective-permute-start.1 = (bf16[2,256,128]{2,1,0:T(8,128)(2,1)S(1)}, bf16[2,256,128]{2,1,0:T(8,128)(2,1)S(1)}, u32[]{:S(2)}, u32[]{:S(2)}) collective-permute-start(bf16[2,256,128]{2,1,0:T(8,128)(2,1)S(1)} %get-tuple-element.43), channel_id=1, source_target_pairs={{0,1},{1,0},{2,3},{3,2},{4,5},{5,4},{6,7},{7,6},{8,9},{9,8},{10,11... | collective-permute-start | bytes 393224 | tf_op jit(solution)/shard_map/ppermute | solution.py:257
  7.7 2.5 %collective-permute-start.2 = (bf16[2,256,128]{2,1,0:T(8,128)(2,1)S(1)}, bf16[2,256,128]{2,1,0:T(8,128)(2,1)S(1)}, u32[]{:S(2)}, u32[]{:S(2)}) collective-permute-start(bf16[2,256,128]{2,1,0:T(8,128)(2,1)S(1)} %get-tuple-element.44), channel_id=1, source_target_pairs={{0,2},{1,3},{2,0},{3,1},{4,6},{5,7},{6,4},{7,5},{8,10},{9,11},{10,... | collective-permute-start | bytes 393224 | tf_op jit(solution)/shard_map/ppermute | solution.py:257
  10.1 0.7 %collective-permute-start.3 = (bf16[2,256,128]{2,1,0:T(8,128)(2,1)S(1)}, bf16[2,256,128]{2,1,0:T(8,128)(2,1)S(1)}, u32[]{:S(2)}, u32[]{:S(2)}) collective-permute-start(bf16[2,256,128]{2,1,0:T(8,128)(2,1)S(1)} %get-tuple-element.45), channel_id=1, source_target_pairs={{0,4},{1,5},{2,6},{3,7},{4,0},{5,1},{6,2},{7,3},{8,12},{9,13},{10,... | collective-permute-start | bytes 393224 | tf_op jit(solution)/shard_map/ppermute | solution.py:257
  10.9 1.1 %local_q.1 = (f32[256,256]{1,0:T(8,128)S(1)}, f32[2,256,128]{2,1,0:T(8,128)S(1)}, bf16[256,256]{1,0:T(8,128)(2,1)S(1)}, f32[1,256]{1,0:T(1,128)S(1)}, bf16[2,272...) custom-call(s32[2,5]{1,0:T(2,128)S(1)} %get-tuple-element.31.offsets, ...), custom_call_target="tpu_custom_call" | custom-call | tf_op jit(solution)/shard_map/local_q/pallas_call | solution.py:280
  12.0 0.8 %collective-permute-start.4 = (bf16[2,272,128]{2,1,0:T(8,128)(2,1)S(1)}, bf16[2,272,128]{2,1,0:T(8,128)(2,1)S(1)}, u32[]{:S(2)}, u32[]{:S(2)}) collective-permute-start(bf16[2,272,128]{2,1,0:T(8,128)(2,1)S(1)} %get-tuple-element.48), channel_id=1, source_target_pairs={{0,4},{1,5},{2,6},{3,7},{4,0},{5,1},{6,2},{7,3},{8,12},{9,13},{10,... | collective-permute-start | bytes 417800 | tf_op jit(solution)/shard_map/ppermute | solution.py:257
  12.8 0.0 collective-permute-done.1.r2
  12.8 0.5 %collective-permute-start.5 = (bf16[2,272,128]{2,1,0:T(8,128)(2,1)S(1)}, bf16[2,272,128]{2,1,0:T(8,128)(2,1)S(1)}, u32[]{:S(2)}, u32[]{:S(2)}) collective-permute-start(bf16[2,272,128]{2,1,0:T(8,128)(2,1)S(1)} %get-tuple-element.49), channel_id=1, source_target_pairs={{0,2},{1,3},{2,0},{3,1},{4,6},{5,7},{6,4},{7,5},{8,10},{9,11},{10,... | collective-permute-start | bytes 417800 | tf_op jit(solution)/shard_map/ppermute | solution.py:257
  13.3 1.9 %collective-permute-done.2.r3 = bf16[2,256,128]{2,1,0:T(8,128)(2,1)S(1)} collective-permute-done((bf16[2,256,128]{2,1,0:T(8,128)(2,1)S(1)}, bf16[2,256,128]{2,1,0:T(8,128)(2,1)S(1)}, u32[]{:S(2)}, u32[]{:S(2)}) %collective-permute-start.2) | collective-permute-done | bytes 131104 | tf_op jit(solution)/shard_map/ppermute | solution.py:257
  15.2 0.0 collective-permute-start.6
  15.2 0.0 collective-permute-done.3.r4
  15.2 0.0 collective-permute-done.r1.refs_1_
  15.2 1.9 %remote_q.1 = (f32[4,2,128,128]{3,2,1,0:T(8,128)S(1)}, f32[128,1,256]{2,1,0:T(1,128)}, bf16[2,240,128]{2,1,0:T(8,128)(2,1)S(1)}) custom-call(s32[2,5]{1,0:T(2,128)S(1)} %get-tuple-element.31.offsets, bf16[256,256]{1,0:T(8,128)(2,1)S(1)} %get-tuple-element.38.scaled, bf16[256,256]{1,0:T(8,128)(2,1)S(1)} %get-tuple-element.33.q, ...), custom_call_target="tpu_custom_call", output_to_operand_aliasing={{2}: (10, {})} | custom-call | tf_op jit(solution)/shard_map/remote_q/pallas_call | solution.py:291
  17.1 8.1 %all-to-all-start = ((f32[128,1,256]{2,1,0:T(1,128)}), f32[128,1,256]{2,1,0:T(1,128)S(1)}, u32[]{:S(2)}, u32[]{:S(2)}) async-start(f32[128,1,256]{2,1,0:T(1,128)} %get-tuple-element.57), calls=%async_computation | async-start | bytes 262144 | tf_op jit(solution)/shard_map/all_to_all | solution.py:301
  25.3 3.4 %collective-permute-start.7 = (bf16[2,240,128]{2,1,0:T(8,128)(2,1)S(1)}, bf16[2,240,128]{2,1,0:T(8,128)(2,1)S(1)}, u32[]{:S(2)}, u32[]{:S(2)}) collective-permute-start(bf16[2,240,128]{2,1,0:T(8,128)(2,1)S(1)} %get-tuple-element.54), channel_id=1, source_target_pairs={{0,8},{1,9},{2,10},{3,11},{4,12},{5,13},{6,14},{7,15},{8,0},{9,1},... | collective-permute-start | bytes 368648 | tf_op jit(solution)/shard_map/ppermute | solution.py:257
  28.6 0.0 collective-permute-done.4.refs_0_
  28.6 0.0 collective-permute-done.5.refs_1_
  28.6 0.0 collective-permute-done.6.refs_2_
  28.6 2.2 %most_kv.1 = (bf16[256,256]{1,0:T(8,128)(2,1)}, f32[256,256]{1,0:T(8,128)S(1)}, f32[256,256]{1,0:T(8,128)S(1)}) custom-call(s32[2,5]{1,0:T(2,128)S(1)} %get-tuple-element.31.offsets, f32[1,256]{1,0:T(1,128)S(1)} %get-tuple-element.32.gain, bf16[256,256]{1,0:T(8,128)(2,1)S(1)} %get-tuple-element.38.scaled, bf16[256,256]{1,0:T(8,128)(2,1)S(1)} %get-tuple-element.34.k, ...), custom_call_target="tpu_custom_call" | custom-call | tf_op jit(solution)/shard_map/most_kv/pallas_call | solution.py:303
  30.8 1.2 %collective-permute-done.7.refs_0_ = bf16[2,240,128]{2,1,0:T(8,128)(2,1)S(1)} collective-permute-done((bf16[2,240,128]{2,1,0:T(8,128)(2,1)S(1)}, bf16[2,240,128]{2,1,0:T(8,128)(2,1)S(1)}, u32[]{:S(2)}, u32[]{:S(2)}) %collective-permute-start.7) | collective-permute-done | bytes 122912 | tf_op jit(solution)/shard_map/ppermute | solution.py:257
  32.0 1.3 %last_kv.1 = (bf16[256,256]{1,0:T(8,128)(2,1)}, bf16[256,256]{1,0:T(8,128)(2,1)}) custom-call(s32[2,5]{1,0:T(2,128)S(1)} %get-tuple-element.31.offsets, f32[1,256]{1,0:T(1,128)S(1)} %get-tuple-element.32.gain, bf16[256,256]{1,0:T(8,128)(2,1)S(1)} %get-tuple-element.34.k, bf16[256,256]{1,0:T(8,128)(2,1)S(1)} %get-tuple-element.35.v, ...), custom_call_target="tpu_custom_call" | custom-call | tf_op jit(solution)/shard_map/last_kv/pallas_call | solution.py:310
  33.3 2.1 %all-to-all-done = f32[128,1,256]{2,1,0:T(1,128)S(1)} async-done(((f32[128,1,256]{2,1,0:T(1,128)}), f32[128,1,256]{2,1,0:T(1,128)S(1)}, u32[]{:S(2)}, u32[]{:S(2)}) %all-to-all-start) | async-done | bytes 131104 | tf_op jit(solution)/shard_map/all_to_all | solution.py:301
  35.5 0.7 %reduce_sum.9 = f32[256]{0:T(256)} reduce(f32[128,1,256]{2,1,0:T(1,128)S(1)} %all-to-all-done, f32[]{:T(128)} %constant.0.clone.1), dimensions={0,1}, to_apply=%region_0.0 | reduce | flops 32512 | bytes 132100 | tf_op jit(solution)/shard_map/reduce_sum | solution.py:313
Async XLA Ops:
  2.0 13.3 %collective-permute-start = (bf16[2,288,128]{2,1,0:T(8,128)(2,1)S(1)}, bf16[2,288,128]{2,1,0:T(8,128)(2,1)S(1)}, u32[]{:S(2)}, u32[]{:S(2)}) collective-permute-start(bf16[2,288,128]{2,1,0:T(8,128)(2,1)S(1)} %get-tuple-element.42), channel_id=1, source_target_pairs={{0,8},{1,9},{2,10},{3,11},{4,12},{5,13},{6,14},{7,15},{8,0},{9,1},... | collective-permute-start | bytes 442376 | tf_op jit(solution)/shard_map/ppermute | solution.py:257
  6.5 6.4 %collective-permute-start.1 = (bf16[2,256,128]{2,1,0:T(8,128)(2,1)S(1)}, bf16[2,256,128]{2,1,0:T(8,128)(2,1)S(1)}, u32[]{:S(2)}, u32[]{:S(2)}) collective-permute-start(bf16[2,256,128]{2,1,0:T(8,128)(2,1)S(1)} %get-tuple-element.43), channel_id=1, source_target_pairs={{0,1},{1,0},{2,3},{3,2},{4,5},{5,4},{6,7},{7,6},{8,9},{9,8},{10,11... | collective-permute-start | bytes 393224 | tf_op jit(solution)/shard_map/ppermute | solution.py:257
  7.7 7.5 %collective-permute-start.2 = (bf16[2,256,128]{2,1,0:T(8,128)(2,1)S(1)}, bf16[2,256,128]{2,1,0:T(8,128)(2,1)S(1)}, u32[]{:S(2)}, u32[]{:S(2)}) collective-permute-start(bf16[2,256,128]{2,1,0:T(8,128)(2,1)S(1)} %get-tuple-element.44), channel_id=1, source_target_pairs={{0,2},{1,3},{2,0},{3,1},{4,6},{5,7},{6,4},{7,5},{8,10},{9,11},{10,... | collective-permute-start | bytes 393224 | tf_op jit(solution)/shard_map/ppermute | solution.py:257
  10.1 5.1 %collective-permute-start.3 = (bf16[2,256,128]{2,1,0:T(8,128)(2,1)S(1)}, bf16[2,256,128]{2,1,0:T(8,128)(2,1)S(1)}, u32[]{:S(2)}, u32[]{:S(2)}) collective-permute-start(bf16[2,256,128]{2,1,0:T(8,128)(2,1)S(1)} %get-tuple-element.45), channel_id=1, source_target_pairs={{0,4},{1,5},{2,6},{3,7},{4,0},{5,1},{6,2},{7,3},{8,12},{9,13},{10,... | collective-permute-start | bytes 393224 | tf_op jit(solution)/shard_map/ppermute | solution.py:257
  12.0 16.6 %collective-permute-start.4 = (bf16[2,272,128]{2,1,0:T(8,128)(2,1)S(1)}, bf16[2,272,128]{2,1,0:T(8,128)(2,1)S(1)}, u32[]{:S(2)}, u32[]{:S(2)}) collective-permute-start(bf16[2,272,128]{2,1,0:T(8,128)(2,1)S(1)} %get-tuple-element.48), channel_id=1, source_target_pairs={{0,4},{1,5},{2,6},{3,7},{4,0},{5,1},{6,2},{7,3},{8,12},{9,13},{10,... | collective-permute-start | bytes 417800 | tf_op jit(solution)/shard_map/ppermute | solution.py:257
  12.8 15.8 %collective-permute-start.5 = (bf16[2,272,128]{2,1,0:T(8,128)(2,1)S(1)}, bf16[2,272,128]{2,1,0:T(8,128)(2,1)S(1)}, u32[]{:S(2)}, u32[]{:S(2)}) collective-permute-start(bf16[2,272,128]{2,1,0:T(8,128)(2,1)S(1)} %get-tuple-element.49), channel_id=1, source_target_pairs={{0,2},{1,3},{2,0},{3,1},{4,6},{5,7},{6,4},{7,5},{8,10},{9,11},{10,... | collective-permute-start | bytes 417800 | tf_op jit(solution)/shard_map/ppermute | solution.py:257
  15.2 13.4 %collective-permute-start.6 = (bf16[2,272,128]{2,1,0:T(8,128)(2,1)S(1)}, bf16[2,272,128]{2,1,0:T(8,128)(2,1)S(1)}, u32[]{:S(2)}, u32[]{:S(2)}) collective-permute-start(bf16[2,272,128]{2,1,0:T(8,128)(2,1)S(1)} %get-tuple-element.50), channel_id=1, source_target_pairs={{0,1},{1,0},{2,3},{3,2},{4,5},{5,4},{6,7},{7,6},{8,9},{9,8},{10,11... | collective-permute-start | bytes 417800 | tf_op jit(solution)/shard_map/ppermute | solution.py:257
  17.1 18.3 %all-to-all-start = ((f32[128,1,256]{2,1,0:T(1,128)}), f32[128,1,256]{2,1,0:T(1,128)S(1)}, u32[]{:S(2)}, u32[]{:S(2)}) async-start(f32[128,1,256]{2,1,0:T(1,128)} %get-tuple-element.57), calls=%async_computation | async-start | bytes 262144 | tf_op jit(solution)/shard_map/all_to_all | solution.py:301
  25.3 6.8 %collective-permute-start.7 = (bf16[2,240,128]{2,1,0:T(8,128)(2,1)S(1)}, bf16[2,240,128]{2,1,0:T(8,128)(2,1)S(1)}, u32[]{:S(2)}, u32[]{:S(2)}) collective-permute-start(bf16[2,240,128]{2,1,0:T(8,128)(2,1)S(1)} %get-tuple-element.54), channel_id=1, source_target_pairs={{0,8},{1,9},{2,10},{3,11},{4,12},{5,13},{6,14},{7,15},{8,0},{9,1},... | collective-permute-start | bytes 368648 | tf_op jit(solution)/shard_map/ppermute | solution.py:257

commit v11 on v10

--- a/solution.py
+++ b/solution.py
@@ -110,21 +110,38 @@
     return slice(b * BLOCK, (b + 1) * BLOCK), slice((1 - b) * BLOCK, (2 - b) * BLOCK)
 
 
-def local_q_kernel(offsets, gain, q, k, v, d, norm, dq, norm_cols, scaled, partial, *seconds):
+def local_q_kernel(offsets, gain, q, k, v, d, norm, dq, scaled, partial, picked, picked_norm, taking, *seconds):
     pack_second(offsets, q, d, norm, seconds)
+    me = lax.axis_index("ctx")
+    row = lax.broadcasted_iota(jnp.int32, taking.shape, 0)
+    flags = jnp.zeros(taking.shape, jnp.float32)
+    parts = []
     for head in range(HEADS):
         c = cols(head)
+        query, key = scale_rows(q[:, c], gain[:, c]), k[:, c]
+        scaled[:, c] = query
+        parts.append((c, key, dot(query, key, NT), dot(d[:, c], v[:, c], NT)))
+    for head, (c, key, scores, pull) in enumerate(parts):
+        column = jnp.transpose(jnp.broadcast_to(norm[head : head + 1, :], (BLOCK, 2 * BLOCK)))
+        for level in range(1, LEVELS):
+            active, block = place(offsets, me, head, level)
+            at = block_rows(block)
+            picked_norm[level - 1, head] = jnp.where(block == 0, column[:BLOCK], column[BLOCK:])
+            for i, source in enumerate((scaled, q, d)):
+                picked[i, level - 1, head] = source[at, c]
+            flags = jnp.where((row == HEADS * (level - 1) + head) & active, 1.0, flags)
+        probs = jnp.exp(scores * SCALE - jnp.concatenate([column, column], axis=1))
+        parts[head] = (c, key, (probs * pull).astype(jnp.bfloat16))
+    for head, (c, key, grads) in enumerate(parts):
         count = block_counts(offsets, head)
-        query, key, value, dout = scale_rows(q[:, c], gain[:, c]), k[:, c], v[:, c], d[:, c]
-        scaled[:, c] = query
-        column = jnp.transpose(jnp.broadcast_to(norm[head : head + 1, :], (BLOCK, 2 * BLOCK)))
-        norm_cols[head] = column
-        probs = jnp.exp(dot(query, key, NT) * SCALE - jnp.concatenate([column, column], axis=1))
-        grads = (probs * dot(dout, value, NT)).astype(jnp.bfloat16)
+        sums = 0.0
         for b in range(2):
             own, other = both_blocks(b)
-            dq[own, c] = count[b] * dot(grads[own, own], key[own], NN) + dot(grads[own, other], key[other], NN)
-        partial[:, c] = jnp.sum(q[:, c].astype(jnp.float32) * dq[:, c], axis=0, keepdims=True)
+            more = count[b] * dot(grads[own, own], key[own], NN) + dot(grads[own, other], key[other], NN)
+            dq[own, c] = more
+            sums = sums + jnp.sum(q[own, c].astype(jnp.float32) * more, axis=0, keepdims=True)
+        partial[:, c] = sums
+    taking[...] = flags
 
 
 def for_each_level(offsets, levels, fn):
@@ -141,40 +158,28 @@
             pl.when(spots[0][0] | spots[1][0])(both)
 
 
-def query_kernel(offsets, scaled, q, d, norm_cols, partial_in, r1, r2, r3, r4, *refs):
-    added, partial, total = refs[len(LATE)], refs[len(LATE) + 1], refs[-1]
+def query_kernel(picked, picked_norm, taking, partial_in, r1, r2, r3, r4, *refs):
+    added, partial = refs[len(LATE)], refs[len(LATE) + 1]
     received = dict(zip(ORDER, (r1, r2, r3, r4)))
-    total[...] = partial_in[...]
-
-    me = lax.axis_index("ctx")
-    spots = {level: [place(offsets, me, head, level) for head in range(HEADS)] for level in range(1, LEVELS)}
-
-    def any_active(level):
-        return spots[level][0][0] | spots[level][1][0]
-
-    def some(levels):
-        parts = []
-        for level in levels:
-            for head in range(HEADS):
-                got, (active, block) = received[level], spots[level][head]
-                c, at = cols(head), block_rows(block)
-                scores = dot(scaled[at, c], got[head, :BLOCK], NT)
-                parts.append((level, head, active, at, c, scores, dot(d[at, c], got[head, BLOCK : 2 * BLOCK], NT)))
-        grads = []
-        for level, head, active, at, c, scores, pull in parts:
-            probs = jnp.exp(scores * SCALE - norm_cols[head, at, :])
-            grads.append((probs * pull).astype(jnp.bfloat16))
-        mores = [dot(grad, received[p[0]][p[1], :BLOCK], NN) for grad, p in zip(grads, parts)]
-        sums = [0.0] * HEADS
-        for more, (level, head, active, at, c, _, _) in zip(mores, parts):
-            more = jnp.where(active, more, 0.0)
-            added[level - 1, head] = more
-            sums[head] = sums[head] + jnp.sum(q[at, c].astype(jnp.float32) * more, axis=0, keepdims=True)
-        for head in range(HEADS):
-            total[:, cols(head)] += sums[head]
-
-    some((1, 2, 3, 4))
-    partial[...] = jnp.broadcast_to((total[...] * SCALE)[None], partial.shape)
+    spots = [(level, head) for level in range(1, LEVELS) for head in range(HEADS)]
+    products = []
+    for level, head in spots:
+        got, n = received[level], level - 1
+        scores = dot(picked[0, n, head], got[head, :BLOCK], NT)
+        products.append((scores, dot(picked[2, n, head], got[head, BLOCK : 2 * BLOCK], NT)))
+    grads = []
+    for (level, head), (scores, pull) in zip(spots, products):
+        probs = jnp.exp(scores * SCALE - picked_norm[level - 1, head])
+        grads.append((probs * pull).astype(jnp.bfloat16))
+    mores = [dot(grad, received[level][head, :BLOCK], NN) for (level, head), grad in zip(spots, grads)]
+    sums = [partial_in[:, cols(head)] for head in range(HEADS)]
+    for (level, head), more in zip(spots, mores):
+        n = level - 1
+        more = jnp.where(taking[HEADS * n + head : HEADS * n + head + 1, :] > 0.0, more, 0.0)
+        added[n, head] = more
+        sums[head] = sums[head] + jnp.sum(picked[1, n, head].astype(jnp.float32) * more, axis=0, keepdims=True)
+    total = jnp.concatenate(sums, axis=1) * SCALE
+    partial[...] = jnp.broadcast_to(total[None], partial.shape)
 
 
 def add_keys(level, spots, got, first, gain, k, v, dk, dv):
@@ -277,13 +282,15 @@
     )(*map(in_hbm, (offsets, k, v, d, norm, gain, q)))
     offsets = table
     got_kv = swap({level: firsts[level - 1] for level in ORDER})
-    dq, norm_cols, scaled, partial, *second = call(
+    dq, scaled, partial, *picks, s1, s2, s3, s4 = call(
         local_q_kernel,
         "local_q",
-        [f32((tokens, width)), f32((HEADS, tokens, HD)), bf16((tokens, width)), f32((1, width))]
+        [f32((tokens, width)), bf16((tokens, width)), f32((1, width))]
+        + [bf16((3, many, HEADS, BLOCK, HD)), f32((many, HEADS, BLOCK, HD)), f32((many * HEADS, HD))]
         + [bf16((HEADS, 2 * BLOCK + (-EARLY if level in LATE else PARTS), HD)) for level in range(1, LEVELS)],
         [SMEM] + [VMEM] * 6,
     )(offsets, gain, q, k, v, d, norm)
+    second = (s1, s2, s3, s4)
     got_qd = swap({level: second[level - 1] for level in SOON})
     axes = ("dp", "ctx")
     everyone = lax.axis_size(axes)
@@ -292,11 +299,11 @@
         query_kernel,
         "remote_q",
         [f32((many, HEADS, BLOCK, HD)), f32((everyone, 1, width))] + [bf16(p.shape) for p in late],
-        [SMEM] + [VMEM] * 9 + [ANY] * len(late),
-        [pltpu.VMEM((1, width), jnp.float32)],
+        [VMEM] * 8 + [ANY] * len(late),
+        (),
         [VMEM] * 2 + [ANY] * len(late),
-        {10 + i: 2 + i for i in range(len(late))},
-    )(offsets, scaled, q, d, norm_cols, partial, *(got_kv[level] for level in ORDER), *late)
+        {8 + i: 2 + i for i in range(len(late))},
+    )(*picks, partial, *(got_kv[level] for level in ORDER), *late)
     got_qd.update(swap(dict(zip(LATE, late))))
     parts = lax.all_to_all(partial, axes, 0, 0, tiled=True)
     acc = pltpu.VMEM((tokens, width), jnp.float32)

time: 36.3 us -> 35.8 us (0.986)
  Pallas kernels: 7.86 us -> 7.25 us
    pallas_call x1, Pallas kernels: 1.87 us -> 1.33 us  [body(): call(query_kernel, 'remote_q', [f32((many, HEADS, BLOCK, HD)), f32((every...]
  transfers between devices with their start and end apart: 9 -> 9, of which waited for: 3 -> 3; matrix products, arithmetic and copies ran while one was open for 0% -> 0% of each run, Pallas kernels for 18% -> 17%
where the time goes in v11:
time: 35.8 us; the launch traced here: 35.6 us
  starting transfers between devices  21.8 us (61%)
  Pallas kernels  7.25 us (20%)
  waiting for transfers between devices  5.21 us (15%)
  other arithmetic  0.71 us (2%)
  between operations  0.67 us (2%)
    ppermute x8, starting transfers between devices, swap(): lax.ppermute(payload, 'ctx', [(i, i ^ half) for i in range(count)])  13.7 us
    all_to_all x1, starting transfers between devices, body(): parts = lax.all_to_all(partial, axes, 0, 0, tiled=True)  8.13 us
    ppermute x8, waiting for transfers between devices, swap(): lax.ppermute(payload, 'ctx', [(i, i ^ half) for i in range(count)])  3.08 us
    pallas_call x1, Pallas kernels, body(): call(most_kernel, 'most_kv', [bf16((tokens, width)), f32((tokens, width))...  2.22 us
    all_to_all x1, waiting for transfers between devices, body(): parts = lax.all_to_all(partial, axes, 0, 0, tiled=True)  2.13 us
    pallas_call x1, Pallas kernels, body(): call(query_kernel, 'remote_q', [f32((many, HEADS, BLOCK, HD)), f32((every...  1.33 us
    pallas_call x1, Pallas kernels, body(): call(pack_kernel, 'pack', [bf16((HEADS, 2 * BLOCK + (PARTS + EARLY) * (le...  1.33 us
    pallas_call x1, Pallas kernels, body(): call(last_kernel, 'last_kv', [bf16((tokens, width))] * 2, [SMEM] + [VMEM]...  1.3 us
  transfers between devices with their start and end apart: 9, of which 3 were waited for; matrix products, arithmetic and copies ran while one was open for 0% of the time, Pallas kernels for 17%

profile of v11, /device:TPU:1, one launch (start us, length us, event | category | flops | bytes accessed | tf_op | source)
XLA Modules:
  0.0 35.6 jit_solution(4756589008678438724)
XLA Ops:
  0.6 1.3 %pack.1 = (bf16[2,256,128]{2,1,0:T(8,128)(2,1)S(1)}, bf16[2,256,128]{2,1,0:T(8,128)(2,1)S(1)}, bf16[2,256,128]{2,1,0:T(8,128)(2,1)S(1)}, bf16[2,288,128]{2,1,0:T...) custom-call(s32[2,5]{1,0:T(2,128)} %offsets_in.1, ...), custom_call_target="tpu_custom_call" | custom-call | tf_op jit(solution)/shard_map/pack/pallas_call | solution.py:274
  2.0 4.5 %collective-permute-start = (bf16[2,288,128]{2,1,0:T(8,128)(2,1)S(1)}, bf16[2,288,128]{2,1,0:T(8,128)(2,1)S(1)}, u32[]{:S(2)}, u32[]{:S(2)}) collective-permute-start(bf16[2,288,128]{2,1,0:T(8,128)(2,1)S(1)} %get-tuple-element.46), channel_id=1, source_target_pairs={{0,8},{1,9},{2,10},{3,11},{4,12},{5,13},{6,14},{7,15},{8,0},{9,1},... | collective-permute-start | bytes 442376 | tf_op jit(solution)/shard_map/ppermute | solution.py:262
  6.5 1.2 %collective-permute-start.1 = (bf16[2,256,128]{2,1,0:T(8,128)(2,1)S(1)}, bf16[2,256,128]{2,1,0:T(8,128)(2,1)S(1)}, u32[]{:S(2)}, u32[]{:S(2)}) collective-permute-start(bf16[2,256,128]{2,1,0:T(8,128)(2,1)S(1)} %get-tuple-element.47), channel_id=1, source_target_pairs={{0,1},{1,0},{2,3},{3,2},{4,5},{5,4},{6,7},{7,6},{8,9},{9,8},{10,11... | collective-permute-start | bytes 393224 | tf_op jit(solution)/shard_map/ppermute | solution.py:262
  7.7 2.5 %collective-permute-start.2 = (bf16[2,256,128]{2,1,0:T(8,128)(2,1)S(1)}, bf16[2,256,128]{2,1,0:T(8,128)(2,1)S(1)}, u32[]{:S(2)}, u32[]{:S(2)}) collective-permute-start(bf16[2,256,128]{2,1,0:T(8,128)(2,1)S(1)} %get-tuple-element.48), channel_id=1, source_target_pairs={{0,2},{1,3},{2,0},{3,1},{4,6},{5,7},{6,4},{7,5},{8,10},{9,11},{10,... | collective-permute-start | bytes 393224 | tf_op jit(solution)/shard_map/ppermute | solution.py:262
  10.1 0.7 %collective-permute-start.3 = (bf16[2,256,128]{2,1,0:T(8,128)(2,1)S(1)}, bf16[2,256,128]{2,1,0:T(8,128)(2,1)S(1)}, u32[]{:S(2)}, u32[]{:S(2)}) collective-permute-start(bf16[2,256,128]{2,1,0:T(8,128)(2,1)S(1)} %get-tuple-element.49), channel_id=1, source_target_pairs={{0,4},{1,5},{2,6},{3,7},{4,0},{5,1},{6,2},{7,3},{8,12},{9,13},{10,... | collective-permute-start | bytes 393224 | tf_op jit(solution)/shard_map/ppermute | solution.py:262
  10.9 1.1 %local_q.1 = (f32[256,256]{1,0:T(8,128)S(1)}, bf16[256,256]{1,0:T(8,128)(2,1)S(1)}, f32[1,256]{1,0:T(1,128)S(1)}, bf16[3,4,2,128,128]{4,3,2,1,0:T(8,128)(2,1)S(1...) custom-call(s32[2,5]{1,0:T(2,128)S(1)} %get-tuple-element.33.offsets, ...), custom_call_target="tpu_custom_call" | custom-call | tf_op jit(solution)/shard_map/local_q/pallas_call | solution.py:285
  11.9 0.8 %collective-permute-start.4 = (bf16[2,272,128]{2,1,0:T(8,128)(2,1)S(1)}, bf16[2,272,128]{2,1,0:T(8,128)(2,1)S(1)}, u32[]{:S(2)}, u32[]{:S(2)}) collective-permute-start(bf16[2,272,128]{2,1,0:T(8,128)(2,1)S(1)} %get-tuple-element.52), channel_id=1, source_target_pairs={{0,4},{1,5},{2,6},{3,7},{4,0},{5,1},{6,2},{7,3},{8,12},{9,13},{10,... | collective-permute-start | bytes 417800 | tf_op jit(solution)/shard_map/ppermute | solution.py:262
  12.7 0.0 collective-permute-done.1.r2
  12.8 0.6 %collective-permute-start.5 = (bf16[2,272,128]{2,1,0:T(8,128)(2,1)S(1)}, bf16[2,272,128]{2,1,0:T(8,128)(2,1)S(1)}, u32[]{:S(2)}, u32[]{:S(2)}) collective-permute-start(bf16[2,272,128]{2,1,0:T(8,128)(2,1)S(1)} %get-tuple-element.53), channel_id=1, source_target_pairs={{0,2},{1,3},{2,0},{3,1},{4,6},{5,7},{6,4},{7,5},{8,10},{9,11},{10,... | collective-permute-start | bytes 417800 | tf_op jit(solution)/shard_map/ppermute | solution.py:262
  13.3 1.9 %collective-permute-done.2.r3 = bf16[2,256,128]{2,1,0:T(8,128)(2,1)S(1)} collective-permute-done((bf16[2,256,128]{2,1,0:T(8,128)(2,1)S(1)}, bf16[2,256,128]{2,1,0:T(8,128)(2,1)S(1)}, u32[]{:S(2)}, u32[]{:S(2)}) %collective-permute-start.2) | collective-permute-done | bytes 131104 | tf_op jit(solution)/shard_map/ppermute | solution.py:262
  15.2 0.0 collective-permute-start.6
  15.2 0.0 collective-permute-done.3.r4
  15.2 0.0 collective-permute-done.r1.refs_1_
  15.2 1.3 %remote_q.1 = (f32[4,2,128,128]{3,2,1,0:T(8,128)S(1)}, f32[128,1,256]{2,1,0:T(1,128)}, bf16[2,240,128]{2,1,0:T(8,128)(2,1)S(1)}) custom-call(bf16[3,4,2,128,128]{4,3,2,1,0:T(8,128)(2,1)S(1)} %get-tuple-element.42.picked, f32[4,2,128,128]{3,2,1,0:T(8,128)S(1)} %get-tuple-element.43.picked_norm, ...), custom_call_target="tpu_custom_call", output_to_operand_aliasing={{2}: (8, {})} | custom-call | tf_op jit(solution)/shard_map/remote_q/pallas_call | solution.py:298
  16.6 8.1 %all-to-all-start = ((f32[128,1,256]{2,1,0:T(1,128)}), f32[128,1,256]{2,1,0:T(1,128)S(1)}, u32[]{:S(2)}, u32[]{:S(2)}) async-start(f32[128,1,256]{2,1,0:T(1,128)} %get-tuple-element.61), calls=%async_computation | async-start | bytes 262144 | tf_op jit(solution)/shard_map/all_to_all | solution.py:308
  24.7 3.4 %collective-permute-start.7 = (bf16[2,240,128]{2,1,0:T(8,128)(2,1)S(1)}, bf16[2,240,128]{2,1,0:T(8,128)(2,1)S(1)}, u32[]{:S(2)}, u32[]{:S(2)}) collective-permute-start(bf16[2,240,128]{2,1,0:T(8,128)(2,1)S(1)} %get-tuple-element.58), channel_id=1, source_target_pairs={{0,8},{1,9},{2,10},{3,11},{4,12},{5,13},{6,14},{7,15},{8,0},{9,1},... | collective-permute-start | bytes 368648 | tf_op jit(solution)/shard_map/ppermute | solution.py:262
  28.1 0.0 collective-permute-done.4.refs_0_
  28.1 0.0 collective-permute-done.5.refs_1_
  28.1 0.0 collective-permute-done.6.refs_2_
  28.1 2.2 %most_kv.1 = (bf16[256,256]{1,0:T(8,128)(2,1)}, f32[256,256]{1,0:T(8,128)S(1)}, f32[256,256]{1,0:T(8,128)S(1)}) custom-call(s32[2,5]{1,0:T(2,128)S(1)} %get-tuple-element.33.offsets, f32[1,256]{1,0:T(1,128)S(1)} %get-tuple-element.34.gain, bf16[256,256]{1,0:T(8,128)(2,1)S(1)} %get-tuple-element.40.scaled, bf16[256,256]{1,0:T(8,128)(2,1)S(1)} %get-tuple-element.36.k, ...), custom_call_target="tpu_custom_call" | custom-call | tf_op jit(solution)/shard_map/most_kv/pallas_call | solution.py:310
  30.3 1.2 %collective-permute-done.7.refs_0_ = bf16[2,240,128]{2,1,0:T(8,128)(2,1)S(1)} collective-permute-done((bf16[2,240,128]{2,1,0:T(8,128)(2,1)S(1)}, bf16[2,240,128]{2,1,0:T(8,128)(2,1)S(1)}, u32[]{:S(2)}, u32[]{:S(2)}) %collective-permute-start.7) | collective-permute-done | bytes 122912 | tf_op jit(solution)/shard_map/ppermute | solution.py:262
  31.5 1.3 %last_kv.1 = (bf16[256,256]{1,0:T(8,128)(2,1)}, bf16[256,256]{1,0:T(8,128)(2,1)}) custom-call(s32[2,5]{1,0:T(2,128)S(1)} %get-tuple-element.33.offsets, f32[1,256]{1,0:T(1,128)S(1)} %get-tuple-element.34.gain, bf16[256,256]{1,0:T(8,128)(2,1)S(1)} %get-tuple-element.36.k, bf16[256,256]{1,0:T(8,128)(2,1)S(1)} %get-tuple-element.37.v, ...), custom_call_target="tpu_custom_call" | custom-call | tf_op jit(solution)/shard_map/last_kv/pallas_call | solution.py:317
  32.8 2.1 %all-to-all-done = f32[128,1,256]{2,1,0:T(1,128)S(1)} async-done(((f32[128,1,256]{2,1,0:T(1,128)}), f32[128,1,256]{2,1,0:T(1,128)S(1)}, u32[]{:S(2)}, u32[]{:S(2)}) %all-to-all-start) | async-done | bytes 131104 | tf_op jit(solution)/shard_map/all_to_all | solution.py:308
  34.9 0.7 %reduce_sum.9 = f32[256]{0:T(256)} reduce(f32[128,1,256]{2,1,0:T(1,128)S(1)} %all-to-all-done, f32[]{:T(128)} %constant.0.clone.1), dimensions={0,1}, to_apply=%region_0.0 | reduce | flops 32512 | bytes 132100 | tf_op jit(solution)/shard_map/reduce_sum | solution.py:320
Async XLA Ops:
  2.0 13.3 %collective-permute-start = (bf16[2,288,128]{2,1,0:T(8,128)(2,1)S(1)}, bf16[2,288,128]{2,1,0:T(8,128)(2,1)S(1)}, u32[]{:S(2)}, u32[]{:S(2)}) collective-permute-start(bf16[2,288,128]{2,1,0:T(8,128)(2,1)S(1)} %get-tuple-element.46), channel_id=1, source_target_pairs={{0,8},{1,9},{2,10},{3,11},{4,12},{5,13},{6,14},{7,15},{8,0},{9,1},... | collective-permute-start | bytes 442376 | tf_op jit(solution)/shard_map/ppermute | solution.py:262
  6.5 6.3 %collective-permute-start.1 = (bf16[2,256,128]{2,1,0:T(8,128)(2,1)S(1)}, bf16[2,256,128]{2,1,0:T(8,128)(2,1)S(1)}, u32[]{:S(2)}, u32[]{:S(2)}) collective-permute-start(bf16[2,256,128]{2,1,0:T(8,128)(2,1)S(1)} %get-tuple-element.47), channel_id=1, source_target_pairs={{0,1},{1,0},{2,3},{3,2},{4,5},{5,4},{6,7},{7,6},{8,9},{9,8},{10,11... | collective-permute-start | bytes 393224 | tf_op jit(solution)/shard_map/ppermute | solution.py:262
  7.7 7.5 %collective-permute-start.2 = (bf16[2,256,128]{2,1,0:T(8,128)(2,1)S(1)}, bf16[2,256,128]{2,1,0:T(8,128)(2,1)S(1)}, u32[]{:S(2)}, u32[]{:S(2)}) collective-permute-start(bf16[2,256,128]{2,1,0:T(8,128)(2,1)S(1)} %get-tuple-element.48), channel_id=1, source_target_pairs={{0,2},{1,3},{2,0},{3,1},{4,6},{5,7},{6,4},{7,5},{8,10},{9,11},{10,... | collective-permute-start | bytes 393224 | tf_op jit(solution)/shard_map/ppermute | solution.py:262
  10.1 5.1 %collective-permute-start.3 = (bf16[2,256,128]{2,1,0:T(8,128)(2,1)S(1)}, bf16[2,256,128]{2,1,0:T(8,128)(2,1)S(1)}, u32[]{:S(2)}, u32[]{:S(2)}) collective-permute-start(bf16[2,256,128]{2,1,0:T(8,128)(2,1)S(1)} %get-tuple-element.49), channel_id=1, source_target_pairs={{0,4},{1,5},{2,6},{3,7},{4,0},{5,1},{6,2},{7,3},{8,12},{9,13},{10,... | collective-permute-start | bytes 393224 | tf_op jit(solution)/shard_map/ppermute | solution.py:262
  11.9 16.1 %collective-permute-start.4 = (bf16[2,272,128]{2,1,0:T(8,128)(2,1)S(1)}, bf16[2,272,128]{2,1,0:T(8,128)(2,1)S(1)}, u32[]{:S(2)}, u32[]{:S(2)}) collective-permute-start(bf16[2,272,128]{2,1,0:T(8,128)(2,1)S(1)} %get-tuple-element.52), channel_id=1, source_target_pairs={{0,4},{1,5},{2,6},{3,7},{4,0},{5,1},{6,2},{7,3},{8,12},{9,13},{10,... | collective-permute-start | bytes 417800 | tf_op jit(solution)/shard_map/ppermute | solution.py:262
  12.8 15.3 %collective-permute-start.5 = (bf16[2,272,128]{2,1,0:T(8,128)(2,1)S(1)}, bf16[2,272,128]{2,1,0:T(8,128)(2,1)S(1)}, u32[]{:S(2)}, u32[]{:S(2)}) collective-permute-start(bf16[2,272,128]{2,1,0:T(8,128)(2,1)S(1)} %get-tuple-element.53), channel_id=1, source_target_pairs={{0,2},{1,3},{2,0},{3,1},{4,6},{5,7},{6,4},{7,5},{8,10},{9,11},{10,... | collective-permute-start | bytes 417800 | tf_op jit(solution)/shard_map/ppermute | solution.py:262
  15.2 12.8 %collective-permute-start.6 = (bf16[2,272,128]{2,1,0:T(8,128)(2,1)S(1)}, bf16[2,272,128]{2,1,0:T(8,128)(2,1)S(1)}, u32[]{:S(2)}, u32[]{:S(2)}) collective-permute-start(bf16[2,272,128]{2,1,0:T(8,128)(2,1)S(1)} %get-tuple-element.54), channel_id=1, source_target_pairs={{0,1},{1,0},{2,3},{3,2},{4,5},{5,4},{6,7},{7,6},{8,9},{9,8},{10,11... | collective-permute-start | bytes 417800 | tf_op jit(solution)/shard_map/ppermute | solution.py:262
  16.6 18.3 %all-to-all-start = ((f32[128,1,256]{2,1,0:T(1,128)}), f32[128,1,256]{2,1,0:T(1,128)S(1)}, u32[]{:S(2)}, u32[]{:S(2)}) async-start(f32[128,1,256]{2,1,0:T(1,128)} %get-tuple-element.61), calls=%async_computation | async-start | bytes 262144 | tf_op jit(solution)/shard_map/all_to_all | solution.py:308
  24.7 6.8 %collective-permute-start.7 = (bf16[2,240,128]{2,1,0:T(8,128)(2,1)S(1)}, bf16[2,240,128]{2,1,0:T(8,128)(2,1)S(1)}, u32[]{:S(2)}, u32[]{:S(2)}) collective-permute-start(bf16[2,240,128]{2,1,0:T(8,128)(2,1)S(1)} %get-tuple-element.58), channel_id=1, source_target_pairs={{0,8},{1,9},{2,10},{3,11},{4,12},{5,13},{6,14},{7,15},{8,0},{9,1},... | collective-permute-start | bytes 368648 | tf_op jit(solution)/shard_map/ppermute | solution.py:262

commit v12 on v11

--- a/solution.py
+++ b/solution.py
@@ -66,9 +66,12 @@
     for i, (source, target) in enumerate(moves):
         copies.append(pltpu.make_async_copy(source, target, sems.at[i]))
         copies[-1].start()
-    for copy in copies:
+    for copy in copies[:3]:
         copy.wait()
-    for level in range(1, LEVELS):
+    for level in sorted(range(1, LEVELS), key=LATE.count):
+        if level == LATE[0]:
+            for copy in copies[3:]:
+                copy.wait()
         first = firsts[level - 1]
         for head in range(HEADS):
             block, c = offsets[head, level] & 1, cols(head)
@@ -236,6 +239,10 @@
     )
     grad_k[...] = (dk[...] * SCALE).astype(jnp.bfloat16)
     grad_v[...] = dv[...].astype(jnp.bfloat16)
+
+
+def sum_kernel(parts, total):
+    total[...] = jnp.sum(parts[...], axis=0)
 
 
 def call(kernel, name, outs, in_specs, scratch=(), out_specs=None, aliases=None):
@@ -317,7 +324,8 @@
     grad_k, grad_v = call(
         last_kernel, "last_kv", [bf16((tokens, width))] * 2, [SMEM] + [VMEM] * (5 + 2 * len(LATE)), [acc, acc]
     )(offsets, gain, k, v, dk, dv, *(got_qd[level] for level in LATE), *(got_kv[level] for level in LATE))
-    return (grad_q[None], grad_k[None], grad_v[None], jnp.sum(parts, axis=(0, 1)))
+    (total,) = call(sum_kernel, "gain", [f32((1, width))], [VMEM])(parts)
+    return (grad_q[None], grad_k[None], grad_v[None], total.reshape(width))
 
 
 def solution(mesh):

time: 35.8 us -> 35.7 us (level)
  other arithmetic: 0.71 us -> 0 us
  Pallas kernels: 7.25 us -> 7.89 us
    reduce_sum x1 -> x0, other arithmetic: 0.71 us -> none  [body(): jnp.sum(parts, axis=(0, 1))]
    pallas_call x0 -> x1, Pallas kernels: none -> 0.71 us  [body(): total, = call(sum_kernel, 'gain', [f32((1, width))], [VMEM])(parts)]
where the time goes in v12:
time: 35.7 us; the launch traced here: 35.5 us
  starting transfers between devices  21.8 us (61%)
  Pallas kernels  7.89 us (22%)
  waiting for transfers between devices  5.22 us (15%)
  between operations  0.67 us (2%)
    ppermute x8, starting transfers between devices, swap(): lax.ppermute(payload, 'ctx', [(i, i ^ half) for i in range(count)])  13.7 us
    all_to_all x1, starting transfers between devices, body(): parts = lax.all_to_all(partial, axes, 0, 0, tiled=True)  8.12 us
    ppermute x8, waiting for transfers between devices, swap(): lax.ppermute(payload, 'ctx', [(i, i ^ half) for i in range(count)])  3.09 us
    pallas_call x1, Pallas kernels, body(): call(most_kernel, 'most_kv', [bf16((tokens, width)), f32((tokens, width))...  2.22 us
    all_to_all x1, waiting for transfers between devices, body(): parts = lax.all_to_all(partial, axes, 0, 0, tiled=True)  2.13 us
    pallas_call x1, Pallas kernels, body(): call(query_kernel, 'remote_q', [f32((many, HEADS, BLOCK, HD)), f32((every...  1.33 us
    pallas_call x1, Pallas kernels, body(): call(last_kernel, 'last_kv', [bf16((tokens, width))] * 2, [SMEM] + [VMEM]...  1.3 us
    pallas_call x1, Pallas kernels, body(): call(pack_kernel, 'pack', [bf16((HEADS, 2 * BLOCK + (PARTS + EARLY) * (le...  1.26 us
  transfers between devices with their start and end apart: 9, of which 3 were waited for; matrix products, arithmetic and copies ran while one was open for 0% of the time, Pallas kernels for 17%

profile of v12, /device:TPU:1, one launch (start us, length us, event | category | flops | bytes accessed | tf_op | source)
XLA Modules:
  0.0 35.5 jit_solution(15017999010060648529)
XLA Ops:
  0.6 1.3 %pack.1 = (bf16[2,256,128]{2,1,0:T(8,128)(2,1)S(1)}, bf16[2,256,128]{2,1,0:T(8,128)(2,1)S(1)}, bf16[2,256,128]{2,1,0:T(8,128)(2,1)S(1)}, bf16[2,288,128]{2,1,0:T...) custom-call(s32[2,5]{1,0:T(2,128)} %offsets_in.1, ...), custom_call_target="tpu_custom_call" | custom-call | tf_op jit(solution)/shard_map/pack/pallas_call | solution.py:281
  1.9 4.5 %collective-permute-start = (bf16[2,288,128]{2,1,0:T(8,128)(2,1)S(1)}, bf16[2,288,128]{2,1,0:T(8,128)(2,1)S(1)}, u32[]{:S(2)}, u32[]{:S(2)}) collective-permute-start(bf16[2,288,128]{2,1,0:T(8,128)(2,1)S(1)} %get-tuple-element.46), channel_id=1, source_target_pairs={{0,8},{1,9},{2,10},{3,11},{4,12},{5,13},{6,14},{7,15},{8,0},{9,1},... | collective-permute-start | bytes 442376 | tf_op jit(solution)/shard_map/ppermute | solution.py:269
  6.4 1.2 %collective-permute-start.1 = (bf16[2,256,128]{2,1,0:T(8,128)(2,1)S(1)}, bf16[2,256,128]{2,1,0:T(8,128)(2,1)S(1)}, u32[]{:S(2)}, u32[]{:S(2)}) collective-permute-start(bf16[2,256,128]{2,1,0:T(8,128)(2,1)S(1)} %get-tuple-element.47), channel_id=1, source_target_pairs={{0,1},{1,0},{2,3},{3,2},{4,5},{5,4},{6,7},{7,6},{8,9},{9,8},{10,11... | collective-permute-start | bytes 393224 | tf_op jit(solution)/shard_map/ppermute | solution.py:269
  7.6 2.5 %collective-permute-start.2 = (bf16[2,256,128]{2,1,0:T(8,128)(2,1)S(1)}, bf16[2,256,128]{2,1,0:T(8,128)(2,1)S(1)}, u32[]{:S(2)}, u32[]{:S(2)}) collective-permute-start(bf16[2,256,128]{2,1,0:T(8,128)(2,1)S(1)} %get-tuple-element.48), channel_id=1, source_target_pairs={{0,2},{1,3},{2,0},{3,1},{4,6},{5,7},{6,4},{7,5},{8,10},{9,11},{10,... | collective-permute-start | bytes 393224 | tf_op jit(solution)/shard_map/ppermute | solution.py:269
  10.1 0.7 %collective-permute-start.3 = (bf16[2,256,128]{2,1,0:T(8,128)(2,1)S(1)}, bf16[2,256,128]{2,1,0:T(8,128)(2,1)S(1)}, u32[]{:S(2)}, u32[]{:S(2)}) collective-permute-start(bf16[2,256,128]{2,1,0:T(8,128)(2,1)S(1)} %get-tuple-element.49), channel_id=1, source_target_pairs={{0,4},{1,5},{2,6},{3,7},{4,0},{5,1},{6,2},{7,3},{8,12},{9,13},{10,... | collective-permute-start | bytes 393224 | tf_op jit(solution)/shard_map/ppermute | solution.py:269
  10.8 1.1 %local_q.1 = (f32[256,256]{1,0:T(8,128)S(1)}, bf16[256,256]{1,0:T(8,128)(2,1)S(1)}, f32[1,256]{1,0:T(1,128)S(1)}, bf16[3,4,2,128,128]{4,3,2,1,0:T(8,128)(2,1)S(1...) custom-call(s32[2,5]{1,0:T(2,128)S(1)} %get-tuple-element.33.offsets, ...), custom_call_target="tpu_custom_call" | custom-call | tf_op jit(solution)/shard_map/local_q/pallas_call | solution.py:292
  11.9 0.8 %collective-permute-start.4 = (bf16[2,272,128]{2,1,0:T(8,128)(2,1)S(1)}, bf16[2,272,128]{2,1,0:T(8,128)(2,1)S(1)}, u32[]{:S(2)}, u32[]{:S(2)}) collective-permute-start(bf16[2,272,128]{2,1,0:T(8,128)(2,1)S(1)} %get-tuple-element.52), channel_id=1, source_target_pairs={{0,4},{1,5},{2,6},{3,7},{4,0},{5,1},{6,2},{7,3},{8,12},{9,13},{10,... | collective-permute-start | bytes 417800 | tf_op jit(solution)/shard_map/ppermute | solution.py:269
  12.7 0.0 collective-permute-done.1.r2
  12.7 0.6 %collective-permute-start.5 = (bf16[2,272,128]{2,1,0:T(8,128)(2,1)S(1)}, bf16[2,272,128]{2,1,0:T(8,128)(2,1)S(1)}, u32[]{:S(2)}, u32[]{:S(2)}) collective-permute-start(bf16[2,272,128]{2,1,0:T(8,128)(2,1)S(1)} %get-tuple-element.53), channel_id=1, source_target_pairs={{0,2},{1,3},{2,0},{3,1},{4,6},{5,7},{6,4},{7,5},{8,10},{9,11},{10,... | collective-permute-start | bytes 417800 | tf_op jit(solution)/shard_map/ppermute | solution.py:269
  13.3 1.9 %collective-permute-done.2.r3 = bf16[2,256,128]{2,1,0:T(8,128)(2,1)S(1)} collective-permute-done((bf16[2,256,128]{2,1,0:T(8,128)(2,1)S(1)}, bf16[2,256,128]{2,1,0:T(8,128)(2,1)S(1)}, u32[]{:S(2)}, u32[]{:S(2)}) %collective-permute-start.2) | collective-permute-done | bytes 131104 | tf_op jit(solution)/shard_map/ppermute | solution.py:269
  15.2 0.0 collective-permute-start.6
  15.2 0.0 collective-permute-done.3.r4
  15.2 0.0 collective-permute-done.r1.refs_1_
  15.2 1.3 %remote_q.1 = (f32[4,2,128,128]{3,2,1,0:T(8,128)S(1)}, f32[128,1,256]{2,1,0:T(1,128)}, bf16[2,240,128]{2,1,0:T(8,128)(2,1)S(1)}) custom-call(bf16[3,4,2,128,128]{4,3,2,1,0:T(8,128)(2,1)S(1)} %get-tuple-element.42.picked, f32[4,2,128,128]{3,2,1,0:T(8,128)S(1)} %get-tuple-element.43.picked_norm, ...), custom_call_target="tpu_custom_call", output_to_operand_aliasing={{2}: (8, {})} | custom-call | tf_op jit(solution)/shard_map/remote_q/pallas_call | solution.py:305
  16.5 8.1 %all-to-all-start = ((f32[128,1,256]{2,1,0:T(1,128)}), f32[128,1,256]{2,1,0:T(1,128)S(1)}, u32[]{:S(2)}, u32[]{:S(2)}) async-start(f32[128,1,256]{2,1,0:T(1,128)} %get-tuple-element.61), calls=%async_computation | async-start | bytes 262144 | tf_op jit(solution)/shard_map/all_to_all | solution.py:315
  24.6 3.4 %collective-permute-start.7 = (bf16[2,240,128]{2,1,0:T(8,128)(2,1)S(1)}, bf16[2,240,128]{2,1,0:T(8,128)(2,1)S(1)}, u32[]{:S(2)}, u32[]{:S(2)}) collective-permute-start(bf16[2,240,128]{2,1,0:T(8,128)(2,1)S(1)} %get-tuple-element.58), channel_id=1, source_target_pairs={{0,8},{1,9},{2,10},{3,11},{4,12},{5,13},{6,14},{7,15},{8,0},{9,1},... | collective-permute-start | bytes 368648 | tf_op jit(solution)/shard_map/ppermute | solution.py:269
  28.0 0.0 collective-permute-done.4.refs_0_
  28.0 0.0 collective-permute-done.5.refs_1_
  28.0 0.0 collective-permute-done.6.refs_2_
  28.0 2.2 %most_kv.1 = (bf16[256,256]{1,0:T(8,128)(2,1)}, f32[256,256]{1,0:T(8,128)S(1)}, f32[256,256]{1,0:T(8,128)S(1)}) custom-call(s32[2,5]{1,0:T(2,128)S(1)} %get-tuple-element.33.offsets, f32[1,256]{1,0:T(1,128)S(1)} %get-tuple-element.34.gain, bf16[256,256]{1,0:T(8,128)(2,1)S(1)} %get-tuple-element.40.scaled, bf16[256,256]{1,0:T(8,128)(2,1)S(1)} %get-tuple-element.36.k, ...), custom_call_target="tpu_custom_call" | custom-call | tf_op jit(solution)/shard_map/most_kv/pallas_call | solution.py:317
  30.2 1.2 %collective-permute-done.7.refs_0_ = bf16[2,240,128]{2,1,0:T(8,128)(2,1)S(1)} collective-permute-done((bf16[2,240,128]{2,1,0:T(8,128)(2,1)S(1)}, bf16[2,240,128]{2,1,0:T(8,128)(2,1)S(1)}, u32[]{:S(2)}, u32[]{:S(2)}) %collective-permute-start.7) | collective-permute-done | bytes 122912 | tf_op jit(solution)/shard_map/ppermute | solution.py:269
  31.4 1.3 %last_kv.1 = (bf16[256,256]{1,0:T(8,128)(2,1)}, bf16[256,256]{1,0:T(8,128)(2,1)}) custom-call(s32[2,5]{1,0:T(2,128)S(1)} %get-tuple-element.33.offsets, f32[1,256]{1,0:T(1,128)S(1)} %get-tuple-element.34.gain, bf16[256,256]{1,0:T(8,128)(2,1)S(1)} %get-tuple-element.36.k, bf16[256,256]{1,0:T(8,128)(2,1)S(1)} %get-tuple-element.37.v, ...), custom_call_target="tpu_custom_call" | custom-call | tf_op jit(solution)/shard_map/last_kv/pallas_call | solution.py:324
  32.7 2.1 %all-to-all-done.parts = f32[128,1,256]{2,1,0:T(1,128)S(1)} async-done(((f32[128,1,256]{2,1,0:T(1,128)}), f32[128,1,256]{2,1,0:T(1,128)S(1)}, u32[]{:S(2)}, u32[]{:S(2)}) %all-to-all-start) | async-done | bytes 131104 | tf_op jit(solution)/shard_map/all_to_all | solution.py:315
  34.8 0.7 %gain.1 = f32[1,256]{1,0:T(1,128)} custom-call(f32[128,1,256]{2,1,0:T(1,128)S(1)} %all-to-all-done.parts), custom_call_target="tpu_custom_call" | custom-call | tf_op jit(solution)/shard_map/gain/pallas_call | solution.py:327
Async XLA Ops:
  1.9 13.3 %collective-permute-start = (bf16[2,288,128]{2,1,0:T(8,128)(2,1)S(1)}, bf16[2,288,128]{2,1,0:T(8,128)(2,1)S(1)}, u32[]{:S(2)}, u32[]{:S(2)}) collective-permute-start(bf16[2,288,128]{2,1,0:T(8,128)(2,1)S(1)} %get-tuple-element.46), channel_id=1, source_target_pairs={{0,8},{1,9},{2,10},{3,11},{4,12},{5,13},{6,14},{7,15},{8,0},{9,1},... | collective-permute-start | bytes 442376 | tf_op jit(solution)/shard_map/ppermute | solution.py:269
  6.4 6.3 %collective-permute-start.1 = (bf16[2,256,128]{2,1,0:T(8,128)(2,1)S(1)}, bf16[2,256,128]{2,1,0:T(8,128)(2,1)S(1)}, u32[]{:S(2)}, u32[]{:S(2)}) collective-permute-start(bf16[2,256,128]{2,1,0:T(8,128)(2,1)S(1)} %get-tuple-element.47), channel_id=1, source_target_pairs={{0,1},{1,0},{2,3},{3,2},{4,5},{5,4},{6,7},{7,6},{8,9},{9,8},{10,11... | collective-permute-start | bytes 393224 | tf_op jit(solution)/shard_map/ppermute | solution.py:269
  7.6 7.5 %collective-permute-start.2 = (bf16[2,256,128]{2,1,0:T(8,128)(2,1)S(1)}, bf16[2,256,128]{2,1,0:T(8,128)(2,1)S(1)}, u32[]{:S(2)}, u32[]{:S(2)}) collective-permute-start(bf16[2,256,128]{2,1,0:T(8,128)(2,1)S(1)} %get-tuple-element.48), channel_id=1, source_target_pairs={{0,2},{1,3},{2,0},{3,1},{4,6},{5,7},{6,4},{7,5},{8,10},{9,11},{10,... | collective-permute-start | bytes 393224 | tf_op jit(solution)/shard_map/ppermute | solution.py:269
  10.1 5.1 %collective-permute-start.3 = (bf16[2,256,128]{2,1,0:T(8,128)(2,1)S(1)}, bf16[2,256,128]{2,1,0:T(8,128)(2,1)S(1)}, u32[]{:S(2)}, u32[]{:S(2)}) collective-permute-start(bf16[2,256,128]{2,1,0:T(8,128)(2,1)S(1)} %get-tuple-element.49), channel_id=1, source_target_pairs={{0,4},{1,5},{2,6},{3,7},{4,0},{5,1},{6,2},{7,3},{8,12},{9,13},{10,... | collective-permute-start | bytes 393224 | tf_op jit(solution)/shard_map/ppermute | solution.py:269
  11.9 16.1 %collective-permute-start.4 = (bf16[2,272,128]{2,1,0:T(8,128)(2,1)S(1)}, bf16[2,272,128]{2,1,0:T(8,128)(2,1)S(1)}, u32[]{:S(2)}, u32[]{:S(2)}) collective-permute-start(bf16[2,272,128]{2,1,0:T(8,128)(2,1)S(1)} %get-tuple-element.52), channel_id=1, source_target_pairs={{0,4},{1,5},{2,6},{3,7},{4,0},{5,1},{6,2},{7,3},{8,12},{9,13},{10,... | collective-permute-start | bytes 417800 | tf_op jit(solution)/shard_map/ppermute | solution.py:269
  12.7 15.3 %collective-permute-start.5 = (bf16[2,272,128]{2,1,0:T(8,128)(2,1)S(1)}, bf16[2,272,128]{2,1,0:T(8,128)(2,1)S(1)}, u32[]{:S(2)}, u32[]{:S(2)}) collective-permute-start(bf16[2,272,128]{2,1,0:T(8,128)(2,1)S(1)} %get-tuple-element.53), channel_id=1, source_target_pairs={{0,2},{1,3},{2,0},{3,1},{4,6},{5,7},{6,4},{7,5},{8,10},{9,11},{10,... | collective-permute-start | bytes 417800 | tf_op jit(solution)/shard_map/ppermute | solution.py:269
  15.2 12.8 %collective-permute-start.6 = (bf16[2,272,128]{2,1,0:T(8,128)(2,1)S(1)}, bf16[2,272,128]{2,1,0:T(8,128)(2,1)S(1)}, u32[]{:S(2)}, u32[]{:S(2)}) collective-permute-start(bf16[2,272,128]{2,1,0:T(8,128)(2,1)S(1)} %get-tuple-element.54), channel_id=1, source_target_pairs={{0,1},{1,0},{2,3},{3,2},{4,5},{5,4},{6,7},{7,6},{8,9},{9,8},{10,11... | collective-permute-start | bytes 417800 | tf_op jit(solution)/shard_map/ppermute | solution.py:269
  16.5 18.3 %all-to-all-start = ((f32[128,1,256]{2,1,0:T(1,128)}), f32[128,1,256]{2,1,0:T(1,128)S(1)}, u32[]{:S(2)}, u32[]{:S(2)}) async-start(f32[128,1,256]{2,1,0:T(1,128)} %get-tuple-element.61), calls=%async_computation | async-start | bytes 262144 | tf_op jit(solution)/shard_map/all_to_all | solution.py:315
  24.6 6.8 %collective-permute-start.7 = (bf16[2,240,128]{2,1,0:T(8,128)(2,1)S(1)}, bf16[2,240,128]{2,1,0:T(8,128)(2,1)S(1)}, u32[]{:S(2)}, u32[]{:S(2)}) collective-permute-start(bf16[2,240,128]{2,1,0:T(8,128)(2,1)S(1)} %get-tuple-element.58), channel_id=1, source_target_pairs={{0,8},{1,9},{2,10},{3,11},{4,12},{5,13},{6,14},{7,15},{8,0},{9,1},... | collective-permute-start | bytes 368648 | tf_op jit(solution)/shard_map/ppermute | solution.py:269

commit v13 on v12

--- a/solution.py
+++ b/solution.py
@@ -12,6 +12,7 @@
 HEADS = 2
 HD = 128
 SCALE = HD**-0.5
+LOG2E = 1.4426950408889634
 LATE, EARLY, PARTS = (4,), 16, 16
 
 HBM = pl.BlockSpec(memory_space=pltpu.HBM)
@@ -129,7 +130,7 @@
         for level in range(1, LEVELS):
             active, block = place(offsets, me, head, level)
             at = block_rows(block)
-            picked_norm[level - 1, head] = jnp.where(block == 0, column[:BLOCK], column[BLOCK:])
+            picked_norm[level - 1, head] = jnp.where(block == 0, column[:BLOCK], column[BLOCK:]) * LOG2E
             for i, source in enumerate((scaled, q, d)):
                 picked[i, level - 1, head] = source[at, c]
             flags = jnp.where((row == HEADS * (level - 1) + head) & active, 1.0, flags)
@@ -172,7 +173,7 @@
         products.append((scores, dot(picked[2, n, head], got[head, BLOCK : 2 * BLOCK], NT)))
     grads = []
     for (level, head), (scores, pull) in zip(spots, products):
-        probs = jnp.exp(scores * SCALE - picked_norm[level - 1, head])
+        probs = jnp.exp2(scores * (SCALE * LOG2E) - picked_norm[level - 1, head])
         grads.append((probs * pull).astype(jnp.bfloat16))
     mores = [dot(grad, received[level][head, :BLOCK], NN) for (level, head), grad in zip(spots, grads)]
     sums = [partial_in[:, cols(head)] for head in range(HEADS)]

time: 35.7 us -> 35.7 us (level)
  Pallas kernels: 7.89 us -> 9.38 us
  waiting for transfers between devices: 5.22 us -> 3.73 us
    ppermute x8, waiting for transfers between devices: 3.09 us -> 2.09 us  [swap(): lax.ppermute(payload, 'ctx', [(i, i ^ half) for i in range(count)])]
    pallas_call x1, Pallas kernels: 2.22 us -> 3.22 us  [body(): call(most_kernel, 'most_kv', [bf16((tokens, width)), f32((tokens, width))...]
    all_to_all x1, waiting for transfers between devices: 2.13 us -> 1.64 us  [body(): parts = lax.all_to_all(partial, axes, 0, 0, tiled=True)]
    pallas_call x1, Pallas kernels: 1.3 us -> 1.79 us  [body(): call(last_kernel, 'last_kv', [bf16((tokens, width))] * 2, [SMEM] + [VMEM]...]
  transfers between devices with their start and end apart: 9 -> 9, of which waited for: 3 -> 3; matrix products, arithmetic and copies ran while one was open for 0% -> 0% of each run, Pallas kernels for 17% -> 21%
where the time goes in v13:
time: 35.7 us; the launch traced here: 35.5 us
  starting transfers between devices  21.8 us (61%)
  Pallas kernels  9.38 us (26%)
  waiting for transfers between devices  3.73 us (10%)
  between operations  0.67 us (2%)
    ppermute x8, starting transfers between devices, swap(): lax.ppermute(payload, 'ctx', [(i, i ^ half) for i in range(count)])  13.7 us
    all_to_all x1, starting transfers between devices, body(): parts = lax.all_to_all(partial, axes, 0, 0, tiled=True)  8.12 us
    pallas_call x1, Pallas kernels, body(): call(most_kernel, 'most_kv', [bf16((tokens, width)), f32((tokens, width))...  3.22 us
    ppermute x8, waiting for transfers between devices, swap(): lax.ppermute(payload, 'ctx', [(i, i ^ half) for i in range(count)])  2.09 us
    pallas_call x1, Pallas kernels, body(): call(last_kernel, 'last_kv', [bf16((tokens, width))] * 2, [SMEM] + [VMEM]...  1.79 us
    all_to_all x1, waiting for transfers between devices, body(): parts = lax.all_to_all(partial, axes, 0, 0, tiled=True)  1.64 us
    pallas_call x1, Pallas kernels, body(): call(query_kernel, 'remote_q', [f32((many, HEADS, BLOCK, HD)), f32((every...  1.33 us
    pallas_call x1, Pallas kernels, body(): call(pack_kernel, 'pack', [bf16((HEADS, 2 * BLOCK + (PARTS + EARLY) * (le...  1.26 us
  transfers between devices with their start and end apart: 9, of which 3 were waited for; matrix products, arithmetic and copies ran while one was open for 0% of the time, Pallas kernels for 21%

profile of v13, /device:TPU:1, one launch (start us, length us, event | category | flops | bytes accessed | tf_op | source)
XLA Modules:
  0.0 35.5 jit_solution(4810078719902796649)
XLA Ops:
  0.6 1.3 %pack.1 = (bf16[2,256,128]{2,1,0:T(8,128)(2,1)S(1)}, bf16[2,256,128]{2,1,0:T(8,128)(2,1)S(1)}, bf16[2,256,128]{2,1,0:T(8,128)(2,1)S(1)}, bf16[2,288,128]{2,1,0:T...) custom-call(s32[2,5]{1,0:T(2,128)} %offsets_in.1, ...), custom_call_target="tpu_custom_call" | custom-call | tf_op jit(solution)/shard_map/pack/pallas_call | solution.py:282
  1.9 4.5 %collective-permute-start = (bf16[2,288,128]{2,1,0:T(8,128)(2,1)S(1)}, bf16[2,288,128]{2,1,0:T(8,128)(2,1)S(1)}, u32[]{:S(2)}, u32[]{:S(2)}) collective-permute-start(bf16[2,288,128]{2,1,0:T(8,128)(2,1)S(1)} %get-tuple-element.46), channel_id=1, source_target_pairs={{0,8},{1,9},{2,10},{3,11},{4,12},{5,13},{6,14},{7,15},{8,0},{9,1},... | collective-permute-start | bytes 442376 | tf_op jit(solution)/shard_map/ppermute | solution.py:270
  6.4 1.2 %collective-permute-start.1 = (bf16[2,256,128]{2,1,0:T(8,128)(2,1)S(1)}, bf16[2,256,128]{2,1,0:T(8,128)(2,1)S(1)}, u32[]{:S(2)}, u32[]{:S(2)}) collective-permute-start(bf16[2,256,128]{2,1,0:T(8,128)(2,1)S(1)} %get-tuple-element.47), channel_id=1, source_target_pairs={{0,1},{1,0},{2,3},{3,2},{4,5},{5,4},{6,7},{7,6},{8,9},{9,8},{10,11... | collective-permute-start | bytes 393224 | tf_op jit(solution)/shard_map/ppermute | solution.py:270
  7.6 2.5 %collective-permute-start.2 = (bf16[2,256,128]{2,1,0:T(8,128)(2,1)S(1)}, bf16[2,256,128]{2,1,0:T(8,128)(2,1)S(1)}, u32[]{:S(2)}, u32[]{:S(2)}) collective-permute-start(bf16[2,256,128]{2,1,0:T(8,128)(2,1)S(1)} %get-tuple-element.48), channel_id=1, source_target_pairs={{0,2},{1,3},{2,0},{3,1},{4,6},{5,7},{6,4},{7,5},{8,10},{9,11},{10,... | collective-permute-start | bytes 393224 | tf_op jit(solution)/shard_map/ppermute | solution.py:270
  10.1 0.7 %collective-permute-start.3 = (bf16[2,256,128]{2,1,0:T(8,128)(2,1)S(1)}, bf16[2,256,128]{2,1,0:T(8,128)(2,1)S(1)}, u32[]{:S(2)}, u32[]{:S(2)}) collective-permute-start(bf16[2,256,128]{2,1,0:T(8,128)(2,1)S(1)} %get-tuple-element.49), channel_id=1, source_target_pairs={{0,4},{1,5},{2,6},{3,7},{4,0},{5,1},{6,2},{7,3},{8,12},{9,13},{10,... | collective-permute-start | bytes 393224 | tf_op jit(solution)/shard_map/ppermute | solution.py:270
  10.8 1.1 %local_q.1 = (f32[256,256]{1,0:T(8,128)S(1)}, bf16[256,256]{1,0:T(8,128)(2,1)S(1)}, f32[1,256]{1,0:T(1,128)S(1)}, bf16[3,4,2,128,128]{4,3,2,1,0:T(8,128)(2,1)S(1...) custom-call(s32[2,5]{1,0:T(2,128)S(1)} %get-tuple-element.33.offsets, ...), custom_call_target="tpu_custom_call" | custom-call | tf_op jit(solution)/shard_map/local_q/pallas_call | solution.py:293
  11.9 0.8 %collective-permute-start.4 = (bf16[2,272,128]{2,1,0:T(8,128)(2,1)S(1)}, bf16[2,272,128]{2,1,0:T(8,128)(2,1)S(1)}, u32[]{:S(2)}, u32[]{:S(2)}) collective-permute-start(bf16[2,272,128]{2,1,0:T(8,128)(2,1)S(1)} %get-tuple-element.52), channel_id=1, source_target_pairs={{0,4},{1,5},{2,6},{3,7},{4,0},{5,1},{6,2},{7,3},{8,12},{9,13},{10,... | collective-permute-start | bytes 417800 | tf_op jit(solution)/shard_map/ppermute | solution.py:270
  12.7 0.0 collective-permute-done.1.r2
  12.7 0.6 %collective-permute-start.5 = (bf16[2,272,128]{2,1,0:T(8,128)(2,1)S(1)}, bf16[2,272,128]{2,1,0:T(8,128)(2,1)S(1)}, u32[]{:S(2)}, u32[]{:S(2)}) collective-permute-start(bf16[2,272,128]{2,1,0:T(8,128)(2,1)S(1)} %get-tuple-element.53), channel_id=1, source_target_pairs={{0,2},{1,3},{2,0},{3,1},{4,6},{5,7},{6,4},{7,5},{8,10},{9,11},{10,... | collective-permute-start | bytes 417800 | tf_op jit(solution)/shard_map/ppermute | solution.py:270
  13.3 1.9 %collective-permute-done.2.r3 = bf16[2,256,128]{2,1,0:T(8,128)(2,1)S(1)} collective-permute-done((bf16[2,256,128]{2,1,0:T(8,128)(2,1)S(1)}, bf16[2,256,128]{2,1,0:T(8,128)(2,1)S(1)}, u32[]{:S(2)}, u32[]{:S(2)}) %collective-permute-start.2) | collective-permute-done | bytes 131104 | tf_op jit(solution)/shard_map/ppermute | solution.py:270
  15.2 0.0 collective-permute-start.6
  15.2 0.0 collective-permute-done.3.r4
  15.2 0.0 collective-permute-done.r1.refs_1_
  15.2 1.3 %remote_q.1 = (f32[4,2,128,128]{3,2,1,0:T(8,128)S(1)}, f32[128,1,256]{2,1,0:T(1,128)}, bf16[2,240,128]{2,1,0:T(8,128)(2,1)S(1)}) custom-call(bf16[3,4,2,128,128]{4,3,2,1,0:T(8,128)(2,1)S(1)} %get-tuple-element.42.picked, f32[4,2,128,128]{3,2,1,0:T(8,128)S(1)} %get-tuple-element.43.picked_norm, ...), custom_call_target="tpu_custom_call", output_to_operand_aliasing={{2}: (8, {})} | custom-call | tf_op jit(solution)/shard_map/remote_q/pallas_call | solution.py:306
  16.5 8.1 %all-to-all-start = ((f32[128,1,256]{2,1,0:T(1,128)}), f32[128,1,256]{2,1,0:T(1,128)S(1)}, u32[]{:S(2)}, u32[]{:S(2)}) async-start(f32[128,1,256]{2,1,0:T(1,128)} %get-tuple-element.61), calls=%async_computation | async-start | bytes 262144 | tf_op jit(solution)/shard_map/all_to_all | solution.py:316
  24.6 3.4 %collective-permute-start.7 = (bf16[2,240,128]{2,1,0:T(8,128)(2,1)S(1)}, bf16[2,240,128]{2,1,0:T(8,128)(2,1)S(1)}, u32[]{:S(2)}, u32[]{:S(2)}) collective-permute-start(bf16[2,240,128]{2,1,0:T(8,128)(2,1)S(1)} %get-tuple-element.58), channel_id=1, source_target_pairs={{0,8},{1,9},{2,10},{3,11},{4,12},{5,13},{6,14},{7,15},{8,0},{9,1},... | collective-permute-start | bytes 368648 | tf_op jit(solution)/shard_map/ppermute | solution.py:270
  28.0 0.0 collective-permute-done.4.refs_0_
  28.0 0.0 collective-permute-done.5.refs_1_
  28.0 0.0 collective-permute-done.6.refs_2_
  28.0 3.2 %most_kv.1 = (bf16[256,256]{1,0:T(8,128)(2,1)}, f32[256,256]{1,0:T(8,128)S(1)}, f32[256,256]{1,0:T(8,128)S(1)}) custom-call(s32[2,5]{1,0:T(2,128)S(1)} %get-tuple-element.33.offsets, f32[1,256]{1,0:T(1,128)S(1)} %get-tuple-element.34.gain, bf16[256,256]{1,0:T(8,128)(2,1)S(1)} %get-tuple-element.40.scaled, bf16[256,256]{1,0:T(8,128)(2,1)S(1)} %get-tuple-element.36.k, ...), custom_call_target="tpu_custom_call" | custom-call | tf_op jit(solution)/shard_map/most_kv/pallas_call | solution.py:318
  31.2 0.2 collective-permute-done.7.refs_0_
  31.4 1.8 %last_kv.1 = (bf16[256,256]{1,0:T(8,128)(2,1)}, bf16[256,256]{1,0:T(8,128)(2,1)}) custom-call(s32[2,5]{1,0:T(2,128)S(1)} %get-tuple-element.33.offsets, f32[1,256]{1,0:T(1,128)S(1)} %get-tuple-element.34.gain, bf16[256,256]{1,0:T(8,128)(2,1)S(1)} %get-tuple-element.36.k, bf16[256,256]{1,0:T(8,128)(2,1)S(1)} %get-tuple-element.37.v, ...), custom_call_target="tpu_custom_call" | custom-call | tf_op jit(solution)/shard_map/last_kv/pallas_call | solution.py:325
  33.2 1.6 %all-to-all-done.parts = f32[128,1,256]{2,1,0:T(1,128)S(1)} async-done(((f32[128,1,256]{2,1,0:T(1,128)}), f32[128,1,256]{2,1,0:T(1,128)S(1)}, u32[]{:S(2)}, u32[]{:S(2)}) %all-to-all-start) | async-done | bytes 131104 | tf_op jit(solution)/shard_map/all_to_all | solution.py:316
  34.8 0.7 %gain.1 = f32[1,256]{1,0:T(1,128)} custom-call(f32[128,1,256]{2,1,0:T(1,128)S(1)} %all-to-all-done.parts), custom_call_target="tpu_custom_call" | custom-call | tf_op jit(solution)/shard_map/gain/pallas_call | solution.py:328
Async XLA Ops:
  1.9 13.3 %collective-permute-start = (bf16[2,288,128]{2,1,0:T(8,128)(2,1)S(1)}, bf16[2,288,128]{2,1,0:T(8,128)(2,1)S(1)}, u32[]{:S(2)}, u32[]{:S(2)}) collective-permute-start(bf16[2,288,128]{2,1,0:T(8,128)(2,1)S(1)} %get-tuple-element.46), channel_id=1, source_target_pairs={{0,8},{1,9},{2,10},{3,11},{4,12},{5,13},{6,14},{7,15},{8,0},{9,1},... | collective-permute-start | bytes 442376 | tf_op jit(solution)/shard_map/ppermute | solution.py:270
  6.4 6.3 %collective-permute-start.1 = (bf16[2,256,128]{2,1,0:T(8,128)(2,1)S(1)}, bf16[2,256,128]{2,1,0:T(8,128)(2,1)S(1)}, u32[]{:S(2)}, u32[]{:S(2)}) collective-permute-start(bf16[2,256,128]{2,1,0:T(8,128)(2,1)S(1)} %get-tuple-element.47), channel_id=1, source_target_pairs={{0,1},{1,0},{2,3},{3,2},{4,5},{5,4},{6,7},{7,6},{8,9},{9,8},{10,11... | collective-permute-start | bytes 393224 | tf_op jit(solution)/shard_map/ppermute | solution.py:270
  7.6 7.5 %collective-permute-start.2 = (bf16[2,256,128]{2,1,0:T(8,128)(2,1)S(1)}, bf16[2,256,128]{2,1,0:T(8,128)(2,1)S(1)}, u32[]{:S(2)}, u32[]{:S(2)}) collective-permute-start(bf16[2,256,128]{2,1,0:T(8,128)(2,1)S(1)} %get-tuple-element.48), channel_id=1, source_target_pairs={{0,2},{1,3},{2,0},{3,1},{4,6},{5,7},{6,4},{7,5},{8,10},{9,11},{10,... | collective-permute-start | bytes 393224 | tf_op jit(solution)/shard_map/ppermute | solution.py:270
  10.1 5.1 %collective-permute-start.3 = (bf16[2,256,128]{2,1,0:T(8,128)(2,1)S(1)}, bf16[2,256,128]{2,1,0:T(8,128)(2,1)S(1)}, u32[]{:S(2)}, u32[]{:S(2)}) collective-permute-start(bf16[2,256,128]{2,1,0:T(8,128)(2,1)S(1)} %get-tuple-element.49), channel_id=1, source_target_pairs={{0,4},{1,5},{2,6},{3,7},{4,0},{5,1},{6,2},{7,3},{8,12},{9,13},{10,... | collective-permute-start | bytes 393224 | tf_op jit(solution)/shard_map/ppermute | solution.py:270
  11.9 16.1 %collective-permute-start.4 = (bf16[2,272,128]{2,1,0:T(8,128)(2,1)S(1)}, bf16[2,272,128]{2,1,0:T(8,128)(2,1)S(1)}, u32[]{:S(2)}, u32[]{:S(2)}) collective-permute-start(bf16[2,272,128]{2,1,0:T(8,128)(2,1)S(1)} %get-tuple-element.52), channel_id=1, source_target_pairs={{0,4},{1,5},{2,6},{3,7},{4,0},{5,1},{6,2},{7,3},{8,12},{9,13},{10,... | collective-permute-start | bytes 417800 | tf_op jit(solution)/shard_map/ppermute | solution.py:270
  12.7 15.3 %collective-permute-start.5 = (bf16[2,272,128]{2,1,0:T(8,128)(2,1)S(1)}, bf16[2,272,128]{2,1,0:T(8,128)(2,1)S(1)}, u32[]{:S(2)}, u32[]{:S(2)}) collective-permute-start(bf16[2,272,128]{2,1,0:T(8,128)(2,1)S(1)} %get-tuple-element.53), channel_id=1, source_target_pairs={{0,2},{1,3},{2,0},{3,1},{4,6},{5,7},{6,4},{7,5},{8,10},{9,11},{10,... | collective-permute-start | bytes 417800 | tf_op jit(solution)/shard_map/ppermute | solution.py:270
  15.2 12.8 %collective-permute-start.6 = (bf16[2,272,128]{2,1,0:T(8,128)(2,1)S(1)}, bf16[2,272,128]{2,1,0:T(8,128)(2,1)S(1)}, u32[]{:S(2)}, u32[]{:S(2)}) collective-permute-start(bf16[2,272,128]{2,1,0:T(8,128)(2,1)S(1)} %get-tuple-element.54), channel_id=1, source_target_pairs={{0,1},{1,0},{2,3},{3,2},{4,5},{5,4},{6,7},{7,6},{8,9},{9,8},{10,11... | collective-permute-start | bytes 417800 | tf_op jit(solution)/shard_map/ppermute | solution.py:270
  16.5 18.3 %all-to-all-start = ((f32[128,1,256]{2,1,0:T(1,128)}), f32[128,1,256]{2,1,0:T(1,128)S(1)}, u32[]{:S(2)}, u32[]{:S(2)}) async-start(f32[128,1,256]{2,1,0:T(1,128)} %get-tuple-element.61), calls=%async_computation | async-start | bytes 262144 | tf_op jit(solution)/shard_map/all_to_all | solution.py:316
  24.6 6.8 %collective-permute-start.7 = (bf16[2,240,128]{2,1,0:T(8,128)(2,1)S(1)}, bf16[2,240,128]{2,1,0:T(8,128)(2,1)S(1)}, u32[]{:S(2)}, u32[]{:S(2)}) collective-permute-start(bf16[2,240,128]{2,1,0:T(8,128)(2,1)S(1)} %get-tuple-element.58), channel_id=1, source_target_pairs={{0,8},{1,9},{2,10},{3,11},{4,12},{5,13},{6,14},{7,15},{8,0},{9,1},... | collective-permute-start | bytes 368648 | tf_op jit(solution)/shard_map/ppermute | solution.py:270
